TPU v7x, 32 devices: a whole 2x2x4 slice. The times are simulated.
32 devices in a mesh: ctx: 8 (over y, x, core), tp: 4 (over z).
Axes of the slice: x: 2, y: 2, z: 4, core: 2. Of those that a mesh axis runs over, the one named last changes fastest.
Arguments:
- queries: bfloat16 [8192, 4096], P('ctx', 'tp'), may hold values from -6 to 6
- keys: bfloat16 [8192, 4096], P('ctx', 'tp'), may hold values from -6 to 6
- values: bfloat16 [8192, 4096], P('ctx', 'tp'), may hold values from -6 to 6
- residues: float32 [16, 4096], P(None, 'tp'), may hold values from -4 to 4
- rates: float32 [16, 4096], P(None, 'tp'), may hold values from 3.0517578e-05 to 0.04
- out_weight: bfloat16 [4096, 4096], P('tp'), may hold values from -0.125 to 0.125
- span_order: int32 [16], replicated, may hold values from 0 to 15, each once
Outputs:
- projected: bfloat16 [8192, 4096], P('ctx', 'tp')
Inputs may be any that keep to these rules, and one draw needn't show every extreme that they name: span_order holds each of 0 .. 15 once.
All inputs are finite; a program needn't handle non-finite values.
Results may differ from a plain program's by a relative error of at most 0.015.
Values may be sent and summed in bfloat16 or wider, within the bound.
No kernel may reach another device: no remote copies, remote signals or barrier semaphores. Data moves between devices by JAX's collectives and lax.ppermute only.
A program may use at most 128 MiB of HBM per device.

v0:
```python
import functools

import jax
import jax.numpy as jnp
from jax import lax
from jax.experimental import pallas as pl
from jax.experimental.pallas import tpu as pltpu
from jax.sharding import PartitionSpec as P

ROWS = 16
LANES = 512


def gate_rows(keys_ref, values_ref, gated_ref, length):
    @pl.loop(0, length // 64)
    def _(step):
        rows = pl.ds(pl.multiple_of(step * 64, 64), 64)
        gated = keys_ref[rows, :].astype(jnp.float32) * values_ref[rows, :].astype(jnp.float32)
        gated_ref[rows, :] = gated.astype(jnp.bfloat16).astype(jnp.float32)


def states_kernel(keys_ref, values_ref, rates_ref, out_ref, gated_ref):
    length = keys_ref.shape[0]
    gate_rows(keys_ref, values_ref, gated_ref, length)
    decay = jnp.exp(-rates_ref[...])

    def body(step, state):
        base = pl.multiple_of(step * ROWS, ROWS)
        for row in range(ROWS):
            state = decay * state + gated_ref[pl.ds(base + row, 1), :]
        return state

    out_ref[0] = lax.fori_loop(0, length // ROWS, body, jnp.zeros(decay.shape, jnp.float32))


def span_states(keys, values, rates, spans):
    tokens, channels = keys.shape
    length, modes = tokens // spans, rates.shape[0]
    lanes = min(LANES, channels)
    rows = pl.BlockSpec((length, lanes), lambda c, s: (s, c))
    table = pl.BlockSpec((modes, lanes), lambda c, s: (0, c))
    return pl.pallas_call(
        states_kernel,
        out_shape=jax.ShapeDtypeStruct((spans, modes, channels), jnp.float32),
        grid=(channels // lanes, spans),
        in_specs=[rows, rows, table],
        out_specs=pl.BlockSpec((1, modes, lanes), lambda c, s: (s, 0, c)),
        scratch_shapes=[pltpu.VMEM((length, lanes), jnp.float32)],
        name="span_states",
    )(keys, values, rates)


def fold_rows(parts):
    index = lax.broadcasted_iota(jnp.int32, parts[0].shape, 0)
    for bit in (1, 2, 4):
        low = (index & bit) == 0
        parts = [
            jnp.where(low, first, second)
            + pltpu.roll(jnp.where(low, second, first), 8 - bit, axis=0)
            for first, second in zip(parts[0::2], parts[1::2])
        ]
    return parts[0]


def convolve_kernel(
    first, gaps_ref, queries_ref, keys_ref, values_ref, states_ref, residues_ref, rates_ref,
    out_ref, gated_ref,
):
    length = keys_ref.shape[0]
    span = first + pl.program_id(1)
    gate_rows(keys_ref, values_ref, gated_ref, length)
    rates = rates_ref[...]
    decay = jnp.exp(-rates)
    scaled = residues_ref[...] * jnp.sqrt(2.0 * rates)

    def carry(source, state):
        gap = gaps_ref[span, source]
        reach = jnp.exp(-rates * (length * jnp.maximum(gap, 0)).astype(jnp.float32))
        return state + jnp.where(gap >= 0, reach, 0.0) * states_ref[source]

    entering = lax.fori_loop(0, states_ref.shape[0], carry, jnp.zeros(rates.shape, jnp.float32))

    def body(step, state):
        base = pl.multiple_of(step * ROWS, ROWS)
        groups = []
        for group in range(0, ROWS, 8):
            parts = []
            for row in range(group, group + 8):
                state = decay * state + gated_ref[pl.ds(base + row, 1), :]
                seen = scaled * state
                total = seen[0:8]
                for mode in range(8, seen.shape[0], 8):
                    total = total + seen[mode : mode + 8]
                parts.append(total)
            groups.append(fold_rows(parts))
        mixed = jnp.concatenate(groups, axis=0).astype(jnp.bfloat16).astype(jnp.float32)
        rows = pl.ds(base, ROWS)
        out_ref[rows, :] = (queries_ref[rows, :].astype(jnp.float32) * mixed).astype(jnp.bfloat16)
        return state

    lax.fori_loop(0, length // ROWS, body, entering)


def convolve(queries, keys, values, states, residues, rates, gaps, spans, first, count):
    tokens, channels = keys.shape
    length, modes = tokens // spans, rates.shape[0]
    lanes = min(LANES, channels)
    rows = pl.BlockSpec((length, lanes), lambda c, s, g: (first + s, c))
    table = pl.BlockSpec((modes, lanes), lambda c, s, g: (0, c))
    every = pl.BlockSpec((states.shape[0], modes, lanes), lambda c, s, g: (0, 0, c))
    return pl.pallas_call(
        functools.partial(convolve_kernel, first),
        out_shape=jax.ShapeDtypeStruct((count * length, channels), jnp.bfloat16),
        grid_spec=pltpu.PrefetchScalarGridSpec(
            num_scalar_prefetch=1,
            grid=(channels // lanes, count),
            in_specs=[rows, rows, rows, every, table, table],
            out_specs=pl.BlockSpec((length, lanes), lambda c, s, g: (s, c)),
            scratch_shapes=[pltpu.VMEM((length, lanes), jnp.float32)],
        ),
        name="convolve",
    )(gaps, queries, keys, values, states, residues, rates)


def local(queries, keys, values, residues, rates, out_weight, span_order):
    spans = span_order.shape[0] // lax.axis_size("ctx")
    own = lax.dynamic_slice_in_dim(span_order, lax.axis_index("ctx") * spans, spans)
    gaps = own[:, None] - 1 - span_order[None, :]
    totals = span_states(keys, values, rates, spans)
    half = totals.shape[1] // 2
    states = jnp.concatenate(
        [
            lax.all_gather(totals[:, :half], "ctx", axis=0, tiled=True),
            lax.all_gather(totals[:, half:], "ctx", axis=0, tiled=True),
        ],
        axis=1,
    )
    output = convolve(queries, keys, values, states, residues, rates, gaps, spans, 0, spans)
    partial_value = jnp.dot(output, out_weight, preferred_element_type=jnp.float32).astype(
        jnp.bfloat16
    )
    return lax.psum_scatter(partial_value, "tp", scatter_dimension=1, tiled=True)


def solution(mesh):
    placed = (
        P("ctx", "tp"),
        P("ctx", "tp"),
        P("ctx", "tp"),
        P(None, "tp"),
        P(None, "tp"),
        P("tp", None),
        P(),
    )
    return jax.shard_map(
        local, mesh=mesh, in_specs=placed, out_specs=P("ctx", "tp"), check_vma=False
    )
```

profile of v0, /device:TPU:0, one launch (start us, length us, event | category | flops | bytes accessed | tf_op | source)
XLA Modules:
  0.0 224.4 jit_solution(9797537611357996272)
XLA Ops:
  6.5 0.0 reduce-scatter.2.cloned.1.call-start
  6.5 0.7 dynamic-slice_add_fusion
  7.3 1.3 broadcast_subtract_fusion.gaps_ref
  8.6 7.5 %span_states.1 = f32[2,16,1024]{2,1,0:T(8,128)} custom-call(bf16[1024,1024]{1,0:T(8,128)(2,1)} %keys_ref.3, bf16[1024,1024]{1,0:T(8,128)(2,1)} %values_ref.3, f32[16,1024]{1,0:T(8,128)} %rates_ref.3), custom_call_target="tpu_custom_call" | custom-call | tf_op jit(solution)/shard_map/span_states/pallas_call | solution.py:42
  16.0 0.9 fusion
  16.9 11.3 %all_gather.6 = f32[16,8,1024]{2,1,0:T(8,128)S(1)} all-gather(f32[2,8,1024]{2,1,0:T(8,128)S(1)} %get-tuple-element.5), channel_id=1, replica_groups=mesh['ctx'=8,'tp'=4] {'ctx'}, dimensions={0}, use_global_device_ids=true | all-gather | bytes 589824 | tf_op jit(solution)/shard_map/all_gather | solution.py:133
  28.2 9.8 %all_gather.7 = f32[16,8,1024]{2,1,0:T(8,128)S(1)} all-gather(f32[2,8,1024]{2,1,0:T(8,128)S(1)} %get-tuple-element.6), channel_id=1, replica_groups=mesh['ctx'=8,'tp'=4] {'ctx'}, dimensions={0}, use_global_device_ids=true | all-gather | bytes 589824 | tf_op jit(solution)/shard_map/all_gather | solution.py:134
  38.0 1.1 pad_maximum_fusion.states_ref
  39.1 18.7 %convolve.1 = bf16[1024,1024]{1,0:T(8,128)(2,1)} custom-call(s32[2,16]{1,0:T(2,128)} %broadcast_subtract_fusion.gaps_ref, bf16[1024,1024]{1,0:T(8,128)(2,1)} %queries_ref.1, bf16[1024,1024]{1,0:T(8,128)(2,1)} %keys_ref.3, bf16[1024,1024]{1,0:T(8,128)(2,1)} %values_ref.3, f32[16,16,1024]{2,1,0:T(8,128)} %pad_maximum_fusion.states_ref, ...), custom_call_target="tpu_custom_call" | custom-call | tf_op jit(solution)/shard_map/convolve/pallas_call | solution.py:111
  57.8 14.7 %convolution_convert_fusion = bf16[1024,4096]{1,0:T(8,128)(2,1)} fusion(bf16[1024,1024]{1,0:T(8,128)(2,1)} %convolve.1, bf16[1024,4096]{1,0:T(8,128)(2,1)} %param.12), kind=kOutput, calls=%fused_computation | convolution fusion | flops 8594128896 | bytes 18874368 | tf_op jit(solution)/shard_map/dot_general | solution.py:139
  72.5 0.0 reduce-scatter.2.cloned.1.call-update
  72.5 145.1 %reduce-scatter.2.cloned.1.call-done = bf16[1024,1024]{1,0:T(8,128)(2,1)} async-done(((bf16[1024,4096]{1,0:T(8,128)(2,1)}), bf16[1024,1024]{1,0:T(8,128)(2,1)}) %reduce-scatter.2.cloned.1.call-update) | async-done | bytes 2097168 | tf_op jit(solution)/shard_map/reduce_scatter | solution.py:142
Async XLA Ops:
  6.5 211.1 %reduce-scatter.2.cloned.1.call-start = ((), (), s32[]{:S(2)}) async-start(), calls=%async_computation.1 | async-start | bytes 10485760 | tf_op jit(solution)/shard_map/reduce_scatter | solution.py:142
Sparse Core Ops, SparseCore 0:
  72.7 144.8 reduce-scatter.1
where the time goes:
time: 225 us; the launch traced here: 224 us
  waiting for transfers between devices  145 us (64%)
  Pallas kernels  26.1 us (12%)
  blocking collectives  21.1 us (9%)
  matrix products  14.7 us (7%)
  between operations  13.4 us (6%)
  other arithmetic  3.1 us (1%)
    reduce_scatter x1, waiting for transfers between devices, local(): lax.psum_scatter(partial_value, 'tp', scatter_dimension=1, tiled=True)  145 us
    pallas_call x1, Pallas kernels, convolve(): pl.pallas_call(functools.partial(convolve_kernel, first), out_shape=jax.S...  18.7 us
    dot_general x1, matrix products, local(): jnp.dot(output, out_weight, preferred_element_type=jnp.float32)  14.7 us
    all_gather x1, blocking collectives, local(): lax.all_gather(totals[:, :half], 'ctx', axis=0, tiled=True)  11.3 us
    all_gather x1, blocking collectives, local(): lax.all_gather(totals[:, half:], 'ctx', axis=0, tiled=True)  9.81 us
    pallas_call x1, Pallas kernels, span_states(): pl.pallas_call(states_kernel, out_shape=jax.ShapeDtypeStruct((spans, mode...  7.46 us
  transfers between devices with their start and end apart: 1, of which 1 were waited for; matrix products, arithmetic and copies ran while one was open for 0% of the time, Pallas kernels for 0%

commit v1 on v0

--- a/solution.py
+++ b/solution.py
@@ -7,8 +7,10 @@
 from jax.experimental.pallas import tpu as pltpu
 from jax.sharding import PartitionSpec as P
 
+
 ROWS = 16
 LANES = 512
+PARTS = 2
 
 
 def gate_rows(keys_ref, values_ref, gated_ref, length):
@@ -101,19 +103,21 @@
     lax.fori_loop(0, length // ROWS, body, entering)
 
 
-def convolve(queries, keys, values, states, residues, rates, gaps, spans, first, count):
+def convolve(queries, keys, values, states, residues, rates, gaps, spans, first, count, part, parts):
     tokens, channels = keys.shape
     length, modes = tokens // spans, rates.shape[0]
-    lanes = min(LANES, channels)
-    rows = pl.BlockSpec((length, lanes), lambda c, s, g: (first + s, c))
-    table = pl.BlockSpec((modes, lanes), lambda c, s, g: (0, c))
-    every = pl.BlockSpec((states.shape[0], modes, lanes), lambda c, s, g: (0, 0, c))
+    width = channels // parts
+    lanes = min(LANES, width)
+    start = part * (width // lanes)
+    rows = pl.BlockSpec((length, lanes), lambda c, s, g: (first + s, start + c))
+    table = pl.BlockSpec((modes, lanes), lambda c, s, g: (0, start + c))
+    every = pl.BlockSpec((states.shape[0], modes, lanes), lambda c, s, g: (0, 0, start + c))
     return pl.pallas_call(
         functools.partial(convolve_kernel, first),
-        out_shape=jax.ShapeDtypeStruct((count * length, channels), jnp.bfloat16),
+        out_shape=jax.ShapeDtypeStruct((count * length, width), jnp.bfloat16),
         grid_spec=pltpu.PrefetchScalarGridSpec(
             num_scalar_prefetch=1,
-            grid=(channels // lanes, count),
+            grid=(width // lanes, count),
             in_specs=[rows, rows, rows, every, table, table],
             out_specs=pl.BlockSpec((length, lanes), lambda c, s, g: (s, c)),
             scratch_shapes=[pltpu.VMEM((length, lanes), jnp.float32)],
@@ -122,10 +126,117 @@
     )(gaps, queries, keys, values, states, residues, rates)
 
 
+def gather_weights(out_weight, parts):
+    n, ctx = lax.axis_size("tp"), lax.axis_size("ctx")
+    me, mine = lax.axis_index("tp"), lax.axis_index("ctx")
+    channels, columns = out_weight.shape[0], out_weight.shape[1] // n
+    rows = channels // ctx
+    strip = lax.dynamic_slice_in_dim(out_weight, mine * rows, rows, 0)
+    pieces = []
+    for shift in range(1, n):
+        target = lax.rem(me + shift, n)
+        piece = lax.dynamic_slice_in_dim(strip, target * columns, columns, 1)
+        pieces.append(lax.ppermute(piece, "tp", [(i, (i + shift) % n) for i in range(n)]))
+    held = jnp.stack(pieces)
+    bits = ctx.bit_length() - 1
+    gathered = []
+    for part in range(parts):
+        order = list(range(1, bits)) if part % 2 == 0 else list(range(bits - 1, 0, -1))
+        order = order + [0]
+        width = columns // parts
+        block = held[:, :, part * width : (part + 1) * width]
+        for bit in order:
+            other = lax.ppermute(block, "ctx", [(i, i ^ (1 << bit)) for i in range(ctx)])
+            low = ((mine >> bit) & 1) == 0
+            block = jnp.stack([jnp.where(low, block, other), jnp.where(low, other, block)])
+        lead = [len(order) - 1 - order.index(bit) for bit in range(bits - 1, -1, -1)]
+        block = jnp.transpose(block, [bits] + lead + [bits + 1, bits + 2])
+        gathered.append(block.reshape(n - 1, channels, width))
+    return gathered
+
+
+def payload_kernel(where_ref, right_ref, left_ref, ahead_ref, behind_ref, to_right_ref, to_left_ref):
+    @pl.when(where_ref[2] > 0)
+    def _():
+        to_right_ref[...] = ahead_ref[...] + right_ref[...]
+
+    @pl.when(where_ref[2] == 0)
+    def _():
+        to_right_ref[...] = ahead_ref[...]
+
+    @pl.when(where_ref[3] > 0)
+    def _():
+        to_left_ref[...] = behind_ref[...] + left_ref[...]
+
+    @pl.when(where_ref[3] == 0)
+    def _():
+        to_left_ref[...] = behind_ref[...]
+
+
+def payload(where, product, ahead, behind):
+    rows, width = ahead.shape
+    tile = min(rows, 256)
+    moved = pl.BlockSpec((tile, width), lambda i, w: (i, 0))
+    return pl.pallas_call(
+        payload_kernel,
+        out_shape=[jax.ShapeDtypeStruct(ahead.shape, ahead.dtype)] * 2,
+        grid_spec=pltpu.PrefetchScalarGridSpec(
+            num_scalar_prefetch=1,
+            grid=(rows // tile,),
+            in_specs=[
+                pl.BlockSpec((tile, width), lambda i, w: (i, w[0])),
+                pl.BlockSpec((tile, width), lambda i, w: (i, w[1])),
+                moved,
+                moved,
+            ],
+            out_specs=[moved, moved],
+        ),
+        name="payload",
+    )(where, product, product, ahead, behind)
+
+
+def exchange(sent, product, parts):
+    n = lax.axis_size("tp")
+    me = lax.axis_index("tp")
+    rights = [(i, i + 1) for i in range(n - 1)]
+    lefts = [(i + 1, i) for i in range(n - 1)]
+    ahead, behind = list(sent), list(sent)
+    from_left = [[None] * parts for _ in range(n + 1)]
+    from_right = [[None] * parts for _ in range(n + 1)]
+    for slot in range(1, n + 1):
+        for part in range(parts):
+            right, left = ahead[part], behind[part]
+            if slot > 1:
+                step = slot - 1
+                where = jnp.stack(
+                    [
+                        lax.rem(me + n - step, n) * parts + part,
+                        lax.rem(me + step, n) * parts + part,
+                        (me < step).astype(jnp.int32),
+                        (me >= n - step).astype(jnp.int32),
+                    ]
+                )
+                right, left = payload(where, product, right, left)
+            right = lax.ppermute(right, "tp", rights)
+            left = lax.ppermute(left, "tp", lefts)
+            ahead[part], behind[part] = right, left
+            from_left[slot][part], from_right[slot][part] = right, left
+    gathered = [
+        [jnp.where(me >= shift, from_left[shift][part], from_right[n - shift][part]) for part in range(parts)]
+        for shift in range(1, n)
+    ]
+    return gathered, from_left[n], from_right[n]
+
+
 def local(queries, keys, values, residues, rates, out_weight, span_order):
+    n = lax.axis_size("tp")
+    me = lax.axis_index("tp")
+    parts = PARTS
     spans = span_order.shape[0] // lax.axis_size("ctx")
     own = lax.dynamic_slice_in_dim(span_order, lax.axis_index("ctx") * spans, spans)
     gaps = own[:, None] - 1 - span_order[None, :]
+    gather = out_weight.shape[0] // lax.axis_size("ctx") >= 128
+    weights = gather_weights(out_weight, parts) if gather else None
     totals = span_states(keys, values, rates, spans)
     half = totals.shape[1] // 2
     states = jnp.concatenate(
@@ -135,11 +246,31 @@
         ],
         axis=1,
     )
-    output = convolve(queries, keys, values, states, residues, rates, gaps, spans, 0, spans)
-    partial_value = jnp.dot(output, out_weight, preferred_element_type=jnp.float32).astype(
-        jnp.bfloat16
+    conv = functools.partial(convolve, queries, keys, values, states, residues, rates, gaps, spans)
+    if not gather:
+        output = conv(0, spans, 0, 1)
+        part = jnp.dot(output, out_weight, preferred_element_type=jnp.float32).astype(jnp.bfloat16)
+        return lax.psum_scatter(part, "tp", scatter_dimension=1, tiled=True)
+    lower = spans // 2
+    sent = []
+    for part in range(parts):
+        sent.append(conv(0, lower, part, parts))
+    rest = conv(lower, spans - lower, 0, 1)
+    columns = out_weight.shape[1] // n
+    product = jnp.dot(rest, out_weight, preferred_element_type=jnp.float32).astype(jnp.bfloat16)
+    gathered, from_left, from_right = exchange(sent, product, parts)
+    whole = jnp.concatenate(sent + [piece for pieces in gathered for piece in pieces], axis=1)
+    mine = lax.dynamic_slice_in_dim(out_weight, me * columns, columns, 1)
+    matrix = jnp.concatenate([mine[None], jnp.concatenate(weights, axis=2)], axis=0)
+    matrix = matrix.reshape(n * mine.shape[0], columns)
+    upper = jnp.dot(whole, matrix, preferred_element_type=jnp.float32).astype(jnp.bfloat16)
+    own_part = lax.dynamic_slice_in_dim(product, me * columns, columns, 1)
+    total = (
+        own_part.astype(jnp.float32)
+        + jnp.concatenate(from_left, axis=1).astype(jnp.float32)
+        + jnp.concatenate(from_right, axis=1).astype(jnp.float32)
     )
-    return lax.psum_scatter(partial_value, "tp", scatter_dimension=1, tiled=True)
+    return jnp.concatenate([upper, total.astype(jnp.bfloat16)], axis=0)
 
 
 def solution(mesh):
@@ -152,6 +283,5 @@
         P("tp", None),
         P(),
     )
-    return jax.shard_map(
-        local, mesh=mesh, in_specs=placed, out_specs=P("ctx", "tp"), check_vma=False
-    )
+
+    return jax.shard_map(local, mesh=mesh, in_specs=placed, out_specs=P("ctx", "tp"), check_vma=False)

time: 225 us -> 206 us (0.916)
  waiting for transfers between devices: 145 us -> 14 us
  starting transfers between devices: 0.01 us -> 58 us
  other arithmetic: 3.1 us -> 32.5 us
  Pallas kernels: 26.1 us -> 50.3 us
  local copies, waits for them, and re-layouts: 0.88 us -> 15.3 us
  between operations: 13.4 us -> 0.47 us
    reduce_scatter x1 -> x0, waiting for transfers between devices: 145 us -> none  [local(): lax.psum_scatter(partial_value, 'tp', scatter_dimension=1, tiled=True)]
    ppermute x0 -> x25, starting transfers between devices: none -> 58 us  [the longest x8 36.5 us: exchange(): right = lax.ppermute(right, 'tp', rights)]
    pallas_call x0 -> x6, Pallas kernels: none -> 18.4 us  [payload(): pl.pallas_call(payload_kernel, out_shape=[jax.ShapeDtypeStruct(ahead.shap...]
    another operation x0 -> x17, other arithmetic: none -> 16.6 us  [the longest x10 11.6 us: gather_weights(): jnp.stack([jnp.where(low, block, other), jnp.where(low, other, block)])]
    ppermute x0 -> x25, waiting for transfers between devices: none -> 14 us  [the longest x8 9.54 us: exchange(): left = lax.ppermute(left, 'tp', lefts)]
    unnamed x0 -> x5, other arithmetic: none -> 9.21 us
    unnamed x0 -> x51, local copies, waits for them, and re-layouts: none -> 7.5 us
    pallas_call x1 -> x3, Pallas kernels: 18.7 us -> 24.4 us  [convolve(): pl.pallas_call(functools.partial(convolve_kernel, first), out_shape=jax.S...]
  transfers between devices with their start and end apart: 1 -> 25, of which waited for: 1 -> 2; matrix products, arithmetic and copies ran while one was open for 0% -> 22% of each run, Pallas kernels for 0% -> 25%
where the time goes in v1:
time: 206 us; the launch traced here: 204 us
  starting transfers between devices  58 us (28%)
  Pallas kernels  50.3 us (24%)
  other arithmetic  32.5 us (16%)
  blocking collectives  19.7 us (10%)
  local copies, waits for them, and re-layouts  15.3 us (7%)
  waiting for transfers between devices  14 us (7%)
  matrix products  13.9 us (7%)
    ppermute x8, starting transfers between devices, exchange(): right = lax.ppermute(right, 'tp', rights)  36.5 us
    pallas_call x3, Pallas kernels, convolve(): pl.pallas_call(functools.partial(convolve_kernel, first), out_shape=jax.S...  24.4 us
    pallas_call x6, Pallas kernels, payload(): pl.pallas_call(payload_kernel, out_shape=[jax.ShapeDtypeStruct(ahead.shap...  18.4 us
    another operation x10, other arithmetic, gather_weights(): jnp.stack([jnp.where(low, block, other), jnp.where(low, other, block)])  11.6 us
    ppermute x8, starting transfers between devices, exchange(): left = lax.ppermute(left, 'tp', lefts)  10.9 us
    all_gather x1, blocking collectives, local(): lax.all_gather(totals[:, :half], 'ctx', axis=0, tiled=True)  9.86 us
    all_gather x1, blocking collectives, local(): lax.all_gather(totals[:, half:], 'ctx', axis=0, tiled=True)  9.83 us
    ppermute x8, waiting for transfers between devices, exchange(): left = lax.ppermute(left, 'tp', lefts)  9.54 us
  transfers between devices with their start and end apart: 25, of which 2 were waited for; matrix products, arithmetic and copies ran while one was open for 22% of the time, Pallas kernels for 25%

profile of v1, /device:TPU:0, one launch (start us, length us, event | category | flops | bytes accessed | tf_op | source)
XLA Modules:
  0.0 204.3 jit_solution(1918736838385793107)
XLA Ops:
  2.3 5.1 %collective-permute-start.14 = (bf16[128,1024]{1,0:T(8,128)(2,1)S(1)}, bf16[128,1024]{1,0:T(8,128)(2,1)}, u32[]{:S(2)}, u32[]{:S(2)}) collective-permute-start(bf16[128,1024]{1,0:T(8,128)(2,1)S(1)} %get-tuple-element.30), channel_id=1, source_target_pairs={{0,3},{1,0},{2,1},{3,2},{4,7},{5,4},{6,5},{7,6},{8,11},{9,8},{10,9... | collective-permute-start | bytes 786440 | tf_op jit(solution)/shard_map/ppermute | solution.py:139
  8.4 7.5 %span_states.1 = f32[2,16,1024]{2,1,0:T(8,128)} custom-call(bf16[1024,1024]{1,0:T(8,128)(2,1)} %keys_ref.7, bf16[1024,1024]{1,0:T(8,128)(2,1)} %values_ref.7, f32[16,1024]{1,0:T(8,128)} %rates_ref.7), custom_call_target="tpu_custom_call" | custom-call | tf_op jit(solution)/shard_map/span_states/pallas_call | solution.py:44
  16.8 9.9 %all_gather.6 = f32[16,8,1024]{2,1,0:T(8,128)S(1)} all-gather(f32[2,8,1024]{2,1,0:T(8,128)S(1)} %get-tuple-element.49), channel_id=1, replica_groups=mesh['ctx'=8,'tp'=4] {'ctx'}, dimensions={0}, use_global_device_ids=true | all-gather | bytes 589824 | tf_op jit(solution)/shard_map/all_gather | solution.py:244
  26.7 9.8 %all_gather.7 = f32[16,8,1024]{2,1,0:T(8,128)S(1)} all-gather(f32[2,8,1024]{2,1,0:T(8,128)S(1)} %get-tuple-element.48), channel_id=1, replica_groups=mesh['ctx'=8,'tp'=4] {'ctx'}, dimensions={0}, use_global_device_ids=true | all-gather | bytes 589824 | tf_op jit(solution)/shard_map/all_gather | solution.py:245
  37.5 6.8 %convolve.4 = bf16[512,512]{1,0:T(8,128)(2,1)} custom-call(s32[2,16]{1,0:T(2,128)} %broadcast_subtract_fusion.gaps_ref, bf16[1024,1024]{1,0:T(8,128)(2,1)} %queries_ref.5, bf16[1024,1024]{1,0:T(8,128)(2,1)} %keys_ref.7, bf16[1024,1024]{1,0:T(8,128)(2,1)} %values_ref.7, f32[16,16,1024]{2,1,0:T(8,128)} %copy-done, f32[16,1024]{1,0:T(8,128)} %residues_ref.5, ...), custom_call_target="tpu_custom_call" | custom-call | tf_op jit(solution)/shard_map/convolve/pallas_call | solution.py:115
  44.4 4.4 %collective-permute-start.5 = (bf16[512,512]{1,0:T(8,128)(2,1)}, bf16[512,512]{1,0:T(8,128)(2,1)S(1)}, u32[]{:S(2)}, u32[]{:S(2)}) collective-permute-start(bf16[512,512]{1,0:T(8,128)(2,1)} %convolve.4), channel_id=1, source_target_pairs={{0,1},{1,2},{2,3},{4,5},{5,6},{6,7},{8,9},{9,10},{10,11},{12,13},{... | collective-permute-start | bytes 1572872 | tf_op jit(solution)/shard_map/ppermute | solution.py:220
  50.1 10.8 %convolve.5 = bf16[512,1024]{1,0:T(8,128)(2,1)} custom-call(s32[2,16]{1,0:T(2,128)} %broadcast_subtract_fusion.gaps_ref, bf16[1024,1024]{1,0:T(8,128)(2,1)} %queries_ref.5, bf16[1024,1024]{1,0:T(8,128)(2,1)} %keys_ref.7, bf16[1024,1024]{1,0:T(8,128)(2,1)} %values_ref.7, f32[16,16,1024]{2,1,0:T(8,128)} %copy-done, f32[16,1024]{1,0:T(8,128)} %residues_ref.5, ...), custom_call_target="tpu_custom_call" | custom-call | tf_op jit(solution)/shard_map/convolve/pallas_call | solution.py:115
  60.9 6.8 %convolve.3 = bf16[512,512]{1,0:T(8,128)(2,1)} custom-call(s32[2,16]{1,0:T(2,128)} %broadcast_subtract_fusion.gaps_ref, bf16[1024,1024]{1,0:T(8,128)(2,1)} %queries_ref.5, bf16[1024,1024]{1,0:T(8,128)(2,1)} %keys_ref.7, bf16[1024,1024]{1,0:T(8,128)(2,1)} %values_ref.7, f32[16,16,1024]{2,1,0:T(8,128)} %copy-done, f32[16,1024]{1,0:T(8,128)} %residues_ref.5, ...), custom_call_target="tpu_custom_call" | custom-call | tf_op jit(solution)/shard_map/convolve/pallas_call | solution.py:115
  67.7 4.7 %collective-permute-start = (bf16[512,512]{1,0:T(8,128)(2,1)}, bf16[512,512]{1,0:T(8,128)(2,1)S(1)}, u32[]{:S(2)}, u32[]{:S(2)}) collective-permute-start(bf16[512,512]{1,0:T(8,128)(2,1)} %convolve.3), channel_id=1, source_target_pairs={{0,1},{1,2},{2,3},{4,5},{5,6},{6,7},{8,9},{9,10},{10,11},{12,13},{... | collective-permute-start | bytes 1572872 | tf_op jit(solution)/shard_map/ppermute | solution.py:220
  76.6 9.4 %convolution_convert_fusion.right_ref.left_ref = bf16[512,4096]{1,0:T(8,128)(2,1)} fusion(bf16[512,1024]{1,0:T(8,128)(2,1)S(1)} %copy-done.20, bf16[1024,4096]{1,0:T(8,128)(2,1)} %param.12), kind=kOutput, calls=%fused_computation.1 | convolution fusion | flops 4297064448 | bytes 13631488 | tf_op jit(solution)/shard_map/dot_general | solution.py:260
  90.1 3.1 %payload.8 = (bf16[512,512]{1,0:T(8,128)(2,1)}, bf16[512,512]{1,0:T(8,128)(2,1)}) custom-call(s32[4]{0:T(128)} %add_add_fusion.3.where_ref, bf16[512,4096]{1,0:T(8,128)(2,1)} %convolution_convert_fusion.right_ref.left_ref, bf16[512,4096]{1,0:T(8,128)(2,1)} %convolution_convert_fusion.right_ref.left_ref, bf16[512,512]{1,0:T(8,128)(2,1)} %copy-done.13, ...), custom_call_target="tpu_custom_call" | custom-call | tf_op jit(solution)/shard_map/payload/pallas_call | solution.py:180
  93.2 5.3 %collective-permute-start.7 = (bf16[512,512]{1,0:T(8,128)(2,1)}, bf16[512,512]{1,0:T(8,128)(2,1)}, u32[]{:S(2)}, u32[]{:S(2)}) collective-permute-start(bf16[512,512]{1,0:T(8,128)(2,1)} %get-tuple-element.20), channel_id=1, source_target_pairs={{0,1},{1,2},{2,3},{4,5},{5,6},{6,7},{8,9},{9,10},{10,11},{12,13},{... | collective-permute-start | bytes 1572872 | tf_op jit(solution)/shard_map/ppermute | solution.py:220
  106.8 3.1 %payload.6 = (bf16[512,512]{1,0:T(8,128)(2,1)}, bf16[512,512]{1,0:T(8,128)(2,1)}) custom-call(s32[4]{0:T(128)} %add_add_fusion.1.where_ref, bf16[512,4096]{1,0:T(8,128)(2,1)} %convolution_convert_fusion.right_ref.left_ref, bf16[512,4096]{1,0:T(8,128)(2,1)} %convolution_convert_fusion.right_ref.left_ref, bf16[512,512]{1,0:T(8,128)(2,1)} %copy-done.14, ...), custom_call_target="tpu_custom_call" | custom-call | tf_op jit(solution)/shard_map/payload/pallas_call | solution.py:180
  109.9 4.6 %collective-permute-start.2 = (bf16[512,512]{1,0:T(8,128)(2,1)}, bf16[512,512]{1,0:T(8,128)(2,1)S(1)}, u32[]{:S(2)}, u32[]{:S(2)}) collective-permute-start(bf16[512,512]{1,0:T(8,128)(2,1)} %get-tuple-element.17), channel_id=1, source_target_pairs={{0,1},{1,2},{2,3},{4,5},{5,6},{6,7},{8,9},{9,10},{10,11},{12,13},{... | collective-permute-start | bytes 1572872 | tf_op jit(solution)/shard_map/ppermute | solution.py:220
  121.5 3.1 %payload.9 = (bf16[512,512]{1,0:T(8,128)(2,1)}, bf16[512,512]{1,0:T(8,128)(2,1)}) custom-call(s32[4]{0:T(128)} %add_add_fusion.2.where_ref, bf16[512,4096]{1,0:T(8,128)(2,1)} %convolution_convert_fusion.right_ref.left_ref, bf16[512,4096]{1,0:T(8,128)(2,1)} %convolution_convert_fusion.right_ref.left_ref, bf16[512,512]{1,0:T(8,128)(2,1)} %collective-permute-done.7.ahead_ref, ...), custom_call_target="tpu_custom_call" | custom-call | tf_op jit(solution)/shard_map/payload/pallas_call | solution.py:180
  124.6 5.3 %collective-permute-start.11 = (bf16[512,512]{1,0:T(8,128)(2,1)}, bf16[512,512]{1,0:T(8,128)(2,1)}, u32[]{:S(2)}, u32[]{:S(2)}) collective-permute-start(bf16[512,512]{1,0:T(8,128)(2,1)} %get-tuple-element.24), channel_id=1, source_target_pairs={{0,1},{1,2},{2,3},{4,5},{5,6},{6,7},{8,9},{9,10},{10,11},{12,13},{... | collective-permute-start | bytes 1572872 | tf_op jit(solution)/shard_map/ppermute | solution.py:220
  132.1 3.1 %payload.7 = (bf16[512,512]{1,0:T(8,128)(2,1)}, bf16[512,512]{1,0:T(8,128)(2,1)}) custom-call(s32[4]{0:T(128)} %add_add_fusion.where_ref, bf16[512,4096]{1,0:T(8,128)(2,1)} %convolution_convert_fusion.right_ref.left_ref, bf16[512,4096]{1,0:T(8,128)(2,1)} %convolution_convert_fusion.right_ref.left_ref, bf16[512,512]{1,0:T(8,128)(2,1)} %copy-done.16, ...), custom_call_target="tpu_custom_call" | custom-call | tf_op jit(solution)/shard_map/payload/pallas_call | solution.py:180
  135.1 5.4 %collective-permute-start.10 = (bf16[512,512]{1,0:T(8,128)(2,1)}, bf16[512,512]{1,0:T(8,128)(2,1)}, u32[]{:S(2)}, u32[]{:S(2)}) collective-permute-start(bf16[512,512]{1,0:T(8,128)(2,1)} %get-tuple-element.23), channel_id=1, source_target_pairs={{0,1},{1,2},{2,3},{4,5},{5,6},{6,7},{8,9},{9,10},{10,11},{12,13},{... | collective-permute-start | bytes 1572872 | tf_op jit(solution)/shard_map/ppermute | solution.py:220
  148.4 3.1 %payload.11 = (bf16[512,512]{1,0:T(8,128)(2,1)}, bf16[512,512]{1,0:T(8,128)(2,1)}) custom-call(s32[4]{0:T(128)} %add_add_fusion.5.where_ref, bf16[512,4096]{1,0:T(8,128)(2,1)} %convolution_convert_fusion.right_ref.left_ref, bf16[512,4096]{1,0:T(8,128)(2,1)} %convolution_convert_fusion.right_ref.left_ref, bf16[512,512]{1,0:T(8,128)(2,1)} %collective-permute-done.11.ahead_ref, ...), custom_call_target="tpu_custom_call" | custom-call | tf_op jit(solution)/shard_map/payload/pallas_call | solution.py:180
  151.4 5.4 %collective-permute-start.22 = (bf16[512,512]{1,0:T(8,128)(2,1)}, bf16[512,512]{1,0:T(8,128)(2,1)}, u32[]{:S(2)}, u32[]{:S(2)}) collective-permute-start(bf16[512,512]{1,0:T(8,128)(2,1)} %get-tuple-element.26), channel_id=1, source_target_pairs={{0,1},{1,2},{2,3},{4,5},{5,6},{6,7},{8,9},{9,10},{10,11},{12,13},{... | collective-permute-start | bytes 1572872 | tf_op jit(solution)/shard_map/ppermute | solution.py:220
  156.8 3.1 %payload.10 = (bf16[512,512]{1,0:T(8,128)(2,1)}, bf16[512,512]{1,0:T(8,128)(2,1)}) custom-call(s32[4]{0:T(128)} %add_add_fusion.4.where_ref, bf16[512,4096]{1,0:T(8,128)(2,1)} %convolution_convert_fusion.right_ref.left_ref, bf16[512,4096]{1,0:T(8,128)(2,1)} %convolution_convert_fusion.right_ref.left_ref, bf16[512,512]{1,0:T(8,128)(2,1)} %collective-permute-done.10.ahead_ref, ...), custom_call_target="tpu_custom_call" | custom-call | tf_op jit(solution)/shard_map/payload/pallas_call | solution.py:180
  174.4 4.5 %collective-permute-done.21 = bf16[512,512]{1,0:T(8,128)(2,1)S(1)} collective-permute-done((bf16[512,512]{1,0:T(8,128)(2,1)}, bf16[512,512]{1,0:T(8,128)(2,1)S(1)}, u32[]{:S(2)}, u32[]{:S(2)}) %collective-permute-start.21) | collective-permute-done | bytes 524320 | tf_op jit(solution)/shard_map/ppermute | solution.py:220
  178.9 9.5 %collective-permute-done.23 = bf16[512,512]{1,0:T(8,128)(2,1)S(1)} collective-permute-done((bf16[512,512]{1,0:T(8,128)(2,1)S(1)}, bf16[512,512]{1,0:T(8,128)(2,1)S(1)}, u32[]{:S(2)}, u32[]{:S(2)}) %collective-permute-start.23) | collective-permute-done | bytes 524320 | tf_op jit(solution)/shard_map/ppermute | solution.py:221
  198.3 4.5 %convolution_convert_fusion.1 = bf16[512,1024]{1,0:T(8,128)(2,1)S(1)} fusion(bf16[512,4096]{1,0:T(8,128)(2,1)S(1)} %copy-done.21, bf16[4096,1024]{1,0:T(8,128)(2,1)S(1)} %bitcast.60), kind=kOutput, calls=%fused_computation.13 | convolution fusion | flops 4295491584 | bytes 13631488 | tf_op jit(solution)/shard_map/dot_general | solution.py:266
  (127 shorter events, 65.7 us)
Async XLA Ops:
  2.3 65.4 %collective-permute-start.14 = (bf16[128,1024]{1,0:T(8,128)(2,1)S(1)}, bf16[128,1024]{1,0:T(8,128)(2,1)}, u32[]{:S(2)}, u32[]{:S(2)}) collective-permute-start(bf16[128,1024]{1,0:T(8,128)(2,1)S(1)} %get-tuple-element.30), channel_id=1, source_target_pairs={{0,3},{1,0},{2,1},{3,2},{4,7},{5,4},{6,5},{7,6},{8,11},{9,8},{10,9... | collective-permute-start | bytes 786440 | tf_op jit(solution)/shard_map/ppermute | solution.py:139
  7.4 65.0 %collective-permute-start.13 = (bf16[128,1024]{1,0:T(8,128)(2,1)}, bf16[128,1024]{1,0:T(8,128)(2,1)}, u32[]{:S(2)}, u32[]{:S(2)}) collective-permute-start(bf16[128,1024]{1,0:T(8,128)(2,1)} %get-tuple-element.31), channel_id=1, source_target_pairs={{0,2},{1,3},{2,0},{3,1},{4,6},{5,7},{6,4},{7,5},{8,10},{9,11},{10,... | collective-permute-start | bytes 786440 | tf_op jit(solution)/shard_map/ppermute | solution.py:139
  7.4 65.0 %collective-permute-start.12 = (bf16[128,1024]{1,0:T(8,128)(2,1)S(1)}, bf16[128,1024]{1,0:T(8,128)(2,1)}, u32[]{:S(2)}, u32[]{:S(2)}) collective-permute-start(bf16[128,1024]{1,0:T(8,128)(2,1)S(1)} %get-tuple-element.29), channel_id=1, source_target_pairs={{0,1},{1,2},{2,3},{3,0},{4,5},{5,6},{6,7},{7,4},{8,9},{9,10},{10,1... | collective-permute-start | bytes 786440 | tf_op jit(solution)/shard_map/ppermute | solution.py:139
  44.4 43.6 %collective-permute-start.5 = (bf16[512,512]{1,0:T(8,128)(2,1)}, bf16[512,512]{1,0:T(8,128)(2,1)S(1)}, u32[]{:S(2)}, u32[]{:S(2)}) collective-permute-start(bf16[512,512]{1,0:T(8,128)(2,1)} %convolve.4), channel_id=1, source_target_pairs={{0,1},{1,2},{2,3},{4,5},{5,6},{6,7},{8,9},{9,10},{10,11},{12,13},{... | collective-permute-start | bytes 1572872 | tf_op jit(solution)/shard_map/ppermute | solution.py:220
  48.8 40.5 %collective-permute-start.6 = (bf16[512,512]{1,0:T(8,128)(2,1)}, bf16[512,512]{1,0:T(8,128)(2,1)S(1)}, u32[]{:S(2)}, u32[]{:S(2)}) collective-permute-start(bf16[512,512]{1,0:T(8,128)(2,1)} %convolve.4), channel_id=1, source_target_pairs={{1,0},{2,1},{3,2},{5,4},{6,5},{7,6},{9,8},{10,9},{11,10},{13,12},{... | collective-permute-start | bytes 1572872 | tf_op jit(solution)/shard_map/ppermute | solution.py:221
  67.7 38.3 %collective-permute-start = (bf16[512,512]{1,0:T(8,128)(2,1)}, bf16[512,512]{1,0:T(8,128)(2,1)S(1)}, u32[]{:S(2)}, u32[]{:S(2)}) collective-permute-start(bf16[512,512]{1,0:T(8,128)(2,1)} %convolve.3), channel_id=1, source_target_pairs={{0,1},{1,2},{2,3},{4,5},{5,6},{6,7},{8,9},{9,10},{10,11},{12,13},{... | collective-permute-start | bytes 1572872 | tf_op jit(solution)/shard_map/ppermute | solution.py:220
  74.6 23.9 %collective-permute-start.15 = (bf16[3,128,512]{2,1,0:T(8,128)(2,1)}, bf16[3,128,512]{2,1,0:T(8,128)(2,1)}, u32[]{:S(2)}, u32[]{:S(2)}) collective-permute-start(bf16[3,128,512]{2,1,0:T(8,128)(2,1)} %get-tuple-element.46), channel_id=1, source_target_pairs={{0,8},{4,12},{8,0},{12,4},{16,24},{20,28},{24,16},{28,20},{1,9},{5... | collective-permute-start | bytes 1179656 | tf_op jit(solution)/shard_map/ppermute | solution.py:149
  75.1 23.4 %collective-permute-start.18 = (bf16[3,128,512]{2,1,0:T(8,128)(2,1)}, bf16[3,128,512]{2,1,0:T(8,128)(2,1)}, u32[]{:S(2)}, u32[]{:S(2)}) collective-permute-start(bf16[3,128,512]{2,1,0:T(8,128)(2,1)} %get-tuple-element.47), channel_id=1, source_target_pairs={{0,16},{4,20},{8,24},{12,28},{16,0},{20,4},{24,8},{28,12},{1,17},{... | collective-permute-start | bytes 1179656 | tf_op jit(solution)/shard_map/ppermute | solution.py:149
  88.0 18.0 %collective-permute-start.1 = (bf16[512,512]{1,0:T(8,128)(2,1)}, bf16[512,512]{1,0:T(8,128)(2,1)}, u32[]{:S(2)}, u32[]{:S(2)}) collective-permute-start(bf16[512,512]{1,0:T(8,128)(2,1)} %convolve.3), channel_id=1, source_target_pairs={{1,0},{2,1},{3,2},{5,4},{6,5},{7,6},{9,8},{10,9},{11,10},{13,12},{... | collective-permute-start | bytes 1572872 | tf_op jit(solution)/shard_map/ppermute | solution.py:221
  93.2 23.6 %collective-permute-start.7 = (bf16[512,512]{1,0:T(8,128)(2,1)}, bf16[512,512]{1,0:T(8,128)(2,1)}, u32[]{:S(2)}, u32[]{:S(2)}) collective-permute-start(bf16[512,512]{1,0:T(8,128)(2,1)} %get-tuple-element.20), channel_id=1, source_target_pairs={{0,1},{1,2},{2,3},{4,5},{5,6},{6,7},{8,9},{9,10},{10,11},{12,13},{... | collective-permute-start | bytes 1572872 | tf_op jit(solution)/shard_map/ppermute | solution.py:220
  100.8 39.7 %collective-permute-start.19 = (bf16[2,3,128,512]{3,2,0,1:T(8,128)(2,1)}, bf16[2,3,128,512]{3,2,0,1:T(8,128)(2,1)}, u32[]{:S(2)}, u32[]{:S(2)}) collective-permute-start(bf16[2,3,128,512]{3,2,0,1:T(8,128)(2,1)} %pad_maximum_fusion.6), channel_id=1, source_target_pairs={{0,8},{4,12},{8,0},{12,4},{16,24},{20,28},{24,16},{28,20},{1,9},{5... | collective-permute-start | bytes 2359304 | tf_op jit(solution)/shard_map/ppermute | solution.py:149
  104.6 17.0 %collective-permute-start.8 = (bf16[512,512]{1,0:T(8,128)(2,1)}, bf16[512,512]{1,0:T(8,128)(2,1)}, u32[]{:S(2)}, u32[]{:S(2)}) collective-permute-start(bf16[512,512]{1,0:T(8,128)(2,1)} %get-tuple-element.21), channel_id=1, source_target_pairs={{1,0},{2,1},{3,2},{5,4},{6,5},{7,6},{9,8},{10,9},{11,10},{13,12},{... | collective-permute-start | bytes 1572872 | tf_op jit(solution)/shard_map/ppermute | solution.py:221
  109.9 20.1 %collective-permute-start.2 = (bf16[512,512]{1,0:T(8,128)(2,1)}, bf16[512,512]{1,0:T(8,128)(2,1)S(1)}, u32[]{:S(2)}, u32[]{:S(2)}) collective-permute-start(bf16[512,512]{1,0:T(8,128)(2,1)} %get-tuple-element.17), channel_id=1, source_target_pairs={{0,1},{1,2},{2,3},{4,5},{5,6},{6,7},{8,9},{9,10},{10,11},{12,13},{... | collective-permute-start | bytes 1572872 | tf_op jit(solution)/shard_map/ppermute | solution.py:220
  114.4 16.8 %collective-permute-start.3 = (bf16[512,512]{1,0:T(8,128)(2,1)}, bf16[512,512]{1,0:T(8,128)(2,1)S(1)}, u32[]{:S(2)}, u32[]{:S(2)}) collective-permute-start(bf16[512,512]{1,0:T(8,128)(2,1)} %get-tuple-element.18), channel_id=1, source_target_pairs={{1,0},{2,1},{3,2},{5,4},{6,5},{7,6},{9,8},{10,9},{11,10},{13,12},{... | collective-permute-start | bytes 1572872 | tf_op jit(solution)/shard_map/ppermute | solution.py:221
  116.7 28.1 %collective-permute-start.16 = (bf16[2,3,128,512]{3,2,1,0:T(8,128)(2,1)}, bf16[2,3,128,512]{3,2,1,0:T(8,128)(2,1)}, u32[]{:S(2)}, u32[]{:S(2)}) collective-permute-start(bf16[2,3,128,512]{3,2,1,0:T(8,128)(2,1)} %pad_maximum_fusion.5), channel_id=1, source_target_pairs={{0,16},{4,20},{8,24},{12,28},{16,0},{20,4},{24,8},{28,12},{1,17},{... | collective-permute-start | bytes 2359304 | tf_op jit(solution)/shard_map/ppermute | solution.py:149
  124.6 23.2 %collective-permute-start.11 = (bf16[512,512]{1,0:T(8,128)(2,1)}, bf16[512,512]{1,0:T(8,128)(2,1)}, u32[]{:S(2)}, u32[]{:S(2)}) collective-permute-start(bf16[512,512]{1,0:T(8,128)(2,1)} %get-tuple-element.24), channel_id=1, source_target_pairs={{0,1},{1,2},{2,3},{4,5},{5,6},{6,7},{8,9},{9,10},{10,11},{12,13},{... | collective-permute-start | bytes 1572872 | tf_op jit(solution)/shard_map/ppermute | solution.py:220
  130.0 18.4 %collective-permute-start.9 = (bf16[512,512]{1,0:T(8,128)(2,1)}, bf16[512,512]{1,0:T(8,128)(2,1)}, u32[]{:S(2)}, u32[]{:S(2)}) collective-permute-start(bf16[512,512]{1,0:T(8,128)(2,1)} %get-tuple-element.22), channel_id=1, source_target_pairs={{1,0},{2,1},{3,2},{5,4},{6,5},{7,6},{9,8},{10,9},{11,10},{13,12},{... | collective-permute-start | bytes 1572872 | tf_op jit(solution)/shard_map/ppermute | solution.py:221
  135.1 21.7 %collective-permute-start.10 = (bf16[512,512]{1,0:T(8,128)(2,1)}, bf16[512,512]{1,0:T(8,128)(2,1)}, u32[]{:S(2)}, u32[]{:S(2)}) collective-permute-start(bf16[512,512]{1,0:T(8,128)(2,1)} %get-tuple-element.23), channel_id=1, source_target_pairs={{0,1},{1,2},{2,3},{4,5},{5,6},{6,7},{8,9},{9,10},{10,11},{12,13},{... | collective-permute-start | bytes 1572872 | tf_op jit(solution)/shard_map/ppermute | solution.py:220
  144.8 45.5 %collective-permute-start.20 = (bf16[2,2,3,128,512]{4,3,1,0,2:T(8,128)(2,1)}, bf16[2,2,3,128,512]{4,3,1,0,2:T(8,128)(2,1)}, u32[]{:S(2)}, u32[]{:S(2)}) collective-permute-start(bf16[2,2,3,128,512]{4,3,1,0,2:T(8,128)(2,1)} %pad_maximum_fusion.3), channel_id=1, source_target_pairs={{0,4},{4,0},{8,12},{12,8},{16,20},{20,16},{24,28},{28,24},{1,5},{5... | collective-permute-start | bytes 4718600 | tf_op jit(solution)/shard_map/ppermute | solution.py:149
  147.8 44.8 %collective-permute-start.17 = (bf16[2,2,3,128,512]{4,3,1,0,2:T(8,128)(2,1)}, bf16[2,2,3,128,512]{4,3,1,0,2:T(8,128)(2,1)}, u32[]{:S(2)}, u32[]{:S(2)}) collective-permute-start(bf16[2,2,3,128,512]{4,3,1,0,2:T(8,128)(2,1)} %copy.20), channel_id=1, source_target_pairs={{0,4},{4,0},{8,12},{12,8},{16,20},{20,16},{24,28},{28,24},{1,5},{5... | collective-permute-start | bytes 4718600 | tf_op jit(solution)/shard_map/ppermute | solution.py:149
  151.4 18.5 %collective-permute-start.22 = (bf16[512,512]{1,0:T(8,128)(2,1)}, bf16[512,512]{1,0:T(8,128)(2,1)}, u32[]{:S(2)}, u32[]{:S(2)}) collective-permute-start(bf16[512,512]{1,0:T(8,128)(2,1)} %get-tuple-element.26), channel_id=1, source_target_pairs={{0,1},{1,2},{2,3},{4,5},{5,6},{6,7},{8,9},{9,10},{10,11},{12,13},{... | collective-permute-start | bytes 1572872 | tf_op jit(solution)/shard_map/ppermute | solution.py:220
  159.9 19.0 %collective-permute-start.21 = (bf16[512,512]{1,0:T(8,128)(2,1)}, bf16[512,512]{1,0:T(8,128)(2,1)S(1)}, u32[]{:S(2)}, u32[]{:S(2)}) collective-permute-start(bf16[512,512]{1,0:T(8,128)(2,1)} %get-tuple-element.25), channel_id=1, source_target_pairs={{0,1},{1,2},{2,3},{4,5},{5,6},{6,7},{8,9},{9,10},{10,11},{12,13},{... | collective-permute-start | bytes 1572872 | tf_op jit(solution)/shard_map/ppermute | solution.py:220
  161.4 17.5 %collective-permute-start.24 = (bf16[512,512]{1,0:T(8,128)(2,1)}, bf16[512,512]{1,0:T(8,128)(2,1)S(1)}, u32[]{:S(2)}, u32[]{:S(2)}) collective-permute-start(bf16[512,512]{1,0:T(8,128)(2,1)} %get-tuple-element.28), channel_id=1, source_target_pairs={{1,0},{2,1},{3,2},{5,4},{6,5},{7,6},{9,8},{10,9},{11,10},{13,12},{... | collective-permute-start | bytes 1572872 | tf_op jit(solution)/shard_map/ppermute | solution.py:221
  170.0 18.5 %collective-permute-start.23 = (bf16[512,512]{1,0:T(8,128)(2,1)S(1)}, bf16[512,512]{1,0:T(8,128)(2,1)S(1)}, u32[]{:S(2)}, u32[]{:S(2)}) collective-permute-start(bf16[512,512]{1,0:T(8,128)(2,1)S(1)} %copy-done.23), channel_id=1, source_target_pairs={{1,0},{2,1},{3,2},{5,4},{6,5},{7,6},{9,8},{10,9},{11,10},{13,12},{... | collective-permute-start | bytes 1572872 | tf_op jit(solution)/shard_map/ppermute | solution.py:221
  (25 other events, 173.2 us)

commit v2 on v0

--- a/solution.py
+++ b/solution.py
@@ -7,8 +7,11 @@
 from jax.experimental.pallas import tpu as pltpu
 from jax.sharding import PartitionSpec as P
 
+
 ROWS = 16
 LANES = 512
+PARTS = 2
+TILE = 128
 
 
 def gate_rows(keys_ref, values_ref, gated_ref, length):
@@ -46,6 +49,7 @@
         in_specs=[rows, rows, table],
         out_specs=pl.BlockSpec((1, modes, lanes), lambda c, s: (s, 0, c)),
         scratch_shapes=[pltpu.VMEM((length, lanes), jnp.float32)],
+        compiler_params=pltpu.CompilerParams(vmem_limit_bytes=8 << 20),
         name="span_states",
     )(keys, values, rates)
 
@@ -63,12 +67,11 @@
 
 
 def convolve_kernel(
-    first, gaps_ref, queries_ref, keys_ref, values_ref, states_ref, residues_ref, rates_ref,
+    span, length, gaps_ref, queries_ref, keys_ref, values_ref, states_ref, residues_ref, rates_ref,
     out_ref, gated_ref,
 ):
-    length = keys_ref.shape[0]
-    span = first + pl.program_id(1)
-    gate_rows(keys_ref, values_ref, gated_ref, length)
+    rows = keys_ref.shape[0]
+    gate_rows(keys_ref, values_ref, gated_ref, rows)
     rates = rates_ref[...]
     decay = jnp.exp(-rates)
     scaled = residues_ref[...] * jnp.sqrt(2.0 * rates)
@@ -98,34 +101,278 @@
         out_ref[rows, :] = (queries_ref[rows, :].astype(jnp.float32) * mixed).astype(jnp.bfloat16)
         return state
 
-    lax.fori_loop(0, length // ROWS, body, entering)
-
-
-def convolve(queries, keys, values, states, residues, rates, gaps, spans, first, count):
-    tokens, channels = keys.shape
-    length, modes = tokens // spans, rates.shape[0]
+    lax.fori_loop(0, rows // ROWS, body, entering)
+
+
+def convolve(queries, keys, values, residues, rates, gaps, length, states, span, part, parts):
+    channels, modes, rows = keys.shape[1] // parts, rates.shape[0], length
     lanes = min(LANES, channels)
-    rows = pl.BlockSpec((length, lanes), lambda c, s, g: (first + s, c))
-    table = pl.BlockSpec((modes, lanes), lambda c, s, g: (0, c))
-    every = pl.BlockSpec((states.shape[0], modes, lanes), lambda c, s, g: (0, 0, c))
-    return pl.pallas_call(
-        functools.partial(convolve_kernel, first),
-        out_shape=jax.ShapeDtypeStruct((count * length, channels), jnp.bfloat16),
+    first = part * (channels // lanes)
+    data = pl.BlockSpec((rows, lanes), lambda c, g: (span, first + c))
+    table = pl.BlockSpec((modes, lanes), lambda c, g: (0, first + c))
+    every = pl.BlockSpec((states.shape[0], modes, lanes), lambda c, g: (0, 0, first + c))
+    return pl.pallas_call(
+        functools.partial(convolve_kernel, span, length),
+        out_shape=jax.ShapeDtypeStruct((rows, channels), jnp.bfloat16),
         grid_spec=pltpu.PrefetchScalarGridSpec(
             num_scalar_prefetch=1,
-            grid=(channels // lanes, count),
-            in_specs=[rows, rows, rows, every, table, table],
-            out_specs=pl.BlockSpec((length, lanes), lambda c, s, g: (s, c)),
-            scratch_shapes=[pltpu.VMEM((length, lanes), jnp.float32)],
+            grid=(channels // lanes,),
+            in_specs=[data, data, data, every, table, table],
+            out_specs=pl.BlockSpec((rows, lanes), lambda c, g: (0, c)),
+            scratch_shapes=[pltpu.VMEM((rows, lanes), jnp.float32)],
         ),
+        compiler_params=pltpu.CompilerParams(vmem_limit_bytes=16 << 20),
         name="convolve",
     )(gaps, queries, keys, values, states, residues, rates)
 
 
+def gather_weights(out_weight):
+    n, ctx = lax.axis_size("tp"), lax.axis_size("ctx")
+    me, mine = lax.axis_index("tp"), lax.axis_index("ctx")
+    channels, columns = out_weight.shape[0], out_weight.shape[1] // n
+    rows = channels // ctx
+    strip = lax.dynamic_slice_in_dim(out_weight, mine * rows, rows, 0)
+    pieces = []
+    for shift in range(1, n):
+        target = lax.rem(me + shift, n)
+        piece = lax.dynamic_slice_in_dim(strip, target * columns, columns, 1)
+        pieces.append(lax.ppermute(piece, "tp", [(i, (i + shift) % n) for i in range(n)]))
+    held = jnp.stack(pieces)
+    strips = {0: held}
+    for other in range(2, ctx, 2):
+        strips[other] = lax.ppermute(held, "ctx", [(i, i ^ other) for i in range(ctx)])
+    for other in range(0, ctx, 2):
+        strips[other + 1] = lax.ppermute(strips[other], "ctx", [(i, i ^ 1) for i in range(ctx)])
+    return [strips[other] for other in range(ctx)]
+
+
+def upper_kernel(n, ctx, parts, where_ref, *refs):
+    weight_ref, strips, refs = refs[0], refs[1 : 1 + ctx], refs[1 + ctx :]
+    sent, refs = refs[:parts], refs[parts:]
+    count = (n - 1) * parts
+    lefts, rights, refs = refs[:count], refs[count : 2 * count], refs[2 * count :]
+    out_ref, matrix_ref, whole_ref, total_ref, result_ref, weight_sem, strip_sem, sent_sem, moved_sem, out_sem = refs
+    columns = matrix_ref.shape[2]
+    height = matrix_ref.shape[1] // ctx
+    width = sent[0].shape[1]
+    me, mine = where_ref[0], where_ref[1]
+
+    own = pltpu.make_async_copy(
+        weight_ref.at[:, pl.ds(pl.multiple_of(me * columns, 128), columns)], matrix_ref.at[0], weight_sem
+    )
+    own.start()
+    kept = []
+    for part in range(parts):
+        copy = pltpu.make_async_copy(sent[part], whole_ref.at[0, :, pl.ds(part * width, width)], sent_sem.at[part])
+        copy.start()
+        kept.append(copy)
+    laid = []
+    for shift in range(1, n):
+        for part in range(parts):
+            at = (shift - 1) * parts + part
+            target = whole_ref.at[shift, :, pl.ds(part * width, width)]
+
+            @pl.when(me >= shift)
+            def _(at=at, target=target):
+                pltpu.make_async_copy(lefts[at], target, moved_sem.at[at]).start()
+
+            @pl.when(me < shift)
+            def _(at=at, target=target):
+                pltpu.make_async_copy(rights[at], target, moved_sem.at[at]).start()
+
+        for other in range(ctx):
+            row = pl.multiple_of(jnp.bitwise_xor(mine, other) * height, 16)
+            copy = pltpu.make_async_copy(
+                strips[other].at[shift - 1], matrix_ref.at[shift, pl.ds(row, height)], strip_sem.at[shift - 1, other]
+            )
+            copy.start()
+            laid.append(copy)
+    for shift in range(n):
+        if shift == 0:
+            own.wait()
+            for copy in kept:
+                copy.wait()
+        else:
+            for part in range(parts):
+                at = (shift - 1) * parts + part
+                target = whole_ref.at[shift, :, pl.ds(part * width, width)]
+                pltpu.make_async_copy(lefts[at], target, moved_sem.at[at]).wait()
+            for other in range(ctx):
+                laid[(shift - 1) * ctx + other].wait()
+
+        @pl.loop(0, columns // 256)
+        def _(step, shift=shift):
+            at = pl.ds(pl.multiple_of(step * 256, 256), 256)
+            piece = jnp.dot(whole_ref[shift], matrix_ref[shift, :, at], preferred_element_type=jnp.float32)
+            if shift == 0:
+                total_ref[:, at] = piece
+            elif shift < n - 1:
+                total_ref[:, at] += piece
+            else:
+                result_ref[:, at] = (total_ref[:, at] + piece).astype(jnp.bfloat16)
+
+    copy = pltpu.make_async_copy(result_ref, out_ref.at[pl.ds(0, sent[0].shape[0])], out_sem)
+    copy.start()
+    copy.wait()
+
+
+def upper(where, out_weight, strips, sent, lefts, rights, rows):
+    n, ctx, parts = lax.axis_size("tp"), lax.axis_size("ctx"), len(sent)
+    channels, columns = out_weight.shape[0], out_weight.shape[1] // n
+    tile = sent[0].shape[0]
+    anywhere = pl.BlockSpec(memory_space=pl.ANY)
+    operands = [out_weight, *strips, *sent, *lefts, *rights]
+    return pl.pallas_call(
+        functools.partial(upper_kernel, n, ctx, parts),
+        out_shape=jax.ShapeDtypeStruct((rows, columns), jnp.bfloat16),
+        grid_spec=pltpu.PrefetchScalarGridSpec(
+            num_scalar_prefetch=1,
+            grid=(1,),
+            in_specs=[anywhere] * len(operands),
+            out_specs=anywhere,
+            scratch_shapes=[
+                pltpu.VMEM((n, channels, columns), jnp.bfloat16),
+                pltpu.VMEM((n, tile, channels), jnp.bfloat16),
+                pltpu.VMEM((tile, columns), jnp.float32),
+                pltpu.VMEM((tile, columns), jnp.bfloat16),
+                pltpu.SemaphoreType.DMA(()),
+                pltpu.SemaphoreType.DMA((n - 1, ctx)),
+                pltpu.SemaphoreType.DMA((parts,)),
+                pltpu.SemaphoreType.DMA(((n - 1) * parts,)),
+                pltpu.SemaphoreType.DMA(()),
+            ],
+        ),
+        compiler_params=pltpu.CompilerParams(vmem_limit_bytes=24 << 20),
+        name="upper",
+    )(where, *operands)
+
+
+def finish_kernel(where_ref, unused_ref, product_ref, left_ref, right_ref, out_ref):
+    out_ref[...] = (
+        product_ref[...].astype(jnp.float32)
+        + left_ref[...].astype(jnp.float32)
+        + right_ref[...].astype(jnp.float32)
+    ).astype(jnp.bfloat16)
+
+
+def finish(where, result, product, left, right, part):
+    rows, columns = left.shape
+    tile, first = min(rows, TILE), result.shape[0] - left.shape[0]
+    moved = pl.BlockSpec((tile, columns), lambda i, w: (i, 0))
+    return pl.pallas_call(
+        finish_kernel,
+        out_shape=jax.ShapeDtypeStruct(result.shape, result.dtype),
+        grid_spec=pltpu.PrefetchScalarGridSpec(
+            num_scalar_prefetch=1,
+            grid=(rows // tile,),
+            in_specs=[
+                pl.BlockSpec(memory_space=pl.ANY),
+                pl.BlockSpec((tile, columns), lambda i, w: (i, w[0])),
+                moved,
+                moved,
+            ],
+            out_specs=pl.BlockSpec((tile, columns), lambda i, w: (first // tile + i, part)),
+        ),
+        input_output_aliases={1: 0},
+        compiler_params=pltpu.CompilerParams(vmem_limit_bytes=4 << 20),
+        name="finish",
+    )(where, result, product, left, right)
+
+
+def payload_kernel(step, where_ref, product_ref, ahead_ref, behind_ref, to_right_ref, to_left_ref):
+    width = ahead_ref.shape[1]
+    for column, source_ref, target_ref in ((0, ahead_ref, to_right_ref), (1, behind_ref, to_left_ref)):
+        at = pl.ds(pl.multiple_of(where_ref[step, column] * width, 128), width)
+        adds = where_ref[step, column + 2] > 0
+
+        @pl.when(adds)
+        def _(at=at, source_ref=source_ref, target_ref=target_ref):
+            @pl.loop(0, source_ref.shape[0] // 64)
+            def _(block):
+                rows = pl.ds(pl.multiple_of(block * 64, 64), 64)
+                target_ref[rows, :] = source_ref[rows, :] + product_ref[rows, at]
+
+        @pl.when(jnp.logical_not(adds))
+        def _(source_ref=source_ref, target_ref=target_ref):
+            @pl.loop(0, source_ref.shape[0] // 64)
+            def _(block):
+                rows = pl.ds(pl.multiple_of(block * 64, 64), 64)
+                target_ref[rows, :] = source_ref[rows, :]
+
+
+def payload(where, step, product, ahead, behind):
+    inside = pl.BlockSpec(memory_space=pltpu.VMEM)
+    return pl.pallas_call(
+        functools.partial(payload_kernel, step),
+        out_shape=[jax.ShapeDtypeStruct(ahead.shape, ahead.dtype)] * 2,
+        in_specs=[pl.BlockSpec(memory_space=pltpu.SMEM), inside, inside, inside],
+        out_specs=[inside, inside],
+        compiler_params=pltpu.CompilerParams(vmem_limit_bytes=1 << 20),
+        name="payload",
+    )(where, product, ahead, behind)
+
+
+def product_kernel(rows_ref, weight_ref, out_ref):
+    out_ref[...] = jnp.dot(rows_ref[...], weight_ref[...], preferred_element_type=jnp.float32).astype(jnp.bfloat16)
+
+
+def local_product(rows, out_weight, part, parts):
+    n = lax.axis_size("tp")
+    height, channels = rows.shape
+    width = out_weight.shape[1] // n // parts
+    return pl.pallas_call(
+        product_kernel,
+        out_shape=jax.ShapeDtypeStruct((height, n * width), jnp.bfloat16),
+        grid=(n,),
+        in_specs=[
+            pl.BlockSpec((height, channels), lambda s: (0, 0)),
+            pl.BlockSpec((channels, width), lambda s: (0, s * parts + part)),
+        ],
+        out_specs=pl.BlockSpec((height, width), lambda s: (0, s)),
+        compiler_params=pltpu.CompilerParams(vmem_limit_bytes=16 << 20),
+        name="local_product",
+    )(rows, out_weight)
+
+
+def exchange(sent, products):
+    n, parts = lax.axis_size("tp"), len(sent)
+    me = lax.axis_index("tp")
+    rights = [(i, i + 1) for i in range(n - 1)]
+    lefts = [(i + 1, i) for i in range(n - 1)]
+    ahead, behind = list(sent), list(sent)
+    from_left, from_right = {}, {}
+    steps = jnp.arange(n)
+    table = jnp.stack(
+        [
+            lax.rem(me + n - steps, n),
+            lax.rem(me + steps, n),
+            (me < steps).astype(jnp.int32),
+            (me >= n - steps).astype(jnp.int32),
+        ],
+        axis=1,
+    )
+    for slot in range(1, n + 1):
+        for part in range(parts):
+            right, left = ahead[part], behind[part]
+            if slot > 1:
+                right, left = payload(table, slot - 1, products[part], right, left)
+            right = lax.ppermute(right, "tp", rights)
+            left = lax.ppermute(left, "tp", lefts)
+            ahead[part], behind[part] = right, left
+            from_left[slot, part], from_right[slot, part] = right, left
+    return from_left, from_right
+
+
 def local(queries, keys, values, residues, rates, out_weight, span_order):
-    spans = span_order.shape[0] // lax.axis_size("ctx")
-    own = lax.dynamic_slice_in_dim(span_order, lax.axis_index("ctx") * spans, spans)
+    n, ctx = lax.axis_size("tp"), lax.axis_size("ctx")
+    me, mine = lax.axis_index("tp"), lax.axis_index("ctx")
+    tokens, channels = queries.shape
+    spans = span_order.shape[0] // ctx
+    length = tokens // spans
+    own = lax.dynamic_slice_in_dim(span_order, mine * spans, spans)
     gaps = own[:, None] - 1 - span_order[None, :]
+    lined = channels // ctx >= 128 and spans == 2
+    strips = gather_weights(out_weight) if lined else None
     totals = span_states(keys, values, rates, spans)
     half = totals.shape[1] // 2
     states = jnp.concatenate(
@@ -135,11 +382,27 @@
         ],
         axis=1,
     )
-    output = convolve(queries, keys, values, states, residues, rates, gaps, spans, 0, spans)
-    partial_value = jnp.dot(output, out_weight, preferred_element_type=jnp.float32).astype(
-        jnp.bfloat16
-    )
-    return lax.psum_scatter(partial_value, "tp", scatter_dimension=1, tiled=True)
+    conv = functools.partial(convolve, queries, keys, values, residues, rates, gaps, length, states)
+    if not lined:
+        outputs = [conv(span, 0, 1) for span in range(spans)]
+        part = jnp.dot(jnp.concatenate(outputs), out_weight, preferred_element_type=jnp.float32)
+        return lax.psum_scatter(part.astype(jnp.bfloat16), "tp", scatter_dimension=1, tiled=True)
+    sent, products = [], []
+    for part in range(PARTS):
+        sent.append(conv(0, part, PARTS))
+    rest = conv(1, 0, 1)
+    for part in range(PARTS):
+        products.append(local_product(rest, out_weight, part, PARTS))
+    from_left, from_right = exchange(sent, products)
+    where = jnp.stack([me, mine])
+    lefts = [from_left[shift, part] for shift in range(1, n) for part in range(PARTS)]
+    rights = [from_right[n - shift, part] for shift in range(1, n) for part in range(PARTS)]
+    result = upper(where, out_weight, strips, sent, lefts, rights, tokens)
+    for part in range(PARTS):
+        result = finish(
+            where, result, products[part], from_left[n, part], from_right[n, part], part
+        )
+    return result
 
 
 def solution(mesh):
@@ -152,6 +415,5 @@
         P("tp", None),
         P(),
     )
-    return jax.shard_map(
-        local, mesh=mesh, in_specs=placed, out_specs=P("ctx", "tp"), check_vma=False
-    )
+
+    return jax.shard_map(local, mesh=mesh, in_specs=placed, out_specs=P("ctx", "tp"), check_vma=False)

time: 225 us -> 209 us (0.929)
  waiting for transfers between devices: 145 us -> 68.1 us
  starting transfers between devices: 0.01 us -> 50.5 us
  Pallas kernels: 26.1 us -> 52.5 us
  matrix products: 14.7 us -> 0 us
  between operations: 13.4 us -> 0.51 us
  local copies, waits for them, and re-layouts: 0.88 us -> 13.3 us
    reduce_scatter x1 -> x0, waiting for transfers between devices: 145 us -> none  [local(): lax.psum_scatter(partial_value, 'tp', scatter_dimension=1, tiled=True)]
    ppermute x0 -> x26, waiting for transfers between devices: none -> 68.1 us  [the longest x8 24.8 us: exchange(): left = lax.ppermute(left, 'tp', lefts)]
    ppermute x0 -> x26, starting transfers between devices: none -> 50.5 us  [the longest x8 30.8 us: exchange(): right = lax.ppermute(right, 'tp', rights)]
    pallas_call x1 -> x14, Pallas kernels: 18.7 us -> 46.6 us  [the longest x3 19.2 us: convolve(): pl.pallas_call(functools.partial(convolve_kernel, span, length), out_shap...]
    dot_general x1 -> x0, matrix products: 14.7 us -> none  [local(): jnp.dot(output, out_weight, preferred_element_type=jnp.float32)]
    unnamed x0 -> x31, local copies, waits for them, and re-layouts: none -> 12.8 us
  transfers between devices with their start and end apart: 1 -> 26, of which waited for: 1 -> 8; matrix products, arithmetic and copies ran while one was open for 0% -> 0% of each run, Pallas kernels for 0% -> 19%
where the time goes in v2:
time: 209 us; the launch traced here: 208 us
  waiting for transfers between devices  68.1 us (33%)
  Pallas kernels  52.5 us (25%)
  starting transfers between devices  50.5 us (24%)
  blocking collectives  21.3 us (10%)
  local copies, waits for them, and re-layouts  13.3 us (6%)
    ppermute x8, starting transfers between devices, exchange(): right = lax.ppermute(right, 'tp', rights)  30.8 us
    ppermute x8, waiting for transfers between devices, exchange(): left = lax.ppermute(left, 'tp', lefts)  24.8 us
    ppermute x3, waiting for transfers between devices, gather_weights(): lax.ppermute(piece, 'tp', [(i, (i + shift) % n) for i in range(n)])  23.3 us
    ppermute x3, waiting for transfers between devices, gather_weights(): lax.ppermute(held, 'ctx', [(i, i ^ other) for i in range(ctx)])  20.1 us
    pallas_call x3, Pallas kernels, convolve(): pl.pallas_call(functools.partial(convolve_kernel, span, length), out_shap...  19.2 us
    unnamed x31, local copies, waits for them, and re-layouts  12.8 us
    all_gather x1, blocking collectives, local(): lax.all_gather(totals[:, :half], 'ctx', axis=0, tiled=True)  11.5 us
    pallas_call x1, Pallas kernels, upper(): pl.pallas_call(functools.partial(upper_kernel, n, ctx, parts), out_shape=...  10.7 us
  transfers between devices with their start and end apart: 26, of which 8 were waited for; matrix products, arithmetic and copies ran while one was open for 0% of the time, Pallas kernels for 19%

profile of v2, /device:TPU:0, one launch (start us, length us, event | category | flops | bytes accessed | tf_op | source)
XLA Modules:
  0.0 208.0 jit_solution(13965611782426625100)
XLA Ops:
  5.5 5.9 %span_states.1 = f32[2,16,1024]{2,1,0:T(8,128)S(1)} custom-call(bf16[1024,1024]{1,0:T(8,128)(2,1)S(1)} %copy-done.1, bf16[1024,1024]{1,0:T(8,128)(2,1)S(1)} %copy-done.3, f32[16,1024]{1,0:T(8,128)S(1)} %copy-done.10), custom_call_target="tpu_custom_call" | custom-call | tf_op jit(solution)/shard_map/span_states/pallas_call | solution.py:45
  11.4 11.5 %all_gather.6 = f32[16,8,1024]{2,1,0:T(8,128)S(1)} all-gather(f32[2,8,1024]{2,1,0:T(8,128)S(1)} %get-tuple-element.33), channel_id=1, replica_groups=mesh['ctx'=8,'tp'=4] {'ctx'}, dimensions={0}, use_global_device_ids=true | all-gather | bytes 589824 | tf_op jit(solution)/shard_map/all_gather | solution.py:380
  23.0 9.8 %all_gather.7 = f32[16,8,1024]{2,1,0:T(8,128)S(1)} all-gather(f32[2,8,1024]{2,1,0:T(8,128)S(1)} %get-tuple-element.32), channel_id=1, replica_groups=mesh['ctx'=8,'tp'=4] {'ctx'}, dimensions={0}, use_global_device_ids=true | all-gather | bytes 589824 | tf_op jit(solution)/shard_map/all_gather | solution.py:381
  32.9 5.3 %convolve.3.refs_9_ = bf16[512,512]{1,0:T(8,128)(2,1)} custom-call(s32[2,16]{1,0:T(2,128)S(1)} %broadcast_subtract_fusion.gaps_ref, bf16[1024,1024]{1,0:T(8,128)(2,1)S(1)} %copy-done.6, bf16[1024,1024]{1,0:T(8,128)(2,1)S(1)} %copy-done.2, bf16[1024,1024]{1,0:T(8,128)(2,1)S(1)} %copy-done.4, f32[16,16,1024]{2,1,0:T(8,128)S(1)} %constant_dynamic-update-slice_fusion.states_ref, ...), custom_call_target="tpu_custom_call" | custom-call | tf_op jit(solution)/shard_map/convolve/pallas_call | solution.py:114
  38.2 4.3 %collective-permute-start.10 = (bf16[512,512]{1,0:T(8,128)(2,1)}, bf16[512,512]{1,0:T(8,128)(2,1)}, u32[]{:S(2)}, u32[]{:S(2)}) collective-permute-start(bf16[512,512]{1,0:T(8,128)(2,1)} %convolve.3.refs_9_), channel_id=1, source_target_pairs={{0,1},{1,2},{2,3},{4,5},{5,6},{6,7},{8,9},{9,10},{10,11},{12,13},{... | collective-permute-start | bytes 1572872 | tf_op jit(solution)/shard_map/ppermute | solution.py:359
  43.8 5.3 %convolve.4.refs_10_ = bf16[512,512]{1,0:T(8,128)(2,1)} custom-call(s32[2,16]{1,0:T(2,128)S(1)} %broadcast_subtract_fusion.gaps_ref, bf16[1024,1024]{1,0:T(8,128)(2,1)S(1)} %copy-done.6, bf16[1024,1024]{1,0:T(8,128)(2,1)S(1)} %copy-done.2, bf16[1024,1024]{1,0:T(8,128)(2,1)S(1)} %copy-done.4, ...), custom_call_target="tpu_custom_call" | custom-call | tf_op jit(solution)/shard_map/convolve/pallas_call | solution.py:114
  49.1 5.3 %collective-permute-start.11 = (bf16[512,512]{1,0:T(8,128)(2,1)}, bf16[512,512]{1,0:T(8,128)(2,1)}, u32[]{:S(2)}, u32[]{:S(2)}) collective-permute-start(bf16[512,512]{1,0:T(8,128)(2,1)} %convolve.4.refs_10_), channel_id=1, source_target_pairs={{0,1},{1,2},{2,3},{4,5},{5,6},{6,7},{8,9},{9,10},{10,11},{12,13},{... | collective-permute-start | bytes 1572872 | tf_op jit(solution)/shard_map/ppermute | solution.py:359
  58.9 8.7 %convolve.5.rows_ref = bf16[512,1024]{1,0:T(8,128)(2,1)S(1)} custom-call(s32[2,16]{1,0:T(2,128)S(1)} %broadcast_subtract_fusion.gaps_ref, bf16[1024,1024]{1,0:T(8,128)(2,1)S(1)} %copy-done.7, bf16[1024,1024]{1,0:T(8,128)(2,1)S(1)} %copy-done.2, bf16[1024,1024]{1,0:T(8,128)(2,1)S(1)} %copy-done.5, ...), custom_call_target="tpu_custom_call" | custom-call | tf_op jit(solution)/shard_map/convolve/pallas_call | solution.py:114
  68.6 3.4 %copy-done = bf16[1024,4096]{1,0:T(8,128)(2,1)S(1)} copy-done((bf16[1024,4096]{1,0:T(8,128)(2,1)S(1)}, bf16[1024,4096]{1,0:T(8,128)(2,1)}, u32[]{:S(2)}) %copy-start) | copy-done | bytes 8388632
  73.2 3.3 %local_product.2.product_ref = bf16[512,2048]{1,0:T(8,128)(2,1)S(1)} custom-call(bf16[512,1024]{1,0:T(8,128)(2,1)S(1)} %copy-done.9, bf16[1024,4096]{1,0:T(8,128)(2,1)S(1)} %copy-done), custom_call_target="tpu_custom_call" | custom-call | tf_op jit(solution)/shard_map/local_product/pallas_call | solution.py:323
  78.4 4.6 %collective-permute-start.13 = (bf16[512,512]{1,0:T(8,128)(2,1)S(1)}, bf16[512,512]{1,0:T(8,128)(2,1)S(1)}, u32[]{:S(2)}, u32[]{:S(2)}) collective-permute-start(bf16[512,512]{1,0:T(8,128)(2,1)S(1)} %get-tuple-element.17), channel_id=1, source_target_pairs={{0,1},{1,2},{2,3},{4,5},{5,6},{6,7},{8,9},{9,10},{10,11},{12,13},{... | collective-permute-start | bytes 1572872 | tf_op jit(solution)/shard_map/ppermute | solution.py:359
  89.7 3.3 %local_product.3.product_ref = bf16[512,2048]{1,0:T(8,128)(2,1)S(1)} custom-call(bf16[512,1024]{1,0:T(8,128)(2,1)S(1)} %copy-done.9, bf16[1024,4096]{1,0:T(8,128)(2,1)S(1)} %copy-done), custom_call_target="tpu_custom_call" | custom-call | tf_op jit(solution)/shard_map/local_product/pallas_call | solution.py:323
  94.5 6.4 %collective-permute-done.2 = bf16[128,1024]{1,0:T(8,128)(2,1)S(1)} collective-permute-done((bf16[128,1024]{1,0:T(8,128)(2,1)S(1)}, bf16[128,1024]{1,0:T(8,128)(2,1)S(1)}, u32[]{:S(2)}, u32[]{:S(2)}) %collective-permute-start.2) | collective-permute-done | bytes 262176 | tf_op jit(solution)/shard_map/ppermute | solution.py:139
  102.2 16.9 %collective-permute-done.1 = bf16[128,1024]{1,0:T(8,128)(2,1)S(1)} collective-permute-done((bf16[128,1024]{1,0:T(8,128)(2,1)S(1)}, bf16[128,1024]{1,0:T(8,128)(2,1)S(1)}, u32[]{:S(2)}, u32[]{:S(2)}) %collective-permute-start.1) | collective-permute-done | bytes 262176 | tf_op jit(solution)/shard_map/ppermute | solution.py:139
  124.8 5.3 %collective-permute-start.17 = (bf16[512,512]{1,0:T(8,128)(2,1)S(1)}, bf16[512,512]{1,0:T(8,128)(2,1)S(1)}, u32[]{:S(2)}, u32[]{:S(2)}) collective-permute-start(bf16[512,512]{1,0:T(8,128)(2,1)S(1)} %get-tuple-element.20), channel_id=1, source_target_pairs={{0,1},{1,2},{2,3},{4,5},{5,6},{6,7},{8,9},{9,10},{10,11},{12,13},{... | collective-permute-start | bytes 1572872 | tf_op jit(solution)/shard_map/ppermute | solution.py:359
  130.1 3.1 %collective-permute-done.18.behind_ref.refs_20_ = bf16[512,512]{1,0:T(8,128)(2,1)S(1)} collective-permute-done((bf16[512,512]{1,0:T(8,128)(2,1)S(1)}, bf16[512,512]{1,0:T(8,128)(2,1)S(1)}, u32[]{:S(2)}, u32[]{:S(2)}) %collective-permute-start.18) | collective-permute-done | bytes 524320 | tf_op jit(solution)/shard_map/ppermute | solution.py:360
  135.4 5.6 %collective-permute-done.4.refs_3_ = bf16[3,128,1024]{2,1,0:T(8,128)(2,1)S(1)} collective-permute-done((bf16[3,128,1024]{2,1,0:T(8,128)(2,1)S(1)}, bf16[3,128,1024]{2,1,0:T(8,128)(2,1)S(1)}, u32[]{:S(2)}, u32[]{:S(2)}) %collective-permute-start.4) | collective-permute-done | bytes 786464 | tf_op jit(solution)/shard_map/ppermute | solution.py:143
  141.0 14.5 %collective-permute-done.6.refs_5_ = bf16[3,128,1024]{2,1,0:T(8,128)(2,1)S(1)} collective-permute-done((bf16[3,128,1024]{2,1,0:T(8,128)(2,1)S(1)}, bf16[3,128,1024]{2,1,0:T(8,128)(2,1)S(1)}, u32[]{:S(2)}, u32[]{:S(2)}) %collective-permute-start.6) | collective-permute-done | bytes 786464 | tf_op jit(solution)/shard_map/ppermute | solution.py:143
  158.7 11.9 %collective-permute-done.20.refs_17_.behind_ref = bf16[512,512]{1,0:T(8,128)(2,1)S(1)} collective-permute-done((bf16[512,512]{1,0:T(8,128)(2,1)S(1)}, bf16[512,512]{1,0:T(8,128)(2,1)S(1)}, u32[]{:S(2)}, u32[]{:S(2)}) %collective-permute-start.20) | collective-permute-done | bytes 524320 | tf_op jit(solution)/shard_map/ppermute | solution.py:360
  171.4 6.8 %collective-permute-done.21.refs_18_.behind_ref = bf16[512,512]{1,0:T(8,128)(2,1)S(1)} collective-permute-done((bf16[512,512]{1,0:T(8,128)(2,1)S(1)}, bf16[512,512]{1,0:T(8,128)(2,1)S(1)}, u32[]{:S(2)}, u32[]{:S(2)}) %collective-permute-start.21) | collective-permute-done | bytes 524320 | tf_op jit(solution)/shard_map/ppermute | solution.py:360
  178.1 3.9 %collective-permute-start.22 = (bf16[512,512]{1,0:T(8,128)(2,1)S(1)}, bf16[512,512]{1,0:T(8,128)(2,1)S(1)}, u32[]{:S(2)}, u32[]{:S(2)}) collective-permute-start(bf16[512,512]{1,0:T(8,128)(2,1)S(1)} %get-tuple-element.25), channel_id=1, source_target_pairs={{0,1},{1,2},{2,3},{4,5},{5,6},{6,7},{8,9},{9,10},{10,11},{12,13},{... | collective-permute-start | bytes 1572872 | tf_op jit(solution)/shard_map/ppermute | solution.py:359
  184.2 4.6 %collective-permute-start.24 = (bf16[512,512]{1,0:T(8,128)(2,1)S(1)}, bf16[512,512]{1,0:T(8,128)(2,1)S(1)}, u32[]{:S(2)}, u32[]{:S(2)}) collective-permute-start(bf16[512,512]{1,0:T(8,128)(2,1)S(1)} %get-tuple-element.27), channel_id=1, source_target_pairs={{0,1},{1,2},{2,3},{4,5},{5,6},{6,7},{8,9},{9,10},{10,11},{12,13},{... | collective-permute-start | bytes 1572872 | tf_op jit(solution)/shard_map/ppermute | solution.py:359
  190.1 10.7 %upper.1.unused_ref = bf16[1024,1024]{1,0:T(8,128)(2,1)} custom-call(s32[2]{0:T(128)S(1)} %pad_add_fusion.1.where_ref, bf16[1024,4096]{1,0:T(8,128)(2,1)S(1)} %bitcast.6, bf16[3,128,1024]{2,1,0:T(8,128)(2,1)S(1)} %pad_maximum_fusion.refs_1_, bf16[3,128,1024]{2,1,0:T(8,128)(2,1)S(1)} %collective-permute-done.3.refs_2_, ...), custom_call_target="tpu_custom_call" | custom-call | tf_op jit(solution)/shard_map/upper/pallas_call | solution.py:225
  203.0 2.9 %collective-permute-done.25.right_ref = bf16[512,512]{1,0:T(8,128)(2,1)S(1)} collective-permute-done((bf16[512,512]{1,0:T(8,128)(2,1)S(1)}, bf16[512,512]{1,0:T(8,128)(2,1)S(1)}, u32[]{:S(2)}, u32[]{:S(2)}) %collective-permute-start.25) | collective-permute-done | bytes 524320 | tf_op jit(solution)/shard_map/ppermute | solution.py:360
  (87 shorter events, 44.3 us)
Async XLA Ops:
  38.2 38.9 %collective-permute-start.10 = (bf16[512,512]{1,0:T(8,128)(2,1)}, bf16[512,512]{1,0:T(8,128)(2,1)}, u32[]{:S(2)}, u32[]{:S(2)}) collective-permute-start(bf16[512,512]{1,0:T(8,128)(2,1)} %convolve.3.refs_9_), channel_id=1, source_target_pairs={{0,1},{1,2},{2,3},{4,5},{5,6},{6,7},{8,9},{9,10},{10,11},{12,13},{... | collective-permute-start | bytes 1572872 | tf_op jit(solution)/shard_map/ppermute | solution.py:359
  42.5 34.6 %collective-permute-start.12 = (bf16[512,512]{1,0:T(8,128)(2,1)}, bf16[512,512]{1,0:T(8,128)(2,1)}, u32[]{:S(2)}, u32[]{:S(2)}) collective-permute-start(bf16[512,512]{1,0:T(8,128)(2,1)} %convolve.3.refs_9_), channel_id=1, source_target_pairs={{1,0},{2,1},{3,2},{5,4},{6,5},{7,6},{9,8},{10,9},{11,10},{13,12},{... | collective-permute-start | bytes 1572872 | tf_op jit(solution)/shard_map/ppermute | solution.py:360
  49.1 36.6 %collective-permute-start.11 = (bf16[512,512]{1,0:T(8,128)(2,1)}, bf16[512,512]{1,0:T(8,128)(2,1)}, u32[]{:S(2)}, u32[]{:S(2)}) collective-permute-start(bf16[512,512]{1,0:T(8,128)(2,1)} %convolve.4.refs_10_), channel_id=1, source_target_pairs={{0,1},{1,2},{2,3},{4,5},{5,6},{6,7},{8,9},{9,10},{10,11},{12,13},{... | collective-permute-start | bytes 1572872 | tf_op jit(solution)/shard_map/ppermute | solution.py:359
  54.4 34.1 %collective-permute-start.14 = (bf16[512,512]{1,0:T(8,128)(2,1)}, bf16[512,512]{1,0:T(8,128)(2,1)}, u32[]{:S(2)}, u32[]{:S(2)}) collective-permute-start(bf16[512,512]{1,0:T(8,128)(2,1)} %convolve.4.refs_10_), channel_id=1, source_target_pairs={{1,0},{2,1},{3,2},{5,4},{6,5},{7,6},{9,8},{10,9},{11,10},{13,12},{... | collective-permute-start | bytes 1572872 | tf_op jit(solution)/shard_map/ppermute | solution.py:360
  78.4 42.7 %collective-permute-start.13 = (bf16[512,512]{1,0:T(8,128)(2,1)S(1)}, bf16[512,512]{1,0:T(8,128)(2,1)S(1)}, u32[]{:S(2)}, u32[]{:S(2)}) collective-permute-start(bf16[512,512]{1,0:T(8,128)(2,1)S(1)} %get-tuple-element.17), channel_id=1, source_target_pairs={{0,1},{1,2},{2,3},{4,5},{5,6},{6,7},{8,9},{9,10},{10,11},{12,13},{... | collective-permute-start | bytes 1572872 | tf_op jit(solution)/shard_map/ppermute | solution.py:359
  83.0 17.9 %collective-permute-start.2 = (bf16[128,1024]{1,0:T(8,128)(2,1)S(1)}, bf16[128,1024]{1,0:T(8,128)(2,1)S(1)}, u32[]{:S(2)}, u32[]{:S(2)}) collective-permute-start(bf16[128,1024]{1,0:T(8,128)(2,1)S(1)} %get-tuple-element.30), channel_id=1, source_target_pairs={{0,3},{1,0},{2,1},{3,2},{4,7},{5,4},{6,5},{7,6},{8,11},{9,8},{10,9... | collective-permute-start | bytes 786440 | tf_op jit(solution)/shard_map/ppermute | solution.py:139
  84.4 38.2 %collective-permute-start.16 = (bf16[512,512]{1,0:T(8,128)(2,1)S(1)}, bf16[512,512]{1,0:T(8,128)(2,1)S(1)}, u32[]{:S(2)}, u32[]{:S(2)}) collective-permute-start(bf16[512,512]{1,0:T(8,128)(2,1)S(1)} %get-tuple-element.19), channel_id=1, source_target_pairs={{1,0},{2,1},{3,2},{5,4},{6,5},{7,6},{9,8},{10,9},{11,10},{13,12},{... | collective-permute-start | bytes 1572872 | tf_op jit(solution)/shard_map/ppermute | solution.py:360
  85.7 33.4 %collective-permute-start.1 = (bf16[128,1024]{1,0:T(8,128)(2,1)S(1)}, bf16[128,1024]{1,0:T(8,128)(2,1)S(1)}, u32[]{:S(2)}, u32[]{:S(2)}) collective-permute-start(bf16[128,1024]{1,0:T(8,128)(2,1)S(1)} %get-tuple-element.31), channel_id=1, source_target_pairs={{0,2},{1,3},{2,0},{3,1},{4,6},{5,7},{6,4},{7,5},{8,10},{9,11},{10,... | collective-permute-start | bytes 786440 | tf_op jit(solution)/shard_map/ppermute | solution.py:139
  88.5 31.9 %collective-permute-start = (bf16[128,1024]{1,0:T(8,128)(2,1)S(1)}, bf16[128,1024]{1,0:T(8,128)(2,1)S(1)}, u32[]{:S(2)}, u32[]{:S(2)}) collective-permute-start(bf16[128,1024]{1,0:T(8,128)(2,1)S(1)} %get-tuple-element.29), channel_id=1, source_target_pairs={{0,1},{1,2},{2,3},{3,0},{4,5},{5,6},{6,7},{7,4},{8,9},{9,10},{10,1... | collective-permute-start | bytes 786440 | tf_op jit(solution)/shard_map/ppermute | solution.py:139
  100.9 23.9 %collective-permute-start.15 = (bf16[512,512]{1,0:T(8,128)(2,1)S(1)}, bf16[512,512]{1,0:T(8,128)(2,1)S(1)}, u32[]{:S(2)}, u32[]{:S(2)}) collective-permute-start(bf16[512,512]{1,0:T(8,128)(2,1)S(1)} %get-tuple-element.18), channel_id=1, source_target_pairs={{0,1},{1,2},{2,3},{4,5},{5,6},{6,7},{8,9},{9,10},{10,11},{12,13},{... | collective-permute-start | bytes 1572872 | tf_op jit(solution)/shard_map/ppermute | solution.py:359
  120.5 20.5 %collective-permute-start.4 = (bf16[3,128,1024]{2,1,0:T(8,128)(2,1)S(1)}, bf16[3,128,1024]{2,1,0:T(8,128)(2,1)S(1)}, u32[]{:S(2)}, u32[]{:S(2)}) collective-permute-start(bf16[3,128,1024]{2,1,0:T(8,128)(2,1)S(1)} %pad_maximum_fusion.refs_1_), channel_id=1, source_target_pairs={{0,8},{4,12},{8,0},{12,4},{16,24},{20,28},{24,16},{28,20},{1,9},{5... | collective-permute-start | bytes 2359304 | tf_op jit(solution)/shard_map/ppermute | solution.py:143
  121.1 34.4 %collective-permute-start.6 = (bf16[3,128,1024]{2,1,0:T(8,128)(2,1)S(1)}, bf16[3,128,1024]{2,1,0:T(8,128)(2,1)S(1)}, u32[]{:S(2)}, u32[]{:S(2)}) collective-permute-start(bf16[3,128,1024]{2,1,0:T(8,128)(2,1)S(1)} %pad_maximum_fusion.refs_1_), channel_id=1, source_target_pairs={{0,16},{4,20},{8,24},{12,28},{16,0},{20,4},{24,8},{28,12},{1,17},{... | collective-permute-start | bytes 2359304 | tf_op jit(solution)/shard_map/ppermute | solution.py:143
  122.6 34.2 %collective-permute-start.8 = (bf16[3,128,1024]{2,1,0:T(8,128)(2,1)S(1)}, bf16[3,128,1024]{2,1,0:T(8,128)(2,1)S(1)}, u32[]{:S(2)}, u32[]{:S(2)}) collective-permute-start(bf16[3,128,1024]{2,1,0:T(8,128)(2,1)S(1)} %pad_maximum_fusion.refs_1_), channel_id=1, source_target_pairs={{0,24},{4,28},{8,16},{12,20},{16,8},{20,12},{24,0},{28,4},{1,25},{... | collective-permute-start | bytes 2359304 | tf_op jit(solution)/shard_map/ppermute | solution.py:143
  124.8 32.1 %collective-permute-start.17 = (bf16[512,512]{1,0:T(8,128)(2,1)S(1)}, bf16[512,512]{1,0:T(8,128)(2,1)S(1)}, u32[]{:S(2)}, u32[]{:S(2)}) collective-permute-start(bf16[512,512]{1,0:T(8,128)(2,1)S(1)} %get-tuple-element.20), channel_id=1, source_target_pairs={{0,1},{1,2},{2,3},{4,5},{5,6},{6,7},{8,9},{9,10},{10,11},{12,13},{... | collective-permute-start | bytes 1572872 | tf_op jit(solution)/shard_map/ppermute | solution.py:359
  133.9 23.5 %collective-permute-start.19 = (bf16[512,512]{1,0:T(8,128)(2,1)S(1)}, bf16[512,512]{1,0:T(8,128)(2,1)S(1)}, u32[]{:S(2)}, u32[]{:S(2)}) collective-permute-start(bf16[512,512]{1,0:T(8,128)(2,1)S(1)} %get-tuple-element.22), channel_id=1, source_target_pairs={{0,1},{1,2},{2,3},{4,5},{5,6},{6,7},{8,9},{9,10},{10,11},{12,13},{... | collective-permute-start | bytes 1572872 | tf_op jit(solution)/shard_map/ppermute | solution.py:359
  141.0 41.9 %collective-permute-start.3 = (bf16[3,128,1024]{2,1,0:T(8,128)(2,1)S(1)}, bf16[3,128,1024]{2,1,0:T(8,128)(2,1)S(1)}, u32[]{:S(2)}, u32[]{:S(2)}) collective-permute-start(bf16[3,128,1024]{2,1,0:T(8,128)(2,1)S(1)} %pad_maximum_fusion.refs_1_), channel_id=1, source_target_pairs={{0,4},{4,0},{8,12},{12,8},{16,20},{20,16},{24,28},{28,24},{1,5},{5... | collective-permute-start | bytes 2359304 | tf_op jit(solution)/shard_map/ppermute | solution.py:145
  156.8 27.3 %collective-permute-start.5 = (bf16[3,128,1024]{2,1,0:T(8,128)(2,1)S(1)}, bf16[3,128,1024]{2,1,0:T(8,128)(2,1)S(1)}, u32[]{:S(2)}, u32[]{:S(2)}) collective-permute-start(bf16[3,128,1024]{2,1,0:T(8,128)(2,1)S(1)} %collective-permute-done.4.refs_3_), channel_id=1, source_target_pairs={{0,4},{4,0},{8,12},{12,8},{16,20},{20,16},{24,28},{28,24},{1,5},{5... | collective-permute-start | bytes 2359304 | tf_op jit(solution)/shard_map/ppermute | solution.py:145
  156.9 31.9 %collective-permute-start.7 = (bf16[3,128,1024]{2,1,0:T(8,128)(2,1)S(1)}, bf16[3,128,1024]{2,1,0:T(8,128)(2,1)S(1)}, u32[]{:S(2)}, u32[]{:S(2)}) collective-permute-start(bf16[3,128,1024]{2,1,0:T(8,128)(2,1)S(1)} %collective-permute-done.6.refs_5_), channel_id=1, source_target_pairs={{0,4},{4,0},{8,12},{12,8},{16,20},{20,16},{24,28},{28,24},{1,5},{5... | collective-permute-start | bytes 2359304 | tf_op jit(solution)/shard_map/ppermute | solution.py:145
  157.4 20.8 %collective-permute-start.21 = (bf16[512,512]{1,0:T(8,128)(2,1)S(1)}, bf16[512,512]{1,0:T(8,128)(2,1)S(1)}, u32[]{:S(2)}, u32[]{:S(2)}) collective-permute-start(bf16[512,512]{1,0:T(8,128)(2,1)S(1)} %get-tuple-element.24), channel_id=1, source_target_pairs={{1,0},{2,1},{3,2},{5,4},{6,5},{7,6},{9,8},{10,9},{11,10},{13,12},{... | collective-permute-start | bytes 1572872 | tf_op jit(solution)/shard_map/ppermute | solution.py:360
  170.6 19.5 %collective-permute-start.9 = (bf16[3,128,1024]{2,1,0:T(8,128)(2,1)S(1)}, bf16[3,128,1024]{2,1,0:T(8,128)(2,1)S(1)}, u32[]{:S(2)}, u32[]{:S(2)}) collective-permute-start(bf16[3,128,1024]{2,1,0:T(8,128)(2,1)S(1)} %collective-permute-done.8.refs_7_), channel_id=1, source_target_pairs={{0,4},{4,0},{8,12},{12,8},{16,20},{20,16},{24,28},{28,24},{1,5},{5... | collective-permute-start | bytes 2359304 | tf_op jit(solution)/shard_map/ppermute | solution.py:145
  178.1 22.7 %collective-permute-start.22 = (bf16[512,512]{1,0:T(8,128)(2,1)S(1)}, bf16[512,512]{1,0:T(8,128)(2,1)S(1)}, u32[]{:S(2)}, u32[]{:S(2)}) collective-permute-start(bf16[512,512]{1,0:T(8,128)(2,1)S(1)} %get-tuple-element.25), channel_id=1, source_target_pairs={{0,1},{1,2},{2,3},{4,5},{5,6},{6,7},{8,9},{9,10},{10,11},{12,13},{... | collective-permute-start | bytes 1572872 | tf_op jit(solution)/shard_map/ppermute | solution.py:359
  182.8 18.0 %collective-permute-start.23 = (bf16[512,512]{1,0:T(8,128)(2,1)S(1)}, bf16[512,512]{1,0:T(8,128)(2,1)S(1)}, u32[]{:S(2)}, u32[]{:S(2)}) collective-permute-start(bf16[512,512]{1,0:T(8,128)(2,1)S(1)} %get-tuple-element.26), channel_id=1, source_target_pairs={{1,0},{2,1},{3,2},{5,4},{6,5},{7,6},{9,8},{10,9},{11,10},{13,12},{... | collective-permute-start | bytes 1572872 | tf_op jit(solution)/shard_map/ppermute | solution.py:360
  184.2 18.9 %collective-permute-start.24 = (bf16[512,512]{1,0:T(8,128)(2,1)S(1)}, bf16[512,512]{1,0:T(8,128)(2,1)S(1)}, u32[]{:S(2)}, u32[]{:S(2)}) collective-permute-start(bf16[512,512]{1,0:T(8,128)(2,1)S(1)} %get-tuple-element.27), channel_id=1, source_target_pairs={{0,1},{1,2},{2,3},{4,5},{5,6},{6,7},{8,9},{9,10},{10,11},{12,13},{... | collective-permute-start | bytes 1572872 | tf_op jit(solution)/shard_map/ppermute | solution.py:359
  188.7 17.2 %collective-permute-start.25 = (bf16[512,512]{1,0:T(8,128)(2,1)S(1)}, bf16[512,512]{1,0:T(8,128)(2,1)S(1)}, u32[]{:S(2)}, u32[]{:S(2)}) collective-permute-start(bf16[512,512]{1,0:T(8,128)(2,1)S(1)} %get-tuple-element.28), channel_id=1, source_target_pairs={{1,0},{2,1},{3,2},{5,4},{6,5},{7,6},{9,8},{10,9},{11,10},{13,12},{... | collective-permute-start | bytes 1572872 | tf_op jit(solution)/shard_map/ppermute | solution.py:360
  (17 other events, 323.6 us)

commit v3 on v2

v3 whole, which is shorter than its diff:
```python
import functools

import jax
import jax.numpy as jnp
from jax import lax
from jax.experimental import pallas as pl
from jax.experimental.pallas import tpu as pltpu
from jax.sharding import PartitionSpec as P


ROWS = 16
LANES = 512
PARTS = 2


def states_kernel(
    spans, keys_ref, values_ref, rates_ref, out_ref, gated_ref, keys_buf, values_buf, gated_buf, rows_buf, sems
):
    tokens, channels = gated_ref.shape
    length, lanes = tokens // spans, keys_buf.shape[2]
    groups = [(span, first) for first in range(0, channels, lanes) for span in range(spans)]
    copies = []
    for index, (span, first) in enumerate(groups):
        at = (pl.ds(span * length, length), pl.ds(first, lanes))
        pair = [
            pltpu.make_async_copy(keys_ref.at[at], keys_buf.at[index], sems.at[0, index]),
            pltpu.make_async_copy(values_ref.at[at], values_buf.at[index], sems.at[1, index]),
        ]
        for copy in pair:
            copy.start()
        copies.append(pair)
    for index, (span, first) in enumerate(groups):
        for copy in copies[index]:
            copy.wait()
        across = pl.ds(first, lanes)
        decay = jnp.exp(-rates_ref[:, across])

        def body(step, state, index=index, span=span, across=across, decay=decay):
            base = pl.multiple_of(step * ROWS, ROWS)
            rows = pl.ds(base, ROWS)
            keys = keys_buf[index, rows, :].astype(jnp.float32)
            gated = (keys * values_buf[index, rows, :].astype(jnp.float32)).astype(jnp.bfloat16)
            gated_buf[index, rows, :] = gated
            rows_buf[rows, :] = gated.astype(jnp.float32)
            for row in range(ROWS):
                state = decay * state + rows_buf[pl.ds(base + row, 1), :]
            return state

        zero = jnp.zeros(decay.shape, jnp.float32)
        out_ref[span, :, across] = lax.fori_loop(0, length // ROWS, body, zero)
        copy = pltpu.make_async_copy(
            gated_buf.at[index], gated_ref.at[pl.ds(span * length, length), across], sems.at[2, index]
        )
        copy.start()
        copies[index] = copy
    for copy in copies:
        copy.wait()


def span_states(keys, values, rates, spans):
    tokens, channels = keys.shape
    length, modes = tokens // spans, rates.shape[0]
    lanes = min(LANES, channels)
    count = spans * (channels // lanes)
    inside = pl.BlockSpec(memory_space=pltpu.VMEM)
    outside = pl.BlockSpec(memory_space=pltpu.HBM)
    return pl.pallas_call(
        functools.partial(states_kernel, spans),
        out_shape=[
            jax.ShapeDtypeStruct((spans, modes, channels), jnp.float32),
            jax.ShapeDtypeStruct((tokens, channels), jnp.bfloat16),
        ],
        in_specs=[outside, outside, inside],
        out_specs=[inside, outside],
        scratch_shapes=[
            pltpu.VMEM((count, length, lanes), jnp.bfloat16),
            pltpu.VMEM((count, length, lanes), jnp.bfloat16),
            pltpu.VMEM((count, length, lanes), jnp.bfloat16),
            pltpu.VMEM((length, lanes), jnp.float32),
            pltpu.SemaphoreType.DMA((3, count)),
        ],
        compiler_params=pltpu.CompilerParams(vmem_limit_bytes=62 << 20),
        name="span_states",
    )(keys, values, rates)


def fold_rows(parts):
    index = lax.broadcasted_iota(jnp.int32, parts[0].shape, 0)
    for bit in (1, 2, 4):
        low = (index & bit) == 0
        parts = [
            jnp.where(low, first, second)
            + pltpu.roll(jnp.where(low, second, first), 8 - bit, axis=0)
            for first, second in zip(parts[0::2], parts[1::2])
        ]
    return parts[0]


def convolve_kernel(
    span, spans, first, count, order_ref, queries_ref, gated_ref, residues_ref, rates_ref, *refs
):
    states, (out_ref, queries_buf, gated_buf, rows_buf, sems) = refs[:count], refs[count:]
    length, width = out_ref.shape
    lanes = queries_buf.shape[2]
    mine = lax.axis_index("ctx")
    copies = []
    for index in range(width // lanes):
        at = (pl.ds(span * length, length), pl.ds(first + index * lanes, lanes))
        pair = [
            pltpu.make_async_copy(gated_ref.at[at], gated_buf.at[index], sems.at[0, index]),
            pltpu.make_async_copy(queries_ref.at[at], queries_buf.at[index], sems.at[1, index]),
        ]
        for copy in pair:
            copy.start()
        copies.append(pair)
    here = order_ref[mine * spans + span]
    for index in range(width // lanes):
        across = pl.ds(first + index * lanes, lanes)
        rates = rates_ref[:, across]
        decay = jnp.exp(-rates)
        scaled = residues_ref[:, across] * jnp.sqrt(2.0 * rates)
        entering = jnp.zeros(rates.shape, jnp.float32)
        for which, states_ref in enumerate(states):

            def carry(source, state, which=which, states_ref=states_ref, rates=rates, across=across):
                block = source
                if count > 1:
                    other = (source // spans) * count + which
                    block = jnp.bitwise_xor(mine, other) * spans + source % spans
                gap = here - 1 - order_ref[block]
                reach = jnp.exp(-rates * (length * jnp.maximum(gap, 0)).astype(jnp.float32))
                return state + jnp.where(gap >= 0, reach, 0.0) * states_ref[source, :, across]

            entering = lax.fori_loop(0, states_ref.shape[0], carry, entering)
        for copy in copies[index]:
            copy.wait()

        def body(step, state, index=index, decay=decay, scaled=scaled):
            base = pl.multiple_of(step * ROWS, ROWS)
            rows = pl.ds(base, ROWS)
            rows_buf[rows, :] = gated_buf[index, rows, :].astype(jnp.float32)
            groups = []
            for group in range(0, ROWS, 8):
                parts = []
                for row in range(group, group + 8):
                    state = decay * state + rows_buf[pl.ds(base + row, 1), :]
                    seen = scaled * state
                    total = seen[0:8]
                    for mode in range(8, seen.shape[0], 8):
                        total = total + seen[mode : mode + 8]
                    parts.append(total)
                groups.append(fold_rows(parts))
            mixed = jnp.concatenate(groups, axis=0).astype(jnp.bfloat16).astype(jnp.float32)
            gate = queries_buf[index, rows, :].astype(jnp.float32)
            out_ref[rows, index * lanes : (index + 1) * lanes] = (gate * mixed).astype(jnp.bfloat16)
            return state

        lax.fori_loop(0, length // ROWS, body, entering)


def convolve(order, queries, gated, residues, rates, states, spans, span, part, parts):
    tokens, channels = queries.shape
    length, width = tokens // spans, channels // parts
    lanes = min(LANES, width)
    inside = pl.BlockSpec(memory_space=pltpu.VMEM)
    return pl.pallas_call(
        functools.partial(convolve_kernel, span, spans, part * width, len(states)),
        out_shape=jax.ShapeDtypeStruct((length, width), jnp.bfloat16),
        in_specs=[
            pl.BlockSpec(memory_space=pltpu.SMEM),
            pl.BlockSpec(memory_space=pltpu.HBM),
            pl.BlockSpec(memory_space=pltpu.HBM),
            inside,
            inside,
            *[inside] * len(states),
        ],
        out_specs=inside,
        scratch_shapes=[
            pltpu.VMEM((width // lanes, length, lanes), jnp.bfloat16),
            pltpu.VMEM((width // lanes, length, lanes), jnp.bfloat16),
            pltpu.VMEM((length, lanes), jnp.float32),
            pltpu.SemaphoreType.DMA((2, width // lanes)),
        ],
        compiler_params=pltpu.CompilerParams(vmem_limit_bytes=6 << 20),
        name="convolve",
    )(order, queries, gated, residues, rates, *states)


def exchange_states(totals):
    ctx = lax.axis_size("ctx")
    near = [totals]
    for other in range(2, ctx, 2):
        near.append(lax.ppermute(totals, "ctx", [(i, i ^ other) for i in range(ctx)]))
    near = jnp.concatenate(near)
    far = lax.ppermute(near, "ctx", [(i, i ^ 1) for i in range(ctx)])
    return [near, far]


def gather_weights(out_weight):
    n, ctx = lax.axis_size("tp"), lax.axis_size("ctx")
    me, mine = lax.axis_index("tp"), lax.axis_index("ctx")
    channels, columns = out_weight.shape[0], out_weight.shape[1] // n
    rows = channels // ctx
    strip = lax.dynamic_slice_in_dim(out_weight, mine * rows, rows, 0)
    pieces = []
    for shift in range(1, n):
        target = lax.rem(me + shift, n)
        piece = lax.dynamic_slice_in_dim(strip, target * columns, columns, 1)
        pieces.append(lax.ppermute(piece, "tp", [(i, (i + shift) % n) for i in range(n)]))
    held = jnp.stack(pieces)
    strips = {0: held}
    for other in range(2, ctx, 2):
        strips[other] = lax.ppermute(held, "ctx", [(i, i ^ other) for i in range(ctx)])
    for other in range(0, ctx, 2):
        strips[other + 1] = lax.ppermute(strips[other], "ctx", [(i, i ^ 1) for i in range(ctx)])
    return [strips[other] for other in range(ctx)]


def upper_kernel(n, ctx, parts, *refs):
    weight_ref, strips, refs = refs[0], refs[1 : 1 + ctx], refs[1 + ctx :]
    sent, refs = refs[:parts], refs[parts:]
    count = (n - 1) * parts
    evens, odds, refs = refs[:count], refs[count : 2 * count], refs[2 * count :]
    out_ref, matrix_ref, whole_ref, total_ref, result_ref, weight_sem, strip_sem, sent_sem, moved_sem, out_sem = refs
    columns = matrix_ref.shape[2]
    height = matrix_ref.shape[1] // ctx
    width = sent[0].shape[1]
    me, mine = lax.axis_index("tp"), lax.axis_index("ctx")

    own = pltpu.make_async_copy(
        weight_ref.at[:, pl.ds(pl.multiple_of(me * columns, 128), columns)], matrix_ref.at[0], weight_sem
    )
    own.start()
    kept = []
    for part in range(parts):
        copy = pltpu.make_async_copy(sent[part], whole_ref.at[0, :, pl.ds(part * width, width)], sent_sem.at[part])
        copy.start()
        kept.append(copy)
    laid = []
    later = lax.rem(me, 2) == 1
    for shift in range(1, n):
        for part in range(parts):
            at = (shift - 1) * parts + part
            target = whole_ref.at[shift, :, pl.ds(part * width, width)]

            passed = me >= shift
            sources = (
                (passed & later, evens[at]),
                (passed & jnp.logical_not(later), odds[at]),
                (jnp.logical_not(passed) & later, odds[(n - shift - 1) * parts + part]),
                (jnp.logical_not(passed) & jnp.logical_not(later), evens[(n - shift - 1) * parts + part]),
            )
            for taken, source in sources:

                @pl.when(taken)
                def _(at=at, source=source, target=target):
                    pltpu.make_async_copy(source, target, moved_sem.at[at]).start()

        for other in range(ctx):
            row = pl.multiple_of(jnp.bitwise_xor(mine, other) * height, 16)
            copy = pltpu.make_async_copy(
                strips[other].at[shift - 1], matrix_ref.at[shift, pl.ds(row, height)], strip_sem.at[shift - 1, other]
            )
            copy.start()
            laid.append(copy)
    for shift in range(n):
        if shift == 0:
            own.wait()
            for copy in kept:
                copy.wait()
        else:
            for part in range(parts):
                at = (shift - 1) * parts + part
                target = whole_ref.at[shift, :, pl.ds(part * width, width)]
                pltpu.make_async_copy(evens[at], target, moved_sem.at[at]).wait()
            for other in range(ctx):
                laid[(shift - 1) * ctx + other].wait()

        @pl.loop(0, columns // 256)
        def _(step, shift=shift):
            at = pl.ds(pl.multiple_of(step * 256, 256), 256)
            piece = jnp.dot(whole_ref[shift], matrix_ref[shift, :, at], preferred_element_type=jnp.float32)
            if shift == 0:
                total_ref[:, at] = piece
            elif shift < n - 1:
                total_ref[:, at] += piece
            else:
                result_ref[:, at] = (total_ref[:, at] + piece).astype(jnp.bfloat16)

    copy = pltpu.make_async_copy(result_ref, out_ref.at[pl.ds(0, sent[0].shape[0])], out_sem)
    copy.start()
    copy.wait()


def upper(out_weight, strips, sent, evens, odds, rows):
    n, ctx, parts = lax.axis_size("tp"), lax.axis_size("ctx"), len(sent)
    channels, columns = out_weight.shape[0], out_weight.shape[1] // n
    tile = sent[0].shape[0]
    anywhere = pl.BlockSpec(memory_space=pl.ANY)
    operands = [out_weight, *strips, *sent, *evens, *odds]
    return pl.pallas_call(
        functools.partial(upper_kernel, n, ctx, parts),
        out_shape=jax.ShapeDtypeStruct((rows, columns), jnp.bfloat16),
        in_specs=[pl.BlockSpec(memory_space=pltpu.HBM)] + [anywhere] * (len(operands) - 1),
        out_specs=anywhere,
        scratch_shapes=[
            pltpu.VMEM((n, channels, columns), jnp.bfloat16),
            pltpu.VMEM((n, tile, channels), jnp.bfloat16),
            pltpu.VMEM((tile, columns), jnp.float32),
            pltpu.VMEM((tile, columns), jnp.bfloat16),
            pltpu.SemaphoreType.DMA(()),
            pltpu.SemaphoreType.DMA((n - 1, ctx)),
            pltpu.SemaphoreType.DMA((parts,)),
            pltpu.SemaphoreType.DMA(((n - 1) * parts,)),
            pltpu.SemaphoreType.DMA(()),
        ],
        compiler_params=pltpu.CompilerParams(vmem_limit_bytes=24 << 20),
        name="upper",
    )(*operands)


def finish_kernel(part, unused_ref, product_ref, left_ref, right_ref, out_ref, result_ref, sem):
    height, width = left_ref.shape
    at = pl.ds(pl.multiple_of(lax.axis_index("tp") * width, 128), width)

    @pl.loop(0, height // 64)
    def _(block):
        rows = pl.ds(pl.multiple_of(block * 64, 64), 64)
        result_ref[rows, :] = (
            product_ref[rows, at].astype(jnp.float32)
            + left_ref[rows, :].astype(jnp.float32)
            + right_ref[rows, :].astype(jnp.float32)
        ).astype(jnp.bfloat16)

    copy = pltpu.make_async_copy(
        result_ref, out_ref.at[pl.ds(out_ref.shape[0] - height, height), pl.ds(part * width, width)], sem
    )
    copy.start()
    copy.wait()


def finish(result, product, left, right, part):
    inside = pl.BlockSpec(memory_space=pltpu.VMEM)
    anywhere = pl.BlockSpec(memory_space=pl.ANY)
    return pl.pallas_call(
        functools.partial(finish_kernel, part),
        out_shape=jax.ShapeDtypeStruct(result.shape, result.dtype),
        in_specs=[anywhere, inside, inside, inside],
        out_specs=anywhere,
        scratch_shapes=[pltpu.VMEM(left.shape, jnp.bfloat16), pltpu.SemaphoreType.DMA(())],
        input_output_aliases={0: 0},
        compiler_params=pltpu.CompilerParams(vmem_limit_bytes=2 << 20),
        name="finish",
    )(result, product, left, right)


def payload_kernel(n, step, product_ref, even_ref, odd_ref, to_even_ref, to_odd_ref):
    me, width = lax.axis_index("tp"), even_ref.shape[1]
    rightward = (lax.rem(me + n - step, n), (me < step).astype(jnp.int32))
    leftward = (lax.rem(me + step, n), (me >= n - step).astype(jnp.int32))
    first = lax.rem(me, 2) == 0
    for flag, source_ref, target_ref in ((first, odd_ref, to_even_ref), (jnp.logical_not(first), even_ref, to_odd_ref)):
        column = jnp.where(flag, rightward[0], leftward[0])
        adds = jnp.where(flag, rightward[1], leftward[1]) > 0
        at = pl.ds(pl.multiple_of(column * width, 128), width)

        @pl.when(adds)
        def _(at=at, source_ref=source_ref, target_ref=target_ref):
            @pl.loop(0, source_ref.shape[0] // 64)
            def _(block):
                rows = pl.ds(pl.multiple_of(block * 64, 64), 64)
                target_ref[rows, :] = source_ref[rows, :] + product_ref[rows, at]

        @pl.when(jnp.logical_not(adds))
        def _(source_ref=source_ref, target_ref=target_ref):
            @pl.loop(0, source_ref.shape[0] // 64)
            def _(block):
                rows = pl.ds(pl.multiple_of(block * 64, 64), 64)
                target_ref[rows, :] = source_ref[rows, :]


def payload(step, product, even, odd):
    inside = pl.BlockSpec(memory_space=pltpu.VMEM)
    return pl.pallas_call(
        functools.partial(payload_kernel, lax.axis_size("tp"), step),
        out_shape=[jax.ShapeDtypeStruct(even.shape, even.dtype)] * 2,
        in_specs=[inside, inside, inside],
        out_specs=[inside, inside],
        compiler_params=pltpu.CompilerParams(vmem_limit_bytes=1 << 20),
        name="payload",
    )(product, even, odd)


def product_kernel(part, parts, rows_ref, weight_ref, out_ref, weight_buf, sems):
    count, _, width = weight_buf.shape
    copies = []
    for group in range(count):
        copy = pltpu.make_async_copy(
            weight_ref.at[:, pl.ds((group * parts + part) * width, width)], weight_buf.at[group], sems.at[group]
        )
        copy.start()
        copies.append(copy)
    for group in range(count):
        copies[group].wait()
        step = min(width, 256)
        for first in range(0, width, step):
            piece = jnp.dot(
                rows_ref[...], weight_buf[group, :, first : first + step], preferred_element_type=jnp.float32
            )
            out_ref[:, group * width + first : group * width + first + step] = piece.astype(jnp.bfloat16)


def local_product(rows, out_weight, part, parts):
    n = lax.axis_size("tp")
    height, channels = rows.shape
    width = out_weight.shape[1] // n // parts
    inside = pl.BlockSpec(memory_space=pltpu.VMEM)
    return pl.pallas_call(
        functools.partial(product_kernel, part, parts),
        out_shape=jax.ShapeDtypeStruct((height, n * width), jnp.bfloat16),
        in_specs=[inside, pl.BlockSpec(memory_space=pltpu.HBM)],
        out_specs=inside,
        scratch_shapes=[pltpu.VMEM((n, channels, width), jnp.bfloat16), pltpu.SemaphoreType.DMA((n,))],
        compiler_params=pltpu.CompilerParams(vmem_limit_bytes=8 << 20),
        name="local_product",
    )(rows, out_weight)


def exchange(sent, products):
    n, parts = lax.axis_size("tp"), len(sent)
    pairs = [
        [pair for i in range(start, n - 1, 2) for pair in ((i, i + 1), (i + 1, i))] for start in range(2)
    ]
    evens, odds = {}, {}
    for slot in range(1, n + 1):
        for part in range(parts):
            if slot == 1:
                even = odd = sent[part]
            else:
                even, odd = payload(slot - 1, products[part], evens[slot - 1, part], odds[slot - 1, part])
            evens[slot, part] = lax.ppermute(even, "tp", pairs[0])
            odds[slot, part] = lax.ppermute(odd, "tp", pairs[1])
    return evens, odds


def local(queries, keys, values, residues, rates, out_weight, span_order):
    n, ctx = lax.axis_size("tp"), lax.axis_size("ctx")
    tokens, channels = queries.shape
    spans = span_order.shape[0] // ctx
    lined = channels // ctx >= 128 and spans == 2 and ctx & (ctx - 1) == 0
    totals, gated = span_states(keys, values, rates, spans)
    strips = gather_weights(out_weight) if lined else None
    states = exchange_states(totals) if lined else [lax.all_gather(totals, "ctx", axis=0, tiled=True)]
    conv = functools.partial(convolve, span_order, queries, gated, residues, rates, states, spans)
    if not lined:
        outputs = [conv(span, 0, 1) for span in range(spans)]
        part = jnp.dot(jnp.concatenate(outputs), out_weight, preferred_element_type=jnp.float32)
        return lax.psum_scatter(part.astype(jnp.bfloat16), "tp", scatter_dimension=1, tiled=True)
    sent, products = [], []
    for part in range(PARTS):
        sent.append(conv(0, part, PARTS))
    rest = conv(1, 0, 1)
    for part in range(PARTS):
        products.append(local_product(rest, out_weight, part, PARTS))
    evens, odds = exchange(sent, products)
    arrived = [[side[slot, part] for slot in range(1, n) for part in range(PARTS)] for side in (evens, odds)]
    result = upper(out_weight, strips, sent, *arrived, tokens)
    for part in range(PARTS):
        result = finish(result, products[part], evens[n, part], odds[n, part], part)
    return result


def solution(mesh):
    placed = (
        P("ctx", "tp"),
        P("ctx", "tp"),
        P("ctx", "tp"),
        P(None, "tp"),
        P(None, "tp"),
        P("tp", None),
        P(),
    )

    return jax.shard_map(local, mesh=mesh, in_specs=placed, out_specs=P("ctx", "tp"), check_vma=False)
```

time: 209 us -> 185 us (0.89)
  the two profiles are of different devices: /device:TPU:0 before, /device:TPU:10 now
where the time goes in v3:
time: 185 us; the launch traced here: 184 us
  waiting for transfers between devices  80.2 us (43%)
  Pallas kernels  51.7 us (28%)
  starting transfers between devices  41 us (22%)
  local copies, waits for them, and re-layouts  10.8 us (6%)
    ppermute x8, starting transfers between devices, exchange(): odds[slot, part] = lax.ppermute(odd, 'tp', pairs[1])  26.2 us
    ppermute x3, waiting for transfers between devices, gather_weights(): lax.ppermute(held, 'ctx', [(i, i ^ other) for i in range(ctx)])  23.7 us
    ppermute x8, waiting for transfers between devices, exchange(): odds[slot, part] = lax.ppermute(odd, 'tp', pairs[1])  23.7 us
    ppermute x3, waiting for transfers between devices, gather_weights(): lax.ppermute(piece, 'tp', [(i, (i + shift) % n) for i in range(n)])  21.1 us
    pallas_call x3, Pallas kernels, convolve(): pl.pallas_call(functools.partial(convolve_kernel, span, spans, part * wid...  19.4 us
    pallas_call x1, Pallas kernels, upper(): pl.pallas_call(functools.partial(upper_kernel, n, ctx, parts), out_shape=...  10.2 us
    pallas_call x1, Pallas kernels, span_states(): pl.pallas_call(functools.partial(states_kernel, spans), out_shape=[jax.Sh...  9.61 us
    unnamed x23, local copies, waits for them, and re-layouts  9.14 us
  transfers between devices with their start and end apart: 30, of which 14 were waited for; matrix products, arithmetic and copies ran while one was open for 1% of the time, Pallas kernels for 19%

profile of v3, /device:TPU:10, one launch (start us, length us, event | category | flops | bytes accessed | tf_op | source)
XLA Modules:
  0.0 184.2 jit_solution(8942367817577418041)
XLA Ops:
  0.0 9.6 %span_states.1 = (f32[2,16,1024]{2,1,0:T(8,128)}, bf16[1024,1024]{1,0:T(8,128)(2,1)}) custom-call(bf16[1024,1024]{1,0:T(8,128)(2,1)} %keys_ref.1, bf16[1024,1024]{1,0:T(8,128)(2,1)} %values_ref.1, f32[16,1024]{1,0:T(8,128)} %rates_ref.7), custom_call_target="tpu_custom_call" | custom-call | tf_op jit(solution)/shard_map/span_states/pallas_call | solution.py:67
  14.1 2.1 %collective-permute-done.10 = f32[2,16,1024]{2,1,0:T(8,128)S(1)} collective-permute-done((f32[2,16,1024]{2,1,0:T(8,128)}, f32[2,16,1024]{2,1,0:T(8,128)S(1)}, u32[]{:S(2)}, u32[]{:S(2)}) %collective-permute-start.10) | collective-permute-done | bytes 131104 | tf_op jit(solution)/shard_map/ppermute | solution.py:193
  24.1 5.4 %convolve.3.refs_9_ = bf16[512,512]{1,0:T(8,128)(2,1)} custom-call(s32[16]{0:T(128)S(1)} %copy-done.7, bf16[1024,1024]{1,0:T(8,128)(2,1)S(1)} %copy-done.1, bf16[1024,1024]{1,0:T(8,128)(2,1)S(1)} %copy-done.3, f32[16,1024]{1,0:T(8,128)S(1)} %copy-done.6, f32[16,1024]{1,0:T(8,128)S(1)} %copy-done.5, ...), custom_call_target="tpu_custom_call" | custom-call | tf_op jit(solution)/shard_map/convolve/pallas_call | solution.py:166
  30.0 4.6 %collective-permute-start.16 = (bf16[512,512]{1,0:T(8,128)(2,1)}, bf16[512,512]{1,0:T(8,128)(2,1)}, u32[]{:S(2)}, u32[]{:S(2)}) collective-permute-start(bf16[512,512]{1,0:T(8,128)(2,1)} %convolve.3.refs_9_), channel_id=1, source_target_pairs={{1,2},{2,1},{5,6},{6,5},{9,10},{10,9},{13,14},{14,13},{17,18},{18,... | collective-permute-start | bytes 1572872 | tf_op jit(solution)/shard_map/ppermute | solution.py:442
  34.6 5.4 %convolve.4.refs_10_ = bf16[512,512]{1,0:T(8,128)(2,1)} custom-call(s32[16]{0:T(128)S(1)} %copy-done.7, bf16[1024,1024]{1,0:T(8,128)(2,1)S(1)} %copy-done.1, bf16[1024,1024]{1,0:T(8,128)(2,1)S(1)} %copy-done.3, f32[16,1024]{1,0:T(8,128)S(1)} %copy-done.6, f32[16,1024]{1,0:T(8,128)S(1)} %copy-done.5, ...), custom_call_target="tpu_custom_call" | custom-call | tf_op jit(solution)/shard_map/convolve/pallas_call | solution.py:166
  45.3 8.6 %convolve.5.rows_ref = bf16[512,1024]{1,0:T(8,128)(2,1)S(1)} custom-call(s32[16]{0:T(128)S(1)} %copy-done.7, bf16[1024,1024]{1,0:T(8,128)(2,1)S(1)} %copy-done.2, bf16[1024,1024]{1,0:T(8,128)(2,1)S(1)} %copy-done.4, f32[16,1024]{1,0:T(8,128)S(1)} %copy-done.6, f32[16,1024]{1,0:T(8,128)S(1)} %copy-done.5, ...), custom_call_target="tpu_custom_call" | custom-call | tf_op jit(solution)/shard_map/convolve/pallas_call | solution.py:166
  53.9 3.4 %copy-done = bf16[1024,4096]{1,0:T(8,128)(2,1)S(1)} copy-done((bf16[1024,4096]{1,0:T(8,128)(2,1)S(1)}, bf16[1024,4096]{1,0:T(8,128)(2,1)}, u32[]{:S(2)}) %copy-start) | copy-done | bytes 8388632
  57.3 3.5 %local_product.2.product_ref = bf16[512,2048]{1,0:T(8,128)(2,1)S(1)} custom-call(bf16[512,1024]{1,0:T(8,128)(2,1)S(1)} %convolve.5.rows_ref, bf16[1024,4096]{1,0:T(8,128)(2,1)S(1)} %copy-done), custom_call_target="tpu_custom_call" | custom-call | tf_op jit(solution)/shard_map/local_product/pallas_call | solution.py:418
  64.3 3.4 %collective-permute-start.20 = (bf16[512,512]{1,0:T(8,128)(2,1)S(1)}, bf16[512,512]{1,0:T(8,128)(2,1)S(1)}, u32[]{:S(2)}, u32[]{:S(2)}) collective-permute-start(bf16[512,512]{1,0:T(8,128)(2,1)S(1)} %get-tuple-element.23), channel_id=1, source_target_pairs={{1,2},{2,1},{5,6},{6,5},{9,10},{10,9},{13,14},{14,13},{17,18},{18,... | collective-permute-start | bytes 1572872 | tf_op jit(solution)/shard_map/ppermute | solution.py:442
  69.4 3.5 %local_product.3.product_ref = bf16[512,2048]{1,0:T(8,128)(2,1)S(1)} custom-call(bf16[512,1024]{1,0:T(8,128)(2,1)S(1)} %convolve.5.rows_ref, bf16[1024,4096]{1,0:T(8,128)(2,1)S(1)} %copy-done), custom_call_target="tpu_custom_call" | custom-call | tf_op jit(solution)/shard_map/local_product/pallas_call | solution.py:418
  74.4 6.0 %collective-permute-done.2 = bf16[128,1024]{1,0:T(8,128)(2,1)S(1)} collective-permute-done((bf16[128,1024]{1,0:T(8,128)(2,1)S(1)}, bf16[128,1024]{1,0:T(8,128)(2,1)S(1)}, u32[]{:S(2)}, u32[]{:S(2)}) %collective-permute-start.2) | collective-permute-done | bytes 262176 | tf_op jit(solution)/shard_map/ppermute | solution.py:209
  80.4 2.5 %collective-permute-start.19 = (bf16[512,512]{1,0:T(8,128)(2,1)S(1)}, bf16[512,512]{1,0:T(8,128)(2,1)S(1)}, u32[]{:S(2)}, u32[]{:S(2)}) collective-permute-start(bf16[512,512]{1,0:T(8,128)(2,1)S(1)} %get-tuple-element.22), channel_id=1, source_target_pairs={{0,1},{1,0},{2,3},{3,2},{4,5},{5,4},{6,7},{7,6},{8,9},{9,8},{10,11... | collective-permute-start | bytes 1572872 | tf_op jit(solution)/shard_map/ppermute | solution.py:441
  82.9 14.0 %collective-permute-done.1 = bf16[128,1024]{1,0:T(8,128)(2,1)S(1)} collective-permute-done((bf16[128,1024]{1,0:T(8,128)(2,1)S(1)}, bf16[128,1024]{1,0:T(8,128)(2,1)S(1)}, u32[]{:S(2)}, u32[]{:S(2)}) %collective-permute-start.1) | collective-permute-done | bytes 262176 | tf_op jit(solution)/shard_map/ppermute | solution.py:209
  96.9 3.7 %collective-permute-start.22 = (bf16[512,512]{1,0:T(8,128)(2,1)S(1)}, bf16[512,512]{1,0:T(8,128)(2,1)S(1)}, u32[]{:S(2)}, u32[]{:S(2)}) collective-permute-start(bf16[512,512]{1,0:T(8,128)(2,1)S(1)} %get-tuple-element.25), channel_id=1, source_target_pairs={{1,2},{2,1},{5,6},{6,5},{9,10},{10,9},{13,14},{14,13},{17,18},{18,... | collective-permute-start | bytes 1572872 | tf_op jit(solution)/shard_map/ppermute | solution.py:442
  105.6 5.9 %collective-permute-done.22.odd_ref.refs_20_ = bf16[512,512]{1,0:T(8,128)(2,1)S(1)} collective-permute-done((bf16[512,512]{1,0:T(8,128)(2,1)S(1)}, bf16[512,512]{1,0:T(8,128)(2,1)S(1)}, u32[]{:S(2)}, u32[]{:S(2)}) %collective-permute-start.22) | collective-permute-done | bytes 524320 | tf_op jit(solution)/shard_map/ppermute | solution.py:442
  111.7 10.6 %collective-permute-done.4.refs_3_ = bf16[3,128,1024]{2,1,0:T(8,128)(2,1)S(1)} collective-permute-done((bf16[3,128,1024]{2,1,0:T(8,128)(2,1)S(1)}, bf16[3,128,1024]{2,1,0:T(8,128)(2,1)S(1)}, u32[]{:S(2)}, u32[]{:S(2)}) %collective-permute-start.4) | collective-permute-done | bytes 786464 | tf_op jit(solution)/shard_map/ppermute | solution.py:213
  122.3 13.2 %collective-permute-done.6.refs_5_ = bf16[3,128,1024]{2,1,0:T(8,128)(2,1)S(1)} collective-permute-done((bf16[3,128,1024]{2,1,0:T(8,128)(2,1)S(1)}, bf16[3,128,1024]{2,1,0:T(8,128)(2,1)S(1)}, u32[]{:S(2)}, u32[]{:S(2)}) %collective-permute-start.6) | collective-permute-done | bytes 786464 | tf_op jit(solution)/shard_map/ppermute | solution.py:213
  135.5 4.1 %collective-permute-start.24 = (bf16[512,512]{1,0:T(8,128)(2,1)S(1)}, bf16[512,512]{1,0:T(8,128)(2,1)S(1)}, u32[]{:S(2)}, u32[]{:S(2)}) collective-permute-start(bf16[512,512]{1,0:T(8,128)(2,1)S(1)} %get-tuple-element.27), channel_id=1, source_target_pairs={{1,2},{2,1},{5,6},{6,5},{9,10},{10,9},{13,14},{14,13},{17,18},{18,... | collective-permute-start | bytes 1572872 | tf_op jit(solution)/shard_map/ppermute | solution.py:442
  142.1 7.9 %collective-permute-done.24.refs_21_.odd_ref = bf16[512,512]{1,0:T(8,128)(2,1)S(1)} collective-permute-done((bf16[512,512]{1,0:T(8,128)(2,1)S(1)}, bf16[512,512]{1,0:T(8,128)(2,1)S(1)}, u32[]{:S(2)}, u32[]{:S(2)}) %collective-permute-start.24) | collective-permute-done | bytes 524320 | tf_op jit(solution)/shard_map/ppermute | solution.py:442
  150.1 7.8 %collective-permute-done.25.refs_22_.odd_ref = bf16[512,512]{1,0:T(8,128)(2,1)S(1)} collective-permute-done((bf16[512,512]{1,0:T(8,128)(2,1)S(1)}, bf16[512,512]{1,0:T(8,128)(2,1)S(1)}, u32[]{:S(2)}, u32[]{:S(2)}) %collective-permute-start.25) | collective-permute-done | bytes 524320 | tf_op jit(solution)/shard_map/ppermute | solution.py:442
  158.1 3.9 %collective-permute-start.27 = (bf16[512,512]{1,0:T(8,128)(2,1)S(1)}, bf16[512,512]{1,0:T(8,128)(2,1)S(1)}, u32[]{:S(2)}, u32[]{:S(2)}) collective-permute-start(bf16[512,512]{1,0:T(8,128)(2,1)S(1)} %get-tuple-element.30), channel_id=1, source_target_pairs={{1,2},{2,1},{5,6},{6,5},{9,10},{10,9},{13,14},{14,13},{17,18},{18,... | collective-permute-start | bytes 1572872 | tf_op jit(solution)/shard_map/ppermute | solution.py:442
  162.2 2.7 %collective-permute-start.29 = (bf16[512,512]{1,0:T(8,128)(2,1)S(1)}, bf16[512,512]{1,0:T(8,128)(2,1)S(1)}, u32[]{:S(2)}, u32[]{:S(2)}) collective-permute-start(bf16[512,512]{1,0:T(8,128)(2,1)S(1)} %get-tuple-element.32), channel_id=1, source_target_pairs={{1,2},{2,1},{5,6},{6,5},{9,10},{10,9},{13,14},{14,13},{17,18},{18,... | collective-permute-start | bytes 1572872 | tf_op jit(solution)/shard_map/ppermute | solution.py:442
  164.9 10.2 %upper.1.unused_ref = bf16[1024,1024]{1,0:T(8,128)(2,1)} custom-call(bf16[1024,4096]{1,0:T(8,128)(2,1)S(1)} %bitcast.4, bf16[3,128,1024]{2,1,0:T(8,128)(2,1)S(1)} %pad_maximum_fusion.refs_1_, bf16[3,128,1024]{2,1,0:T(8,128)(2,1)S(1)} %collective-permute-done.3.refs_2_, bf16[3,128,1024]{2,1,0:T(8,128)(2,1)S(1)} %collective-permute-done.4.refs_3_, ...), custom_call_target="tpu_custom_call" | custom-call | tf_op jit(solution)/shard_map/upper/pallas_call | solution.py:301
  176.1 5.0 %collective-permute-done.28.left_ref = bf16[512,512]{1,0:T(8,128)(2,1)S(1)} collective-permute-done((bf16[512,512]{1,0:T(8,128)(2,1)S(1)}, bf16[512,512]{1,0:T(8,128)(2,1)S(1)}, u32[]{:S(2)}, u32[]{:S(2)}) %collective-permute-start.28) | collective-permute-done | bytes 524320 | tf_op jit(solution)/shard_map/ppermute | solution.py:441
  (78 shorter events, 36.9 us)
Async XLA Ops:
  29.5 31.4 %collective-permute-start.14 = (bf16[512,512]{1,0:T(8,128)(2,1)}, bf16[512,512]{1,0:T(8,128)(2,1)}, u32[]{:S(2)}, u32[]{:S(2)}) collective-permute-start(bf16[512,512]{1,0:T(8,128)(2,1)} %convolve.3.refs_9_), channel_id=1, source_target_pairs={{0,1},{1,0},{2,3},{3,2},{4,5},{5,4},{6,7},{7,6},{8,9},{9,8},{10,11... | collective-permute-start | bytes 1572872 | tf_op jit(solution)/shard_map/ppermute | solution.py:441
  30.0 30.9 %collective-permute-start.16 = (bf16[512,512]{1,0:T(8,128)(2,1)}, bf16[512,512]{1,0:T(8,128)(2,1)}, u32[]{:S(2)}, u32[]{:S(2)}) collective-permute-start(bf16[512,512]{1,0:T(8,128)(2,1)} %convolve.3.refs_9_), channel_id=1, source_target_pairs={{1,2},{2,1},{5,6},{6,5},{9,10},{10,9},{13,14},{14,13},{17,18},{18,... | collective-permute-start | bytes 1572872 | tf_op jit(solution)/shard_map/ppermute | solution.py:442
  40.0 27.7 %collective-permute-start.15 = (bf16[512,512]{1,0:T(8,128)(2,1)}, bf16[512,512]{1,0:T(8,128)(2,1)}, u32[]{:S(2)}, u32[]{:S(2)}) collective-permute-start(bf16[512,512]{1,0:T(8,128)(2,1)} %convolve.4.refs_10_), channel_id=1, source_target_pairs={{0,1},{1,0},{2,3},{3,2},{4,5},{5,4},{6,7},{7,6},{8,9},{9,8},{10,11... | collective-permute-start | bytes 1572872 | tf_op jit(solution)/shard_map/ppermute | solution.py:441
  40.1 27.7 %collective-permute-start.18 = (bf16[512,512]{1,0:T(8,128)(2,1)}, bf16[512,512]{1,0:T(8,128)(2,1)}, u32[]{:S(2)}, u32[]{:S(2)}) collective-permute-start(bf16[512,512]{1,0:T(8,128)(2,1)} %convolve.4.refs_10_), channel_id=1, source_target_pairs={{1,2},{2,1},{5,6},{6,5},{9,10},{10,9},{13,14},{14,13},{17,18},{18,... | collective-permute-start | bytes 1572872 | tf_op jit(solution)/shard_map/ppermute | solution.py:442
  62.2 40.5 %collective-permute-start.17 = (bf16[512,512]{1,0:T(8,128)(2,1)S(1)}, bf16[512,512]{1,0:T(8,128)(2,1)S(1)}, u32[]{:S(2)}, u32[]{:S(2)}) collective-permute-start(bf16[512,512]{1,0:T(8,128)(2,1)S(1)} %get-tuple-element.21), channel_id=1, source_target_pairs={{0,1},{1,0},{2,3},{3,2},{4,5},{5,4},{6,7},{7,6},{8,9},{9,8},{10,11... | collective-permute-start | bytes 1572872 | tf_op jit(solution)/shard_map/ppermute | solution.py:441
  63.8 16.7 %collective-permute-start.2 = (bf16[128,1024]{1,0:T(8,128)(2,1)S(1)}, bf16[128,1024]{1,0:T(8,128)(2,1)S(1)}, u32[]{:S(2)}, u32[]{:S(2)}) collective-permute-start(bf16[128,1024]{1,0:T(8,128)(2,1)S(1)} %get-tuple-element.34), channel_id=1, source_target_pairs={{0,3},{1,0},{2,1},{3,2},{4,7},{5,4},{6,5},{7,6},{8,11},{9,8},{10,9... | collective-permute-start | bytes 786440 | tf_op jit(solution)/shard_map/ppermute | solution.py:209
  64.3 40.0 %collective-permute-start.20 = (bf16[512,512]{1,0:T(8,128)(2,1)S(1)}, bf16[512,512]{1,0:T(8,128)(2,1)S(1)}, u32[]{:S(2)}, u32[]{:S(2)}) collective-permute-start(bf16[512,512]{1,0:T(8,128)(2,1)S(1)} %get-tuple-element.23), channel_id=1, source_target_pairs={{1,2},{2,1},{5,6},{6,5},{9,10},{10,9},{13,14},{14,13},{17,18},{18,... | collective-permute-start | bytes 1572872 | tf_op jit(solution)/shard_map/ppermute | solution.py:442
  67.7 29.2 %collective-permute-start.1 = (bf16[128,1024]{1,0:T(8,128)(2,1)S(1)}, bf16[128,1024]{1,0:T(8,128)(2,1)S(1)}, u32[]{:S(2)}, u32[]{:S(2)}) collective-permute-start(bf16[128,1024]{1,0:T(8,128)(2,1)S(1)} %get-tuple-element.35), channel_id=1, source_target_pairs={{0,2},{1,3},{2,0},{3,1},{4,6},{5,7},{6,4},{7,5},{8,10},{9,11},{10,... | collective-permute-start | bytes 786440 | tf_op jit(solution)/shard_map/ppermute | solution.py:209
  67.8 33.9 %collective-permute-start = (bf16[128,1024]{1,0:T(8,128)(2,1)S(1)}, bf16[128,1024]{1,0:T(8,128)(2,1)S(1)}, u32[]{:S(2)}, u32[]{:S(2)}) collective-permute-start(bf16[128,1024]{1,0:T(8,128)(2,1)S(1)} %get-tuple-element.33), channel_id=1, source_target_pairs={{0,1},{1,2},{2,3},{3,0},{4,5},{5,6},{6,7},{7,4},{8,9},{9,10},{10,1... | collective-permute-start | bytes 786440 | tf_op jit(solution)/shard_map/ppermute | solution.py:209
  80.4 25.1 %collective-permute-start.19 = (bf16[512,512]{1,0:T(8,128)(2,1)S(1)}, bf16[512,512]{1,0:T(8,128)(2,1)S(1)}, u32[]{:S(2)}, u32[]{:S(2)}) collective-permute-start(bf16[512,512]{1,0:T(8,128)(2,1)S(1)} %get-tuple-element.22), channel_id=1, source_target_pairs={{0,1},{1,0},{2,3},{3,2},{4,5},{5,4},{6,7},{7,6},{8,9},{9,8},{10,11... | collective-permute-start | bytes 1572872 | tf_op jit(solution)/shard_map/ppermute | solution.py:441
  101.8 20.5 %collective-permute-start.4 = (bf16[3,128,1024]{2,1,0:T(8,128)(2,1)S(1)}, bf16[3,128,1024]{2,1,0:T(8,128)(2,1)S(1)}, u32[]{:S(2)}, u32[]{:S(2)}) collective-permute-start(bf16[3,128,1024]{2,1,0:T(8,128)(2,1)S(1)} %pad_maximum_fusion.refs_1_), channel_id=1, source_target_pairs={{0,8},{4,12},{8,0},{12,4},{16,24},{20,28},{24,16},{28,20},{1,9},{5... | collective-permute-start | bytes 2359304 | tf_op jit(solution)/shard_map/ppermute | solution.py:213
  102.7 32.8 %collective-permute-start.6 = (bf16[3,128,1024]{2,1,0:T(8,128)(2,1)S(1)}, bf16[3,128,1024]{2,1,0:T(8,128)(2,1)S(1)}, u32[]{:S(2)}, u32[]{:S(2)}) collective-permute-start(bf16[3,128,1024]{2,1,0:T(8,128)(2,1)S(1)} %pad_maximum_fusion.refs_1_), channel_id=1, source_target_pairs={{0,16},{4,20},{8,24},{12,28},{16,0},{20,4},{24,8},{28,12},{1,17},{... | collective-permute-start | bytes 2359304 | tf_op jit(solution)/shard_map/ppermute | solution.py:213
  104.2 35.3 %collective-permute-start.8 = (bf16[3,128,1024]{2,1,0:T(8,128)(2,1)S(1)}, bf16[3,128,1024]{2,1,0:T(8,128)(2,1)S(1)}, u32[]{:S(2)}, u32[]{:S(2)}) collective-permute-start(bf16[3,128,1024]{2,1,0:T(8,128)(2,1)S(1)} %pad_maximum_fusion.refs_1_), channel_id=1, source_target_pairs={{0,24},{4,28},{8,16},{12,20},{16,8},{20,12},{24,0},{28,4},{1,25},{... | collective-permute-start | bytes 2359304 | tf_op jit(solution)/shard_map/ppermute | solution.py:213
  105.5 34.1 %collective-permute-start.21 = (bf16[512,512]{1,0:T(8,128)(2,1)S(1)}, bf16[512,512]{1,0:T(8,128)(2,1)S(1)}, u32[]{:S(2)}, u32[]{:S(2)}) collective-permute-start(bf16[512,512]{1,0:T(8,128)(2,1)S(1)} %get-tuple-element.24), channel_id=1, source_target_pairs={{0,1},{1,0},{2,3},{3,2},{4,5},{5,4},{6,7},{7,6},{8,9},{9,8},{10,11... | collective-permute-start | bytes 1572872 | tf_op jit(solution)/shard_map/ppermute | solution.py:441
  111.7 28.5 %collective-permute-start.23 = (bf16[512,512]{1,0:T(8,128)(2,1)S(1)}, bf16[512,512]{1,0:T(8,128)(2,1)S(1)}, u32[]{:S(2)}, u32[]{:S(2)}) collective-permute-start(bf16[512,512]{1,0:T(8,128)(2,1)S(1)} %get-tuple-element.26), channel_id=1, source_target_pairs={{0,1},{1,0},{2,3},{3,2},{4,5},{5,4},{6,7},{7,6},{8,9},{9,8},{10,11... | collective-permute-start | bytes 1572872 | tf_op jit(solution)/shard_map/ppermute | solution.py:441
  122.3 35.8 %collective-permute-start.3 = (bf16[3,128,1024]{2,1,0:T(8,128)(2,1)S(1)}, bf16[3,128,1024]{2,1,0:T(8,128)(2,1)S(1)}, u32[]{:S(2)}, u32[]{:S(2)}) collective-permute-start(bf16[3,128,1024]{2,1,0:T(8,128)(2,1)S(1)} %pad_maximum_fusion.refs_1_), channel_id=1, source_target_pairs={{0,4},{4,0},{8,12},{12,8},{16,20},{20,16},{24,28},{28,24},{1,5},{5... | collective-permute-start | bytes 2359304 | tf_op jit(solution)/shard_map/ppermute | solution.py:215
  139.6 22.5 %collective-permute-start.5 = (bf16[3,128,1024]{2,1,0:T(8,128)(2,1)S(1)}, bf16[3,128,1024]{2,1,0:T(8,128)(2,1)S(1)}, u32[]{:S(2)}, u32[]{:S(2)}) collective-permute-start(bf16[3,128,1024]{2,1,0:T(8,128)(2,1)S(1)} %collective-permute-done.4.refs_3_), channel_id=1, source_target_pairs={{0,4},{4,0},{8,12},{12,8},{16,20},{20,16},{24,28},{28,24},{1,5},{5... | collective-permute-start | bytes 2359304 | tf_op jit(solution)/shard_map/ppermute | solution.py:215
  139.6 22.5 %collective-permute-start.7 = (bf16[3,128,1024]{2,1,0:T(8,128)(2,1)S(1)}, bf16[3,128,1024]{2,1,0:T(8,128)(2,1)S(1)}, u32[]{:S(2)}, u32[]{:S(2)}) collective-permute-start(bf16[3,128,1024]{2,1,0:T(8,128)(2,1)S(1)} %collective-permute-done.6.refs_5_), channel_id=1, source_target_pairs={{0,4},{4,0},{8,12},{12,8},{16,20},{20,16},{24,28},{28,24},{1,5},{5... | collective-permute-start | bytes 2359304 | tf_op jit(solution)/shard_map/ppermute | solution.py:215
  140.1 17.8 %collective-permute-start.25 = (bf16[512,512]{1,0:T(8,128)(2,1)S(1)}, bf16[512,512]{1,0:T(8,128)(2,1)S(1)}, u32[]{:S(2)}, u32[]{:S(2)}) collective-permute-start(bf16[512,512]{1,0:T(8,128)(2,1)S(1)} %get-tuple-element.28), channel_id=1, source_target_pairs={{1,2},{2,1},{5,6},{6,5},{9,10},{10,9},{13,14},{14,13},{17,18},{18,... | collective-permute-start | bytes 1572872 | tf_op jit(solution)/shard_map/ppermute | solution.py:442
  149.9 14.9 %collective-permute-start.9 = (bf16[3,128,1024]{2,1,0:T(8,128)(2,1)S(1)}, bf16[3,128,1024]{2,1,0:T(8,128)(2,1)S(1)}, u32[]{:S(2)}, u32[]{:S(2)}) collective-permute-start(bf16[3,128,1024]{2,1,0:T(8,128)(2,1)S(1)} %collective-permute-done.8.refs_7_), channel_id=1, source_target_pairs={{0,4},{4,0},{8,12},{12,8},{16,20},{20,16},{24,28},{28,24},{1,5},{5... | collective-permute-start | bytes 2359304 | tf_op jit(solution)/shard_map/ppermute | solution.py:215
  157.9 17.1 %collective-permute-start.26 = (bf16[512,512]{1,0:T(8,128)(2,1)S(1)}, bf16[512,512]{1,0:T(8,128)(2,1)S(1)}, u32[]{:S(2)}, u32[]{:S(2)}) collective-permute-start(bf16[512,512]{1,0:T(8,128)(2,1)S(1)} %get-tuple-element.29), channel_id=1, source_target_pairs={{0,1},{1,0},{2,3},{3,2},{4,5},{5,4},{6,7},{7,6},{8,9},{9,8},{10,11... | collective-permute-start | bytes 1572872 | tf_op jit(solution)/shard_map/ppermute | solution.py:441
  158.1 16.9 %collective-permute-start.27 = (bf16[512,512]{1,0:T(8,128)(2,1)S(1)}, bf16[512,512]{1,0:T(8,128)(2,1)S(1)}, u32[]{:S(2)}, u32[]{:S(2)}) collective-permute-start(bf16[512,512]{1,0:T(8,128)(2,1)S(1)} %get-tuple-element.30), channel_id=1, source_target_pairs={{1,2},{2,1},{5,6},{6,5},{9,10},{10,9},{13,14},{14,13},{17,18},{18,... | collective-permute-start | bytes 1572872 | tf_op jit(solution)/shard_map/ppermute | solution.py:442
  162.1 19.0 %collective-permute-start.28 = (bf16[512,512]{1,0:T(8,128)(2,1)S(1)}, bf16[512,512]{1,0:T(8,128)(2,1)S(1)}, u32[]{:S(2)}, u32[]{:S(2)}) collective-permute-start(bf16[512,512]{1,0:T(8,128)(2,1)S(1)} %get-tuple-element.31), channel_id=1, source_target_pairs={{0,1},{1,0},{2,3},{3,2},{4,5},{5,4},{6,7},{7,6},{8,9},{9,8},{10,11... | collective-permute-start | bytes 1572872 | tf_op jit(solution)/shard_map/ppermute | solution.py:441
  162.2 21.1 %collective-permute-start.29 = (bf16[512,512]{1,0:T(8,128)(2,1)S(1)}, bf16[512,512]{1,0:T(8,128)(2,1)S(1)}, u32[]{:S(2)}, u32[]{:S(2)}) collective-permute-start(bf16[512,512]{1,0:T(8,128)(2,1)S(1)} %get-tuple-element.32), channel_id=1, source_target_pairs={{1,2},{2,1},{5,6},{6,5},{9,10},{10,9},{13,14},{14,13},{17,18},{18,... | collective-permute-start | bytes 1572872 | tf_op jit(solution)/shard_map/ppermute | solution.py:442
  (16 other events, 283.1 us)

commit v4 on v3

--- a/solution.py
+++ b/solution.py
@@ -13,12 +13,19 @@
 PARTS = 2
 
 
+def held_out(array):
+    return pltpu.with_memory_space_constraint(array, pltpu.HBM)
+
+
 def states_kernel(
-    spans, keys_ref, values_ref, rates_ref, out_ref, gated_ref, keys_buf, values_buf, gated_buf, rows_buf, sems
+    spans, keys_ref, values_ref, rates_hbm, out_ref, gated_ref,
+    rates_ref, keys_buf, values_buf, gated_buf, rows_buf, sems, rates_sem,
 ):
     tokens, channels = gated_ref.shape
     length, lanes = tokens // spans, keys_buf.shape[2]
     groups = [(span, first) for first in range(0, channels, lanes) for span in range(spans)]
+    table = pltpu.make_async_copy(rates_hbm, rates_ref, rates_sem)
+    table.start()
     copies = []
     for index, (span, first) in enumerate(groups):
         at = (pl.ds(span * length, length), pl.ds(first, lanes))
@@ -29,6 +36,7 @@
         for copy in pair:
             copy.start()
         copies.append(pair)
+    table.wait()
     for index, (span, first) in enumerate(groups):
         for copy in copies[index]:
             copy.wait()
@@ -70,18 +78,20 @@
             jax.ShapeDtypeStruct((spans, modes, channels), jnp.float32),
             jax.ShapeDtypeStruct((tokens, channels), jnp.bfloat16),
         ],
-        in_specs=[outside, outside, inside],
-        out_specs=[inside, outside],
+        in_specs=[outside, outside, outside],
+        out_specs=[inside, pl.BlockSpec(memory_space=pl.ANY)],
         scratch_shapes=[
+            pltpu.VMEM((modes, channels), jnp.float32),
             pltpu.VMEM((count, length, lanes), jnp.bfloat16),
             pltpu.VMEM((count, length, lanes), jnp.bfloat16),
             pltpu.VMEM((count, length, lanes), jnp.bfloat16),
             pltpu.VMEM((length, lanes), jnp.float32),
             pltpu.SemaphoreType.DMA((3, count)),
+            pltpu.SemaphoreType.DMA(()),
         ],
-        compiler_params=pltpu.CompilerParams(vmem_limit_bytes=62 << 20),
+        compiler_params=pltpu.CompilerParams(vmem_limit_bytes=8 << 20),
         name="span_states",
-    )(keys, values, rates)
+    )(held_out(keys), held_out(values), held_out(rates))
 
 
 def fold_rows(parts):
@@ -168,8 +178,8 @@
         out_shape=jax.ShapeDtypeStruct((length, width), jnp.bfloat16),
         in_specs=[
             pl.BlockSpec(memory_space=pltpu.SMEM),
-            pl.BlockSpec(memory_space=pltpu.HBM),
-            pl.BlockSpec(memory_space=pltpu.HBM),
+            pl.BlockSpec(memory_space=pl.ANY),
+            pl.BlockSpec(memory_space=pl.ANY),
             inside,
             inside,
             *[inside] * len(states),
@@ -209,7 +219,7 @@
         pieces.append(lax.ppermute(piece, "tp", [(i, (i + shift) % n) for i in range(n)]))
     held = jnp.stack(pieces)
     strips = {0: held}
-    for other in range(2, ctx, 2):
+    for other in range(ctx - 2, 0, -2):
         strips[other] = lax.ppermute(held, "ctx", [(i, i ^ other) for i in range(ctx)])
     for other in range(0, ctx, 2):
         strips[other + 1] = lax.ppermute(strips[other], "ctx", [(i, i ^ 1) for i in range(ctx)])
@@ -316,7 +326,7 @@
         ],
         compiler_params=pltpu.CompilerParams(vmem_limit_bytes=24 << 20),
         name="upper",
-    )(*operands)
+    )(held_out(out_weight), *operands[1:])
 
 
 def finish_kernel(part, unused_ref, product_ref, left_ref, right_ref, out_ref, result_ref, sem):
@@ -418,7 +428,7 @@
     return pl.pallas_call(
         functools.partial(product_kernel, part, parts),
         out_shape=jax.ShapeDtypeStruct((height, n * width), jnp.bfloat16),
-        in_specs=[inside, pl.BlockSpec(memory_space=pltpu.HBM)],
+        in_specs=[inside, pl.BlockSpec(memory_space=pl.ANY)],
         out_specs=inside,
         scratch_shapes=[pltpu.VMEM((n, channels, width), jnp.bfloat16), pltpu.SemaphoreType.DMA((n,))],
         compiler_params=pltpu.CompilerParams(vmem_limit_bytes=8 << 20),

time: 185 us -> 180 us (0.973)
  local copies, waits for them, and re-layouts: 10.8 us -> 6.65 us
    unnamed x23 -> x17, local copies, waits for them, and re-layouts: 9.14 us -> 5.01 us
  transfers between devices with their start and end apart: 30 -> 30, of which waited for: 14 -> 14; matrix products, arithmetic and copies ran while one was open for 1% -> 1% of each run, Pallas kernels for 19% -> 20%
where the time goes in v4:
time: 180 us
  waiting for transfers between devices  80.6 us (45%)
  Pallas kernels  51 us (28%)
  starting transfers between devices  41 us (23%)
  local copies, waits for them, and re-layouts  6.65 us (4%)
    ppermute x8, starting transfers between devices, exchange(): odds[slot, part] = lax.ppermute(odd, 'tp', pairs[1])  26.2 us
    ppermute x3, waiting for transfers between devices, gather_weights(): lax.ppermute(held, 'ctx', [(i, i ^ other) for i in range(ctx)])  23.7 us
    ppermute x8, waiting for transfers between devices, exchange(): odds[slot, part] = lax.ppermute(odd, 'tp', pairs[1])  23.7 us
    ppermute x3, waiting for transfers between devices, gather_weights(): lax.ppermute(piece, 'tp', [(i, (i + shift) % n) for i in range(n)])  21.3 us
    pallas_call x3, Pallas kernels, convolve(): pl.pallas_call(functools.partial(convolve_kernel, span, spans, part * wid...  19.4 us
    pallas_call x1, Pallas kernels, upper(): pl.pallas_call(functools.partial(upper_kernel, n, ctx, parts), out_shape=...  10.7 us
    pallas_call x1, Pallas kernels, span_states(): pl.pallas_call(functools.partial(states_kernel, spans), out_shape=[jax.Sh...  8.52 us
    pallas_call x2, Pallas kernels, local_product(): pl.pallas_call(functools.partial(product_kernel, part, parts), out_shape=...  7.07 us
  transfers between devices with their start and end apart: 30, of which 14 were waited for; matrix products, arithmetic and copies ran while one was open for 1% of the time, Pallas kernels for 20%

profile of v4, /device:TPU:10, one launch (start us, length us, event | category | flops | bytes accessed | tf_op | source)
XLA Modules:
  0.0 179.8 jit_solution(6915439523616949996)
XLA Ops:
  0.0 8.5 %span_states.1 = (f32[2,16,1024]{2,1,0:T(8,128)S(1)}, bf16[1024,1024]{1,0:T(8,128)(2,1)S(1)}) custom-call(bf16[1024,1024]{1,0:T(8,128)(2,1)} %keys_ref.1, bf16[1024,1024]{1,0:T(8,128)(2,1)} %values_ref.1, f32[16,1024]{1,0:T(8,128)} %rates_ref.5), custom_call_target="tpu_custom_call" | custom-call | tf_op jit(solution)/shard_map/span_states/pallas_call | solution.py:75
  12.1 2.9 %collective-permute-done.10 = f32[2,16,1024]{2,1,0:T(8,128)S(1)} collective-permute-done((f32[2,16,1024]{2,1,0:T(8,128)S(1)}, f32[2,16,1024]{2,1,0:T(8,128)S(1)}, u32[]{:S(2)}, u32[]{:S(2)}) %collective-permute-start.10) | collective-permute-done | bytes 131104 | tf_op jit(solution)/shard_map/ppermute | solution.py:203
  19.6 5.4 %convolve.3.refs_9_ = bf16[512,512]{1,0:T(8,128)(2,1)} custom-call(s32[16]{0:T(128)S(1)} %copy-done.6, bf16[1024,1024]{1,0:T(8,128)(2,1)S(1)} %copy-done.1, bf16[1024,1024]{1,0:T(8,128)(2,1)S(1)} %get-tuple-element.19.gated_ref, f32[16,1024]{1,0:T(8,128)S(1)} %copy-done.5, f32[16,1024]{1,0:T(8,128)S(1)} %copy-done.4, ...), custom_call_target="tpu_custom_call" | custom-call | tf_op jit(solution)/shard_map/convolve/pallas_call | solution.py:176
  25.5 4.6 %collective-permute-start.16 = (bf16[512,512]{1,0:T(8,128)(2,1)}, bf16[512,512]{1,0:T(8,128)(2,1)}, u32[]{:S(2)}, u32[]{:S(2)}) collective-permute-start(bf16[512,512]{1,0:T(8,128)(2,1)} %convolve.3.refs_9_), channel_id=1, source_target_pairs={{1,2},{2,1},{5,6},{6,5},{9,10},{10,9},{13,14},{14,13},{17,18},{18,... | collective-permute-start | bytes 1572872 | tf_op jit(solution)/shard_map/ppermute | solution.py:452
  30.1 5.4 %convolve.4.refs_10_ = bf16[512,512]{1,0:T(8,128)(2,1)} custom-call(s32[16]{0:T(128)S(1)} %copy-done.6, bf16[1024,1024]{1,0:T(8,128)(2,1)S(1)} %copy-done.1, bf16[1024,1024]{1,0:T(8,128)(2,1)S(1)} %get-tuple-element.19.gated_ref, f32[16,1024]{1,0:T(8,128)S(1)} %copy-done.5, f32[16,1024]{1,0:T(8,128)S(1)} %copy-done.4, ...), custom_call_target="tpu_custom_call" | custom-call | tf_op jit(solution)/shard_map/convolve/pallas_call | solution.py:176
  40.8 8.6 %convolve.5.rows_ref = bf16[512,1024]{1,0:T(8,128)(2,1)S(1)} custom-call(s32[16]{0:T(128)S(1)} %copy-done.6, bf16[1024,1024]{1,0:T(8,128)(2,1)S(1)} %copy-done.1, bf16[1024,1024]{1,0:T(8,128)(2,1)S(1)} %copy-done.3, f32[16,1024]{1,0:T(8,128)S(1)} %copy-done.5, f32[16,1024]{1,0:T(8,128)S(1)} %copy-done.4, ...), custom_call_target="tpu_custom_call" | custom-call | tf_op jit(solution)/shard_map/convolve/pallas_call | solution.py:176
  49.4 3.4 %copy-done = bf16[1024,4096]{1,0:T(8,128)(2,1)S(1)} copy-done((bf16[1024,4096]{1,0:T(8,128)(2,1)S(1)}, bf16[1024,4096]{1,0:T(8,128)(2,1)}, u32[]{:S(2)}) %copy-start) | copy-done | bytes 8388632
  52.8 3.5 %local_product.2.product_ref = bf16[512,2048]{1,0:T(8,128)(2,1)S(1)} custom-call(bf16[512,1024]{1,0:T(8,128)(2,1)S(1)} %convolve.5.rows_ref, bf16[1024,4096]{1,0:T(8,128)(2,1)S(1)} %copy-done), custom_call_target="tpu_custom_call" | custom-call | tf_op jit(solution)/shard_map/local_product/pallas_call | solution.py:428
  59.8 3.4 %collective-permute-start.20 = (bf16[512,512]{1,0:T(8,128)(2,1)S(1)}, bf16[512,512]{1,0:T(8,128)(2,1)S(1)}, u32[]{:S(2)}, u32[]{:S(2)}) collective-permute-start(bf16[512,512]{1,0:T(8,128)(2,1)S(1)} %get-tuple-element.23), channel_id=1, source_target_pairs={{1,2},{2,1},{5,6},{6,5},{9,10},{10,9},{13,14},{14,13},{17,18},{18,... | collective-permute-start | bytes 1572872 | tf_op jit(solution)/shard_map/ppermute | solution.py:452
  64.9 3.5 %local_product.3.product_ref = bf16[512,2048]{1,0:T(8,128)(2,1)S(1)} custom-call(bf16[512,1024]{1,0:T(8,128)(2,1)S(1)} %convolve.5.rows_ref, bf16[1024,4096]{1,0:T(8,128)(2,1)S(1)} %copy-done), custom_call_target="tpu_custom_call" | custom-call | tf_op jit(solution)/shard_map/local_product/pallas_call | solution.py:428
  69.8 6.2 %collective-permute-done.2 = bf16[128,1024]{1,0:T(8,128)(2,1)S(1)} collective-permute-done((bf16[128,1024]{1,0:T(8,128)(2,1)S(1)}, bf16[128,1024]{1,0:T(8,128)(2,1)S(1)}, u32[]{:S(2)}, u32[]{:S(2)}) %collective-permute-start.2) | collective-permute-done | bytes 262176 | tf_op jit(solution)/shard_map/ppermute | solution.py:219
  76.0 2.5 %collective-permute-start.19 = (bf16[512,512]{1,0:T(8,128)(2,1)S(1)}, bf16[512,512]{1,0:T(8,128)(2,1)S(1)}, u32[]{:S(2)}, u32[]{:S(2)}) collective-permute-start(bf16[512,512]{1,0:T(8,128)(2,1)S(1)} %get-tuple-element.22), channel_id=1, source_target_pairs={{0,1},{1,0},{2,3},{3,2},{4,5},{5,4},{6,7},{7,6},{8,9},{9,8},{10,11... | collective-permute-start | bytes 1572872 | tf_op jit(solution)/shard_map/ppermute | solution.py:451
  78.5 14.0 %collective-permute-done.1 = bf16[128,1024]{1,0:T(8,128)(2,1)S(1)} collective-permute-done((bf16[128,1024]{1,0:T(8,128)(2,1)S(1)}, bf16[128,1024]{1,0:T(8,128)(2,1)S(1)}, u32[]{:S(2)}, u32[]{:S(2)}) %collective-permute-start.1) | collective-permute-done | bytes 262176 | tf_op jit(solution)/shard_map/ppermute | solution.py:219
  92.4 3.7 %collective-permute-start.22 = (bf16[512,512]{1,0:T(8,128)(2,1)S(1)}, bf16[512,512]{1,0:T(8,128)(2,1)S(1)}, u32[]{:S(2)}, u32[]{:S(2)}) collective-permute-start(bf16[512,512]{1,0:T(8,128)(2,1)S(1)} %get-tuple-element.25), channel_id=1, source_target_pairs={{1,2},{2,1},{5,6},{6,5},{9,10},{10,9},{13,14},{14,13},{17,18},{18,... | collective-permute-start | bytes 1572872 | tf_op jit(solution)/shard_map/ppermute | solution.py:452
  101.2 5.9 %collective-permute-done.22.odd_ref.refs_20_ = bf16[512,512]{1,0:T(8,128)(2,1)S(1)} collective-permute-done((bf16[512,512]{1,0:T(8,128)(2,1)S(1)}, bf16[512,512]{1,0:T(8,128)(2,1)S(1)}, u32[]{:S(2)}, u32[]{:S(2)}) %collective-permute-start.22) | collective-permute-done | bytes 524320 | tf_op jit(solution)/shard_map/ppermute | solution.py:452
  107.3 10.6 %collective-permute-done.4.refs_3_ = bf16[3,128,1024]{2,1,0:T(8,128)(2,1)S(1)} collective-permute-done((bf16[3,128,1024]{2,1,0:T(8,128)(2,1)S(1)}, bf16[3,128,1024]{2,1,0:T(8,128)(2,1)S(1)}, u32[]{:S(2)}, u32[]{:S(2)}) %collective-permute-start.4) | collective-permute-done | bytes 786464 | tf_op jit(solution)/shard_map/ppermute | solution.py:223
  117.8 13.2 %collective-permute-done.6.refs_5_ = bf16[3,128,1024]{2,1,0:T(8,128)(2,1)S(1)} collective-permute-done((bf16[3,128,1024]{2,1,0:T(8,128)(2,1)S(1)}, bf16[3,128,1024]{2,1,0:T(8,128)(2,1)S(1)}, u32[]{:S(2)}, u32[]{:S(2)}) %collective-permute-start.6) | collective-permute-done | bytes 786464 | tf_op jit(solution)/shard_map/ppermute | solution.py:223
  131.0 4.1 %collective-permute-start.24 = (bf16[512,512]{1,0:T(8,128)(2,1)S(1)}, bf16[512,512]{1,0:T(8,128)(2,1)S(1)}, u32[]{:S(2)}, u32[]{:S(2)}) collective-permute-start(bf16[512,512]{1,0:T(8,128)(2,1)S(1)} %get-tuple-element.27), channel_id=1, source_target_pairs={{1,2},{2,1},{5,6},{6,5},{9,10},{10,9},{13,14},{14,13},{17,18},{18,... | collective-permute-start | bytes 1572872 | tf_op jit(solution)/shard_map/ppermute | solution.py:452
  137.6 7.9 %collective-permute-done.24.refs_21_.odd_ref = bf16[512,512]{1,0:T(8,128)(2,1)S(1)} collective-permute-done((bf16[512,512]{1,0:T(8,128)(2,1)S(1)}, bf16[512,512]{1,0:T(8,128)(2,1)S(1)}, u32[]{:S(2)}, u32[]{:S(2)}) %collective-permute-start.24) | collective-permute-done | bytes 524320 | tf_op jit(solution)/shard_map/ppermute | solution.py:452
  145.7 7.8 %collective-permute-done.25.refs_22_.odd_ref = bf16[512,512]{1,0:T(8,128)(2,1)S(1)} collective-permute-done((bf16[512,512]{1,0:T(8,128)(2,1)S(1)}, bf16[512,512]{1,0:T(8,128)(2,1)S(1)}, u32[]{:S(2)}, u32[]{:S(2)}) %collective-permute-start.25) | collective-permute-done | bytes 524320 | tf_op jit(solution)/shard_map/ppermute | solution.py:452
  153.7 3.9 %collective-permute-start.27 = (bf16[512,512]{1,0:T(8,128)(2,1)S(1)}, bf16[512,512]{1,0:T(8,128)(2,1)S(1)}, u32[]{:S(2)}, u32[]{:S(2)}) collective-permute-start(bf16[512,512]{1,0:T(8,128)(2,1)S(1)} %get-tuple-element.30), channel_id=1, source_target_pairs={{1,2},{2,1},{5,6},{6,5},{9,10},{10,9},{13,14},{14,13},{17,18},{18,... | collective-permute-start | bytes 1572872 | tf_op jit(solution)/shard_map/ppermute | solution.py:452
  157.7 2.7 %collective-permute-start.29 = (bf16[512,512]{1,0:T(8,128)(2,1)S(1)}, bf16[512,512]{1,0:T(8,128)(2,1)S(1)}, u32[]{:S(2)}, u32[]{:S(2)}) collective-permute-start(bf16[512,512]{1,0:T(8,128)(2,1)S(1)} %get-tuple-element.32), channel_id=1, source_target_pairs={{1,2},{2,1},{5,6},{6,5},{9,10},{10,9},{13,14},{14,13},{17,18},{18,... | collective-permute-start | bytes 1572872 | tf_op jit(solution)/shard_map/ppermute | solution.py:452
  160.4 10.7 %upper.1.unused_ref = bf16[1024,1024]{1,0:T(8,128)(2,1)} custom-call(bf16[1024,4096]{1,0:T(8,128)(2,1)} %refs_0_.1, bf16[3,128,1024]{2,1,0:T(8,128)(2,1)S(1)} %pad_maximum_fusion.refs_1_, bf16[3,128,1024]{2,1,0:T(8,128)(2,1)S(1)} %collective-permute-done.3.refs_2_, bf16[3,128,1024]{2,1,0:T(8,128)(2,1)S(1)} %collective-permute-done.4.refs_3_, ...), custom_call_target="tpu_custom_call" | custom-call | tf_op jit(solution)/shard_map/upper/pallas_call | solution.py:311
  172.1 4.5 %collective-permute-done.28.left_ref = bf16[512,512]{1,0:T(8,128)(2,1)S(1)} collective-permute-done((bf16[512,512]{1,0:T(8,128)(2,1)S(1)}, bf16[512,512]{1,0:T(8,128)(2,1)S(1)}, u32[]{:S(2)}, u32[]{:S(2)}) %collective-permute-start.28) | collective-permute-done | bytes 524320 | tf_op jit(solution)/shard_map/ppermute | solution.py:451
  (71 shorter events, 32.6 us)
Async XLA Ops:
  25.0 31.3 %collective-permute-start.14 = (bf16[512,512]{1,0:T(8,128)(2,1)}, bf16[512,512]{1,0:T(8,128)(2,1)}, u32[]{:S(2)}, u32[]{:S(2)}) collective-permute-start(bf16[512,512]{1,0:T(8,128)(2,1)} %convolve.3.refs_9_), channel_id=1, source_target_pairs={{0,1},{1,0},{2,3},{3,2},{4,5},{5,4},{6,7},{7,6},{8,9},{9,8},{10,11... | collective-permute-start | bytes 1572872 | tf_op jit(solution)/shard_map/ppermute | solution.py:451
  25.5 30.8 %collective-permute-start.16 = (bf16[512,512]{1,0:T(8,128)(2,1)}, bf16[512,512]{1,0:T(8,128)(2,1)}, u32[]{:S(2)}, u32[]{:S(2)}) collective-permute-start(bf16[512,512]{1,0:T(8,128)(2,1)} %convolve.3.refs_9_), channel_id=1, source_target_pairs={{1,2},{2,1},{5,6},{6,5},{9,10},{10,9},{13,14},{14,13},{17,18},{18,... | collective-permute-start | bytes 1572872 | tf_op jit(solution)/shard_map/ppermute | solution.py:452
  35.5 27.7 %collective-permute-start.15 = (bf16[512,512]{1,0:T(8,128)(2,1)}, bf16[512,512]{1,0:T(8,128)(2,1)}, u32[]{:S(2)}, u32[]{:S(2)}) collective-permute-start(bf16[512,512]{1,0:T(8,128)(2,1)} %convolve.4.refs_10_), channel_id=1, source_target_pairs={{0,1},{1,0},{2,3},{3,2},{4,5},{5,4},{6,7},{7,6},{8,9},{9,8},{10,11... | collective-permute-start | bytes 1572872 | tf_op jit(solution)/shard_map/ppermute | solution.py:451
  35.6 27.7 %collective-permute-start.18 = (bf16[512,512]{1,0:T(8,128)(2,1)}, bf16[512,512]{1,0:T(8,128)(2,1)}, u32[]{:S(2)}, u32[]{:S(2)}) collective-permute-start(bf16[512,512]{1,0:T(8,128)(2,1)} %convolve.4.refs_10_), channel_id=1, source_target_pairs={{1,2},{2,1},{5,6},{6,5},{9,10},{10,9},{13,14},{14,13},{17,18},{18,... | collective-permute-start | bytes 1572872 | tf_op jit(solution)/shard_map/ppermute | solution.py:452
  57.7 40.6 %collective-permute-start.17 = (bf16[512,512]{1,0:T(8,128)(2,1)S(1)}, bf16[512,512]{1,0:T(8,128)(2,1)S(1)}, u32[]{:S(2)}, u32[]{:S(2)}) collective-permute-start(bf16[512,512]{1,0:T(8,128)(2,1)S(1)} %get-tuple-element.21), channel_id=1, source_target_pairs={{0,1},{1,0},{2,3},{3,2},{4,5},{5,4},{6,7},{7,6},{8,9},{9,8},{10,11... | collective-permute-start | bytes 1572872 | tf_op jit(solution)/shard_map/ppermute | solution.py:451
  59.3 16.6 %collective-permute-start.2 = (bf16[128,1024]{1,0:T(8,128)(2,1)S(1)}, bf16[128,1024]{1,0:T(8,128)(2,1)S(1)}, u32[]{:S(2)}, u32[]{:S(2)}) collective-permute-start(bf16[128,1024]{1,0:T(8,128)(2,1)S(1)} %get-tuple-element.34), channel_id=1, source_target_pairs={{0,3},{1,0},{2,1},{3,2},{4,7},{5,4},{6,5},{7,6},{8,11},{9,8},{10,9... | collective-permute-start | bytes 786440 | tf_op jit(solution)/shard_map/ppermute | solution.py:219
  59.8 40.0 %collective-permute-start.20 = (bf16[512,512]{1,0:T(8,128)(2,1)S(1)}, bf16[512,512]{1,0:T(8,128)(2,1)S(1)}, u32[]{:S(2)}, u32[]{:S(2)}) collective-permute-start(bf16[512,512]{1,0:T(8,128)(2,1)S(1)} %get-tuple-element.23), channel_id=1, source_target_pairs={{1,2},{2,1},{5,6},{6,5},{9,10},{10,9},{13,14},{14,13},{17,18},{18,... | collective-permute-start | bytes 1572872 | tf_op jit(solution)/shard_map/ppermute | solution.py:452
  63.2 29.2 %collective-permute-start.1 = (bf16[128,1024]{1,0:T(8,128)(2,1)S(1)}, bf16[128,1024]{1,0:T(8,128)(2,1)S(1)}, u32[]{:S(2)}, u32[]{:S(2)}) collective-permute-start(bf16[128,1024]{1,0:T(8,128)(2,1)S(1)} %get-tuple-element.35), channel_id=1, source_target_pairs={{0,2},{1,3},{2,0},{3,1},{4,6},{5,7},{6,4},{7,5},{8,10},{9,11},{10,... | collective-permute-start | bytes 786440 | tf_op jit(solution)/shard_map/ppermute | solution.py:219
  63.3 33.9 %collective-permute-start = (bf16[128,1024]{1,0:T(8,128)(2,1)S(1)}, bf16[128,1024]{1,0:T(8,128)(2,1)S(1)}, u32[]{:S(2)}, u32[]{:S(2)}) collective-permute-start(bf16[128,1024]{1,0:T(8,128)(2,1)S(1)} %get-tuple-element.33), channel_id=1, source_target_pairs={{0,1},{1,2},{2,3},{3,0},{4,5},{5,6},{6,7},{7,4},{8,9},{9,10},{10,1... | collective-permute-start | bytes 786440 | tf_op jit(solution)/shard_map/ppermute | solution.py:219
  76.0 25.1 %collective-permute-start.19 = (bf16[512,512]{1,0:T(8,128)(2,1)S(1)}, bf16[512,512]{1,0:T(8,128)(2,1)S(1)}, u32[]{:S(2)}, u32[]{:S(2)}) collective-permute-start(bf16[512,512]{1,0:T(8,128)(2,1)S(1)} %get-tuple-element.22), channel_id=1, source_target_pairs={{0,1},{1,0},{2,3},{3,2},{4,5},{5,4},{6,7},{7,6},{8,9},{9,8},{10,11... | collective-permute-start | bytes 1572872 | tf_op jit(solution)/shard_map/ppermute | solution.py:451
  97.4 20.5 %collective-permute-start.4 = (bf16[3,128,1024]{2,1,0:T(8,128)(2,1)S(1)}, bf16[3,128,1024]{2,1,0:T(8,128)(2,1)S(1)}, u32[]{:S(2)}, u32[]{:S(2)}) collective-permute-start(bf16[3,128,1024]{2,1,0:T(8,128)(2,1)S(1)} %pad_maximum_fusion.refs_1_), channel_id=1, source_target_pairs={{0,8},{4,12},{8,0},{12,4},{16,24},{20,28},{24,16},{28,20},{1,9},{5... | collective-permute-start | bytes 2359304 | tf_op jit(solution)/shard_map/ppermute | solution.py:223
  98.3 32.8 %collective-permute-start.6 = (bf16[3,128,1024]{2,1,0:T(8,128)(2,1)S(1)}, bf16[3,128,1024]{2,1,0:T(8,128)(2,1)S(1)}, u32[]{:S(2)}, u32[]{:S(2)}) collective-permute-start(bf16[3,128,1024]{2,1,0:T(8,128)(2,1)S(1)} %pad_maximum_fusion.refs_1_), channel_id=1, source_target_pairs={{0,16},{4,20},{8,24},{12,28},{16,0},{20,4},{24,8},{28,12},{1,17},{... | collective-permute-start | bytes 2359304 | tf_op jit(solution)/shard_map/ppermute | solution.py:223
  99.8 35.3 %collective-permute-start.8 = (bf16[3,128,1024]{2,1,0:T(8,128)(2,1)S(1)}, bf16[3,128,1024]{2,1,0:T(8,128)(2,1)S(1)}, u32[]{:S(2)}, u32[]{:S(2)}) collective-permute-start(bf16[3,128,1024]{2,1,0:T(8,128)(2,1)S(1)} %pad_maximum_fusion.refs_1_), channel_id=1, source_target_pairs={{0,24},{4,28},{8,16},{12,20},{16,8},{20,12},{24,0},{28,4},{1,25},{... | collective-permute-start | bytes 2359304 | tf_op jit(solution)/shard_map/ppermute | solution.py:223
  101.1 34.1 %collective-permute-start.21 = (bf16[512,512]{1,0:T(8,128)(2,1)S(1)}, bf16[512,512]{1,0:T(8,128)(2,1)S(1)}, u32[]{:S(2)}, u32[]{:S(2)}) collective-permute-start(bf16[512,512]{1,0:T(8,128)(2,1)S(1)} %get-tuple-element.24), channel_id=1, source_target_pairs={{0,1},{1,0},{2,3},{3,2},{4,5},{5,4},{6,7},{7,6},{8,9},{9,8},{10,11... | collective-permute-start | bytes 1572872 | tf_op jit(solution)/shard_map/ppermute | solution.py:451
  107.2 28.5 %collective-permute-start.23 = (bf16[512,512]{1,0:T(8,128)(2,1)S(1)}, bf16[512,512]{1,0:T(8,128)(2,1)S(1)}, u32[]{:S(2)}, u32[]{:S(2)}) collective-permute-start(bf16[512,512]{1,0:T(8,128)(2,1)S(1)} %get-tuple-element.26), channel_id=1, source_target_pairs={{0,1},{1,0},{2,3},{3,2},{4,5},{5,4},{6,7},{7,6},{8,9},{9,8},{10,11... | collective-permute-start | bytes 1572872 | tf_op jit(solution)/shard_map/ppermute | solution.py:451
  117.8 35.8 %collective-permute-start.3 = (bf16[3,128,1024]{2,1,0:T(8,128)(2,1)S(1)}, bf16[3,128,1024]{2,1,0:T(8,128)(2,1)S(1)}, u32[]{:S(2)}, u32[]{:S(2)}) collective-permute-start(bf16[3,128,1024]{2,1,0:T(8,128)(2,1)S(1)} %pad_maximum_fusion.refs_1_), channel_id=1, source_target_pairs={{0,4},{4,0},{8,12},{12,8},{16,20},{20,16},{24,28},{28,24},{1,5},{5... | collective-permute-start | bytes 2359304 | tf_op jit(solution)/shard_map/ppermute | solution.py:225
  135.1 22.5 %collective-permute-start.5 = (bf16[3,128,1024]{2,1,0:T(8,128)(2,1)S(1)}, bf16[3,128,1024]{2,1,0:T(8,128)(2,1)S(1)}, u32[]{:S(2)}, u32[]{:S(2)}) collective-permute-start(bf16[3,128,1024]{2,1,0:T(8,128)(2,1)S(1)} %collective-permute-done.4.refs_3_), channel_id=1, source_target_pairs={{0,4},{4,0},{8,12},{12,8},{16,20},{20,16},{24,28},{28,24},{1,5},{5... | collective-permute-start | bytes 2359304 | tf_op jit(solution)/shard_map/ppermute | solution.py:225
  135.2 22.5 %collective-permute-start.7 = (bf16[3,128,1024]{2,1,0:T(8,128)(2,1)S(1)}, bf16[3,128,1024]{2,1,0:T(8,128)(2,1)S(1)}, u32[]{:S(2)}, u32[]{:S(2)}) collective-permute-start(bf16[3,128,1024]{2,1,0:T(8,128)(2,1)S(1)} %collective-permute-done.6.refs_5_), channel_id=1, source_target_pairs={{0,4},{4,0},{8,12},{12,8},{16,20},{20,16},{24,28},{28,24},{1,5},{5... | collective-permute-start | bytes 2359304 | tf_op jit(solution)/shard_map/ppermute | solution.py:225
  135.7 17.8 %collective-permute-start.25 = (bf16[512,512]{1,0:T(8,128)(2,1)S(1)}, bf16[512,512]{1,0:T(8,128)(2,1)S(1)}, u32[]{:S(2)}, u32[]{:S(2)}) collective-permute-start(bf16[512,512]{1,0:T(8,128)(2,1)S(1)} %get-tuple-element.28), channel_id=1, source_target_pairs={{1,2},{2,1},{5,6},{6,5},{9,10},{10,9},{13,14},{14,13},{17,18},{18,... | collective-permute-start | bytes 1572872 | tf_op jit(solution)/shard_map/ppermute | solution.py:452
  145.5 14.9 %collective-permute-start.9 = (bf16[3,128,1024]{2,1,0:T(8,128)(2,1)S(1)}, bf16[3,128,1024]{2,1,0:T(8,128)(2,1)S(1)}, u32[]{:S(2)}, u32[]{:S(2)}) collective-permute-start(bf16[3,128,1024]{2,1,0:T(8,128)(2,1)S(1)} %collective-permute-done.8.refs_7_), channel_id=1, source_target_pairs={{0,4},{4,0},{8,12},{12,8},{16,20},{20,16},{24,28},{28,24},{1,5},{5... | collective-permute-start | bytes 2359304 | tf_op jit(solution)/shard_map/ppermute | solution.py:225
  153.5 17.6 %collective-permute-start.26 = (bf16[512,512]{1,0:T(8,128)(2,1)S(1)}, bf16[512,512]{1,0:T(8,128)(2,1)S(1)}, u32[]{:S(2)}, u32[]{:S(2)}) collective-permute-start(bf16[512,512]{1,0:T(8,128)(2,1)S(1)} %get-tuple-element.29), channel_id=1, source_target_pairs={{0,1},{1,0},{2,3},{3,2},{4,5},{5,4},{6,7},{7,6},{8,9},{9,8},{10,11... | collective-permute-start | bytes 1572872 | tf_op jit(solution)/shard_map/ppermute | solution.py:451
  153.7 17.4 %collective-permute-start.27 = (bf16[512,512]{1,0:T(8,128)(2,1)S(1)}, bf16[512,512]{1,0:T(8,128)(2,1)S(1)}, u32[]{:S(2)}, u32[]{:S(2)}) collective-permute-start(bf16[512,512]{1,0:T(8,128)(2,1)S(1)} %get-tuple-element.30), channel_id=1, source_target_pairs={{1,2},{2,1},{5,6},{6,5},{9,10},{10,9},{13,14},{14,13},{17,18},{18,... | collective-permute-start | bytes 1572872 | tf_op jit(solution)/shard_map/ppermute | solution.py:452
  157.6 19.0 %collective-permute-start.28 = (bf16[512,512]{1,0:T(8,128)(2,1)S(1)}, bf16[512,512]{1,0:T(8,128)(2,1)S(1)}, u32[]{:S(2)}, u32[]{:S(2)}) collective-permute-start(bf16[512,512]{1,0:T(8,128)(2,1)S(1)} %get-tuple-element.31), channel_id=1, source_target_pairs={{0,1},{1,0},{2,3},{3,2},{4,5},{5,4},{6,7},{7,6},{8,9},{9,8},{10,11... | collective-permute-start | bytes 1572872 | tf_op jit(solution)/shard_map/ppermute | solution.py:451
  157.7 21.1 %collective-permute-start.29 = (bf16[512,512]{1,0:T(8,128)(2,1)S(1)}, bf16[512,512]{1,0:T(8,128)(2,1)S(1)}, u32[]{:S(2)}, u32[]{:S(2)}) collective-permute-start(bf16[512,512]{1,0:T(8,128)(2,1)S(1)} %get-tuple-element.32), channel_id=1, source_target_pairs={{1,2},{2,1},{5,6},{6,5},{9,10},{10,9},{13,14},{14,13},{17,18},{18,... | collective-permute-start | bytes 1572872 | tf_op jit(solution)/shard_map/ppermute | solution.py:452
  (13 other events, 156.3 us)

commit v5 on v4

--- a/solution.py
+++ b/solution.py
@@ -11,6 +11,10 @@
 ROWS = 16
 LANES = 512
 PARTS = 2
+FIRST = 4
+WIDE = 512
+UNROLL = 8
+DEPTH = 2
 
 
 def held_out(array):
@@ -55,7 +59,7 @@
             return state
 
         zero = jnp.zeros(decay.shape, jnp.float32)
-        out_ref[span, :, across] = lax.fori_loop(0, length // ROWS, body, zero)
+        out_ref[span, :, across] = lax.fori_loop(0, length // ROWS, body, zero, unroll=DEPTH)
         copy = pltpu.make_async_copy(
             gated_buf.at[index], gated_ref.at[pl.ds(span * length, length), across], sems.at[2, index]
         )
@@ -68,7 +72,7 @@
 def span_states(keys, values, rates, spans):
     tokens, channels = keys.shape
     length, modes = tokens // spans, rates.shape[0]
-    lanes = min(LANES, channels)
+    lanes = min(WIDE, channels)
     count = spans * (channels // lanes)
     inside = pl.BlockSpec(memory_space=pltpu.VMEM)
     outside = pl.BlockSpec(memory_space=pltpu.HBM)
@@ -106,13 +110,46 @@
     return parts[0]
 
 
+def entering_state(span, spans, length, order_ref, rates, states, across):
+    mine, count = lax.axis_index("ctx"), len(states)
+    here = order_ref[mine * spans + span]
+    entering = jnp.zeros(rates.shape, jnp.float32)
+    for which, states_ref in enumerate(states):
+
+        def carry(source, state, which=which, states_ref=states_ref):
+            block = source
+            if count > 1:
+                other = (source // spans) * count + which
+                block = jnp.bitwise_xor(mine, other) * spans + source % spans
+            gap = here - 1 - order_ref[block]
+            reach = jnp.exp(-rates * (length * jnp.maximum(gap, 0)).astype(jnp.float32))
+            return state + jnp.where(gap >= 0, reach, 0.0) * states_ref[source, :, across]
+
+        entering = lax.fori_loop(0, states_ref.shape[0], carry, entering, unroll=UNROLL)
+    return entering
+
+
+def filtered_rows(decay, scaled, rows_buf, base, state):
+    groups = []
+    for group in range(0, ROWS, 8):
+        parts = []
+        for row in range(group, group + 8):
+            state = decay * state + rows_buf[pl.ds(base + row, 1), :]
+            seen = scaled * state
+            total = seen[0:8]
+            for mode in range(8, seen.shape[0], 8):
+                total = total + seen[mode : mode + 8]
+            parts.append(total)
+        groups.append(fold_rows(parts))
+    return jnp.concatenate(groups, axis=0), state
+
+
 def convolve_kernel(
     span, spans, first, count, order_ref, queries_ref, gated_ref, residues_ref, rates_ref, *refs
 ):
     states, (out_ref, queries_buf, gated_buf, rows_buf, sems) = refs[:count], refs[count:]
     length, width = out_ref.shape
     lanes = queries_buf.shape[2]
-    mine = lax.axis_index("ctx")
     copies = []
     for index in range(width // lanes):
         at = (pl.ds(span * length, length), pl.ds(first + index * lanes, lanes))
@@ -123,25 +160,12 @@
         for copy in pair:
             copy.start()
         copies.append(pair)
-    here = order_ref[mine * spans + span]
     for index in range(width // lanes):
         across = pl.ds(first + index * lanes, lanes)
         rates = rates_ref[:, across]
         decay = jnp.exp(-rates)
         scaled = residues_ref[:, across] * jnp.sqrt(2.0 * rates)
-        entering = jnp.zeros(rates.shape, jnp.float32)
-        for which, states_ref in enumerate(states):
-
-            def carry(source, state, which=which, states_ref=states_ref, rates=rates, across=across):
-                block = source
-                if count > 1:
-                    other = (source // spans) * count + which
-                    block = jnp.bitwise_xor(mine, other) * spans + source % spans
-                gap = here - 1 - order_ref[block]
-                reach = jnp.exp(-rates * (length * jnp.maximum(gap, 0)).astype(jnp.float32))
-                return state + jnp.where(gap >= 0, reach, 0.0) * states_ref[source, :, across]
-
-            entering = lax.fori_loop(0, states_ref.shape[0], carry, entering)
+        entering = entering_state(span, spans, length, order_ref, rates, states, across)
         for copy in copies[index]:
             copy.wait()
 
@@ -149,32 +173,22 @@
             base = pl.multiple_of(step * ROWS, ROWS)
             rows = pl.ds(base, ROWS)
             rows_buf[rows, :] = gated_buf[index, rows, :].astype(jnp.float32)
-            groups = []
-            for group in range(0, ROWS, 8):
-                parts = []
-                for row in range(group, group + 8):
-                    state = decay * state + rows_buf[pl.ds(base + row, 1), :]
-                    seen = scaled * state
-                    total = seen[0:8]
-                    for mode in range(8, seen.shape[0], 8):
-                        total = total + seen[mode : mode + 8]
-                    parts.append(total)
-                groups.append(fold_rows(parts))
-            mixed = jnp.concatenate(groups, axis=0).astype(jnp.bfloat16).astype(jnp.float32)
+            sums, state = filtered_rows(decay, scaled, rows_buf, base, state)
+            mixed = sums.astype(jnp.bfloat16).astype(jnp.float32)
             gate = queries_buf[index, rows, :].astype(jnp.float32)
             out_ref[rows, index * lanes : (index + 1) * lanes] = (gate * mixed).astype(jnp.bfloat16)
             return state
 
-        lax.fori_loop(0, length // ROWS, body, entering)
-
-
-def convolve(order, queries, gated, residues, rates, states, spans, span, part, parts):
-    tokens, channels = queries.shape
-    length, width = tokens // spans, channels // parts
-    lanes = min(LANES, width)
+        lax.fori_loop(0, length // ROWS, body, entering, unroll=DEPTH)
+
+
+def convolve(order, queries, gated, residues, rates, states, spans, span, first, width):
+    tokens, _ = queries.shape
+    length = tokens // spans
+    lanes = width if width % LANES else LANES
     inside = pl.BlockSpec(memory_space=pltpu.VMEM)
     return pl.pallas_call(
-        functools.partial(convolve_kernel, span, spans, part * width, len(states)),
+        functools.partial(convolve_kernel, span, spans, first, len(states)),
         out_shape=jax.ShapeDtypeStruct((length, width), jnp.bfloat16),
         in_specs=[
             pl.BlockSpec(memory_space=pltpu.SMEM),
@@ -191,9 +205,120 @@
             pltpu.VMEM((length, lanes), jnp.float32),
             pltpu.SemaphoreType.DMA((2, width // lanes)),
         ],
-        compiler_params=pltpu.CompilerParams(vmem_limit_bytes=6 << 20),
+        compiler_params=pltpu.CompilerParams(vmem_limit_bytes=8 << 20),
         name="convolve",
     )(order, queries, gated, residues, rates, *states)
+
+
+def response_kernel(span, first, gated_ref, residues_ref, rates_ref, out_ref, gated_buf, rows_buf, sem):
+    length, width = out_ref.shape
+    at = (pl.ds(span * length, length), pl.ds(first, width))
+    copy = pltpu.make_async_copy(gated_ref.at[at], gated_buf, sem)
+    copy.start()
+    rates = rates_ref[:, at[1]]
+    decay = jnp.exp(-rates)
+    scaled = residues_ref[:, at[1]] * jnp.sqrt(2.0 * rates)
+    copy.wait()
+
+    def body(step, state):
+        base = pl.multiple_of(step * ROWS, ROWS)
+        rows = pl.ds(base, ROWS)
+        rows_buf[rows, :] = gated_buf[rows, :].astype(jnp.float32)
+        out_ref[rows, :], state = filtered_rows(decay, scaled, rows_buf, base, state)
+        return state
+
+    lax.fori_loop(0, length // ROWS, body, jnp.zeros(rates.shape, jnp.float32), unroll=DEPTH)
+
+
+def span_response(gated, residues, rates, spans, span, first, width):
+    length = gated.shape[0] // spans
+    inside = pl.BlockSpec(memory_space=pltpu.VMEM)
+    return pl.pallas_call(
+        functools.partial(response_kernel, span, first),
+        out_shape=jax.ShapeDtypeStruct((length, width), jnp.float32),
+        in_specs=[pl.BlockSpec(memory_space=pl.ANY), inside, inside],
+        out_specs=inside,
+        scratch_shapes=[
+            pltpu.VMEM((length, width), jnp.bfloat16),
+            pltpu.VMEM((length, width), jnp.float32),
+            pltpu.SemaphoreType.DMA(()),
+        ],
+        compiler_params=pltpu.CompilerParams(vmem_limit_bytes=4 << 20),
+        name="span_response",
+    )(gated, residues, rates)
+
+
+def complete_kernel(
+    span, spans, first, count, order_ref, queries_ref, response_ref, residues_ref, rates_ref, *refs
+):
+    states, (out_ref, queries_buf, state_buf, sem) = refs[:count], refs[count:]
+    length, width = out_ref.shape
+    across = pl.ds(first, width)
+    copy = pltpu.make_async_copy(queries_ref.at[pl.ds(span * length, length), across], queries_buf, sem)
+    copy.start()
+    rates = rates_ref[:, across]
+    modes = rates.shape[0]
+    entering = entering_state(span, spans, length, order_ref, rates, states, across)
+    decay = jnp.exp(-rates * float(ROWS))
+
+    def spread(block, state):
+        state_buf[block] = state
+        return decay * state
+
+    lax.fori_loop(0, length // ROWS, spread, entering, unroll=4)
+    copy.wait()
+    lags = lax.broadcasted_iota(jnp.int32, (8, 128), 0).astype(jnp.float32)
+    for tile in range(0, width, 128):
+        here = pl.ds(first + tile, 128)
+        cells = slice(tile, tile + 128)
+        tables = []
+        for mode in range(modes):
+            rate = rates_ref[mode : mode + 1, here]
+            scale = residues_ref[mode : mode + 1, here] * jnp.sqrt(2.0 * rate)
+            tables.append([scale * jnp.exp(-rate * (lags + float(start + 1))) for start in range(0, ROWS, 8)])
+
+        def body(block, unused, tables=tables, cells=cells):
+            base = pl.multiple_of(block * ROWS, ROWS)
+            sums = []
+            for half in range(ROWS // 8):
+                total = [response_ref[pl.ds(base + 8 * half, 8), cells], None]
+                for mode in range(modes):
+                    term = tables[mode][half] * state_buf[block, mode : mode + 1, cells]
+                    total[mode % 2] = term if total[mode % 2] is None else total[mode % 2] + term
+                sums.append(total[0] + total[1])
+            mixed = jnp.concatenate(sums, axis=0).astype(jnp.bfloat16).astype(jnp.float32)
+            rows = pl.ds(base, ROWS)
+            gate = queries_buf[rows, cells].astype(jnp.float32)
+            out_ref[rows, cells] = (gate * mixed).astype(jnp.bfloat16)
+            return unused
+
+        lax.fori_loop(0, length // ROWS, body, 0, unroll=2)
+
+
+def complete(order, queries, response, residues, rates, states, spans, span, first):
+    length, width = response.shape
+    modes = rates.shape[0]
+    inside = pl.BlockSpec(memory_space=pltpu.VMEM)
+    return pl.pallas_call(
+        functools.partial(complete_kernel, span, spans, first, len(states)),
+        out_shape=jax.ShapeDtypeStruct((length, width), jnp.bfloat16),
+        in_specs=[
+            pl.BlockSpec(memory_space=pltpu.SMEM),
+            pl.BlockSpec(memory_space=pl.ANY),
+            inside,
+            inside,
+            inside,
+            *[inside] * len(states),
+        ],
+        out_specs=inside,
+        scratch_shapes=[
+            pltpu.VMEM((length, width), jnp.bfloat16),
+            pltpu.VMEM((length // ROWS, modes, width), jnp.float32),
+            pltpu.SemaphoreType.DMA(()),
+        ],
+        compiler_params=pltpu.CompilerParams(vmem_limit_bytes=4 << 20),
+        name="complete",
+    )(order, queries, response, residues, rates, *states)
 
 
 def exchange_states(totals):
@@ -206,17 +331,41 @@
     return [near, far]
 
 
+def strips_kernel(weight_ref, *refs):
+    outs, sems = refs[:-1], refs[-1]
+    rows, columns = outs[0].shape
+    start = pl.multiple_of(lax.axis_index("ctx") * rows, 16)
+    copies = []
+    for index, out_ref in enumerate(outs):
+        target = jnp.bitwise_xor(lax.axis_index("tp"), index + 1)
+        at = (pl.ds(start, rows), pl.ds(pl.multiple_of(target * columns, 128), columns))
+        copy = pltpu.make_async_copy(weight_ref.at[at], out_ref, sems.at[index])
+        copy.start()
+        copies.append(copy)
+    for copy in copies:
+        copy.wait()
+
+
+def weight_strips(out_weight):
+    n, ctx = lax.axis_size("tp"), lax.axis_size("ctx")
+    shape = (out_weight.shape[0] // ctx, out_weight.shape[1] // n)
+    return pl.pallas_call(
+        strips_kernel,
+        out_shape=[jax.ShapeDtypeStruct(shape, out_weight.dtype)] * (n - 1),
+        in_specs=[pl.BlockSpec(memory_space=pl.ANY)],
+        out_specs=[pl.BlockSpec(memory_space=pltpu.VMEM)] * (n - 1),
+        scratch_shapes=[pltpu.SemaphoreType.DMA((n - 1,))],
+        compiler_params=pltpu.CompilerParams(vmem_limit_bytes=1 << 20),
+        name="weight_strips",
+    )(held_out(out_weight))
+
+
 def gather_weights(out_weight):
     n, ctx = lax.axis_size("tp"), lax.axis_size("ctx")
-    me, mine = lax.axis_index("tp"), lax.axis_index("ctx")
-    channels, columns = out_weight.shape[0], out_weight.shape[1] // n
-    rows = channels // ctx
-    strip = lax.dynamic_slice_in_dim(out_weight, mine * rows, rows, 0)
     pieces = []
+    cut = weight_strips(out_weight)
     for shift in range(1, n):
-        target = lax.rem(me + shift, n)
-        piece = lax.dynamic_slice_in_dim(strip, target * columns, columns, 1)
-        pieces.append(lax.ppermute(piece, "tp", [(i, (i + shift) % n) for i in range(n)]))
+        pieces.append(lax.ppermute(cut[shift - 1], "tp", [(i, i ^ shift) for i in range(n)]))
     held = jnp.stack(pieces)
     strips = {0: held}
     for other in range(ctx - 2, 0, -2):
@@ -234,7 +383,8 @@
     out_ref, matrix_ref, whole_ref, total_ref, result_ref, weight_sem, strip_sem, sent_sem, moved_sem, out_sem = refs
     columns = matrix_ref.shape[2]
     height = matrix_ref.shape[1] // ctx
-    width = sent[0].shape[1]
+    ends = [sum(ref.shape[1] for ref in sent[:part]) for part in range(parts)]
+    spots = [pl.ds(start, ref.shape[1]) for start, ref in zip(ends, sent)]
     me, mine = lax.axis_index("tp"), lax.axis_index("ctx")
 
     own = pltpu.make_async_copy(
@@ -243,7 +393,7 @@
     own.start()
     kept = []
     for part in range(parts):
-        copy = pltpu.make_async_copy(sent[part], whole_ref.at[0, :, pl.ds(part * width, width)], sent_sem.at[part])
+        copy = pltpu.make_async_copy(sent[part], whole_ref.at[0, :, spots[part]], sent_sem.at[part])
         copy.start()
         kept.append(copy)
     laid = []
@@ -251,20 +401,16 @@
     for shift in range(1, n):
         for part in range(parts):
             at = (shift - 1) * parts + part
-            target = whole_ref.at[shift, :, pl.ds(part * width, width)]
-
-            passed = me >= shift
-            sources = (
-                (passed & later, evens[at]),
-                (passed & jnp.logical_not(later), odds[at]),
-                (jnp.logical_not(passed) & later, odds[(n - shift - 1) * parts + part]),
-                (jnp.logical_not(passed) & jnp.logical_not(later), evens[(n - shift - 1) * parts + part]),
-            )
-            for taken, source in sources:
-
-                @pl.when(taken)
-                def _(at=at, source=source, target=target):
-                    pltpu.make_async_copy(source, target, moved_sem.at[at]).start()
+            target = whole_ref.at[shift, :, spots[part]]
+
+            away = jnp.bitwise_xor(me, shift) - me
+            for slot in range(1, n):
+                index = (slot - 1) * parts + part
+                for source, sign in ((evens[index], 1), (odds[index], -1)):
+
+                    @pl.when(away == jnp.where(later, -slot * sign, slot * sign))
+                    def _(at=at, source=source, target=target):
+                        pltpu.make_async_copy(source, target, moved_sem.at[at]).start()
 
         for other in range(ctx):
             row = pl.multiple_of(jnp.bitwise_xor(mine, other) * height, 16)
@@ -281,7 +427,7 @@
         else:
             for part in range(parts):
                 at = (shift - 1) * parts + part
-                target = whole_ref.at[shift, :, pl.ds(part * width, width)]
+                target = whole_ref.at[shift, :, spots[part]]
                 pltpu.make_async_copy(evens[at], target, moved_sem.at[at]).wait()
             for other in range(ctx):
                 laid[(shift - 1) * ctx + other].wait()
@@ -329,7 +475,7 @@
     )(held_out(out_weight), *operands[1:])
 
 
-def finish_kernel(part, unused_ref, product_ref, left_ref, right_ref, out_ref, result_ref, sem):
+def finish_kernel(first, unused_ref, product_ref, left_ref, right_ref, out_ref, result_ref, sem):
     height, width = left_ref.shape
     at = pl.ds(pl.multiple_of(lax.axis_index("tp") * width, 128), width)
 
@@ -343,17 +489,17 @@
         ).astype(jnp.bfloat16)
 
     copy = pltpu.make_async_copy(
-        result_ref, out_ref.at[pl.ds(out_ref.shape[0] - height, height), pl.ds(part * width, width)], sem
+        result_ref, out_ref.at[pl.ds(out_ref.shape[0] - height, height), pl.ds(first, width)], sem
     )
     copy.start()
     copy.wait()
 
 
-def finish(result, product, left, right, part):
+def finish(result, product, left, right, first):
     inside = pl.BlockSpec(memory_space=pltpu.VMEM)
     anywhere = pl.BlockSpec(memory_space=pl.ANY)
     return pl.pallas_call(
-        functools.partial(finish_kernel, part),
+        functools.partial(finish_kernel, first),
         out_shape=jax.ShapeDtypeStruct(result.shape, result.dtype),
         in_specs=[anywhere, inside, inside, inside],
         out_specs=anywhere,
@@ -401,32 +547,32 @@
     )(product, even, odd)
 
 
-def product_kernel(part, parts, rows_ref, weight_ref, out_ref, weight_buf, sems):
+def product_kernel(start, columns, rows_ref, weight_ref, out_ref, weight_buf, sems):
     count, _, width = weight_buf.shape
     copies = []
     for group in range(count):
         copy = pltpu.make_async_copy(
-            weight_ref.at[:, pl.ds((group * parts + part) * width, width)], weight_buf.at[group], sems.at[group]
+            weight_ref.at[:, pl.ds(group * columns + start, width)], weight_buf.at[group], sems.at[group]
         )
         copy.start()
         copies.append(copy)
     for group in range(count):
         copies[group].wait()
-        step = min(width, 256)
-        for first in range(0, width, step):
+        for first in range(0, width, 256):
+            step = min(width - first, 256)
             piece = jnp.dot(
                 rows_ref[...], weight_buf[group, :, first : first + step], preferred_element_type=jnp.float32
             )
             out_ref[:, group * width + first : group * width + first + step] = piece.astype(jnp.bfloat16)
 
 
-def local_product(rows, out_weight, part, parts):
+def local_product(rows, out_weight, start, width):
     n = lax.axis_size("tp")
     height, channels = rows.shape
-    width = out_weight.shape[1] // n // parts
+    columns = out_weight.shape[1] // n
     inside = pl.BlockSpec(memory_space=pltpu.VMEM)
     return pl.pallas_call(
-        functools.partial(product_kernel, part, parts),
+        functools.partial(product_kernel, start, columns),
         out_shape=jax.ShapeDtypeStruct((height, n * width), jnp.bfloat16),
         in_specs=[inside, pl.BlockSpec(memory_space=pl.ANY)],
         out_specs=inside,
@@ -457,26 +603,30 @@
     n, ctx = lax.axis_size("tp"), lax.axis_size("ctx")
     tokens, channels = queries.shape
     spans = span_order.shape[0] // ctx
-    lined = channels // ctx >= 128 and spans == 2 and ctx & (ctx - 1) == 0
+    lined = channels // ctx >= 128 and spans == 2 and ctx & (ctx - 1) == 0 and n & (n - 1) == 0
     totals, gated = span_states(keys, values, rates, spans)
     strips = gather_weights(out_weight) if lined else None
     states = exchange_states(totals) if lined else [lax.all_gather(totals, "ctx", axis=0, tiled=True)]
     conv = functools.partial(convolve, span_order, queries, gated, residues, rates, states, spans)
     if not lined:
-        outputs = [conv(span, 0, 1) for span in range(spans)]
+        outputs = [conv(span, 0, channels) for span in range(spans)]
         part = jnp.dot(jnp.concatenate(outputs), out_weight, preferred_element_type=jnp.float32)
         return lax.psum_scatter(part.astype(jnp.bfloat16), "tp", scatter_dimension=1, tiled=True)
+    lead = channels // 128 * FIRST // 8 * 128
+    spots = [(0, lead), (lead, channels - lead)]
     sent, products = [], []
-    for part in range(PARTS):
-        sent.append(conv(0, part, PARTS))
-    rest = conv(1, 0, 1)
-    for part in range(PARTS):
-        products.append(local_product(rest, out_weight, part, PARTS))
+    response = span_response(gated, residues, rates, spans, 0, *spots[0])
+    sent.append(complete(span_order, queries, response, residues, rates, states, spans, 0, spots[0][0]))
+    for part in range(1, PARTS):
+        sent.append(conv(0, *spots[part]))
+    rest = conv(1, 0, channels)
+    for part, spot in enumerate(spots):
+        products.append(local_product(rest, out_weight, *spot))
     evens, odds = exchange(sent, products)
     arrived = [[side[slot, part] for slot in range(1, n) for part in range(PARTS)] for side in (evens, odds)]
     result = upper(out_weight, strips, sent, *arrived, tokens)
     for part in range(PARTS):
-        result = finish(result, products[part], evens[n, part], odds[n, part], part)
+        result = finish(result, products[part], evens[n, part], odds[n, part], spots[part][0])
     return result
 
 

time: 180 us -> 172 us (0.956)
  the two profiles are of different devices: /device:TPU:10 before, /device:TPU:0 now
where the time goes in v5:
time: 172 us; the launch traced here: 170 us
  waiting for transfers between devices  62 us (36%)
  starting transfers between devices  60.1 us (35%)
  Pallas kernels  47.3 us (28%)
    ppermute x8, starting transfers between devices, exchange(): evens[slot, part] = lax.ppermute(even, 'tp', pairs[0])  40.9 us
    ppermute x3, waiting for transfers between devices, gather_weights(): lax.ppermute(cut[shift - 1], 'tp', [(i, i ^ shift) for i in range(n)])  28.5 us
    ppermute x3, waiting for transfers between devices, gather_weights(): lax.ppermute(held, 'ctx', [(i, i ^ other) for i in range(ctx)])  21.9 us
    pallas_call x2, Pallas kernels, convolve(): pl.pallas_call(functools.partial(convolve_kernel, span, spans, first, len...  11.6 us
    pallas_call x1, Pallas kernels, upper(): pl.pallas_call(functools.partial(upper_kernel, n, ctx, parts), out_shape=...  10.2 us
    pallas_call x1, Pallas kernels, span_states(): pl.pallas_call(functools.partial(states_kernel, spans), out_shape=[jax.Sh...  8.14 us
    pallas_call x2, Pallas kernels, local_product(): pl.pallas_call(functools.partial(product_kernel, start, columns), out_sha...  7.16 us
    ppermute x3, waiting for transfers between devices, exchange_states(): lax.ppermute(totals, 'ctx', [(i, i ^ other) for i in range(ctx)])  6.19 us
  transfers between devices with their start and end apart: 30, of which 8 were waited for; matrix products, arithmetic and copies ran while one was open for 0% of the time, Pallas kernels for 21%

profile of v5, /device:TPU:0, one launch (start us, length us, event | category | flops | bytes accessed | tf_op | source)
XLA Modules:
  0.0 169.9 jit_solution(14429278790746392397)
XLA Ops:
  0.0 8.1 %span_states.1 = (f32[2,16,1024]{2,1,0:T(8,128)S(1)}, bf16[1024,1024]{1,0:T(8,128)(2,1)S(1)}) custom-call(bf16[1024,1024]{1,0:T(8,128)(2,1)} %keys_ref.1, bf16[1024,1024]{1,0:T(8,128)(2,1)} %values_ref.1, f32[16,1024]{1,0:T(8,128)} %rates_ref.7), custom_call_target="tpu_custom_call" | custom-call | tf_op jit(solution)/shard_map/span_states/pallas_call | solution.py:79
  8.2 3.0 %collective-permute-start.10 = (f32[2,16,1024]{2,1,0:T(8,128)S(1)}, f32[2,16,1024]{2,1,0:T(8,128)S(1)}, u32[]{:S(2)}, u32[]{:S(2)}) collective-permute-start(f32[2,16,1024]{2,1,0:T(8,128)S(1)} %get-tuple-element.26), channel_id=1, source_target_pairs={{0,8},{4,12},{8,0},{12,4},{16,24},{20,28},{24,16},{28,20},{1,9},{5... | collective-permute-start | bytes 393224 | tf_op jit(solution)/shard_map/ppermute | solution.py:328
  12.8 2.3 %collective-permute-done.10 = f32[2,16,1024]{2,1,0:T(8,128)S(1)} collective-permute-done((f32[2,16,1024]{2,1,0:T(8,128)S(1)}, f32[2,16,1024]{2,1,0:T(8,128)S(1)}, u32[]{:S(2)}, u32[]{:S(2)}) %collective-permute-start.10) | collective-permute-done | bytes 131104 | tf_op jit(solution)/shard_map/ppermute | solution.py:328
  15.1 3.9 %collective-permute-done.11 = f32[2,16,1024]{2,1,0:T(8,128)S(1)} collective-permute-done((f32[2,16,1024]{2,1,0:T(8,128)S(1)}, f32[2,16,1024]{2,1,0:T(8,128)S(1)}, u32[]{:S(2)}, u32[]{:S(2)}) %collective-permute-start.11) | collective-permute-done | bytes 131104 | tf_op jit(solution)/shard_map/ppermute | solution.py:328
  19.1 3.2 %span_response.1.response_ref = f32[512,512]{1,0:T(8,128)S(1)} custom-call(bf16[1024,1024]{1,0:T(8,128)(2,1)S(1)} %get-tuple-element.25.gated_ref, f32[16,1024]{1,0:T(8,128)S(1)} %copy-done.2, f32[16,1024]{1,0:T(8,128)S(1)} %copy-done.1), custom_call_target="tpu_custom_call" | custom-call | tf_op jit(solution)/shard_map/span_response/pallas_call | solution.py:236
  22.3 2.8 %complete.1.refs_9_ = bf16[512,512]{1,0:T(8,128)(2,1)S(1)} custom-call(s32[16]{0:T(128)S(1)} %copy-done.3, bf16[1024,1024]{1,0:T(8,128)(2,1)S(1)} %copy-done, f32[512,512]{1,0:T(8,128)S(1)} %span_response.1.response_ref, f32[16,1024]{1,0:T(8,128)S(1)} %copy-done.2, f32[16,1024]{1,0:T(8,128)S(1)} %copy-done.1, ...), custom_call_target="tpu_custom_call" | custom-call | tf_op jit(solution)/shard_map/complete/pallas_call | solution.py:302
  25.2 1.6 collective-permute-start.14
  27.5 4.0 %convolve.2.refs_10_ = bf16[512,512]{1,0:T(8,128)(2,1)S(1)} custom-call(s32[16]{0:T(128)S(1)} %copy-done.3, bf16[1024,1024]{1,0:T(8,128)(2,1)S(1)} %copy-done, bf16[1024,1024]{1,0:T(8,128)(2,1)S(1)} %get-tuple-element.25.gated_ref, f32[16,1024]{1,0:T(8,128)S(1)} %copy-done.2, f32[16,1024]{1,0:T(8,128)S(1)} %copy-done.1, ...), custom_call_target="tpu_custom_call" | custom-call | tf_op jit(solution)/shard_map/convolve/pallas_call | solution.py:190
  31.6 4.4 %collective-permute-start.15 = (bf16[512,512]{1,0:T(8,128)(2,1)S(1)}, bf16[512,512]{1,0:T(8,128)(2,1)S(1)}, u32[]{:S(2)}, u32[]{:S(2)}) collective-permute-start(bf16[512,512]{1,0:T(8,128)(2,1)S(1)} %convolve.2.refs_10_), channel_id=1, source_target_pairs={{0,1},{1,0},{2,3},{3,2},{4,5},{5,4},{6,7},{7,6},{8,9},{9,8},{10,11... | collective-permute-start | bytes 1572872 | tf_op jit(solution)/shard_map/ppermute | solution.py:597
  37.9 7.6 %convolve.3.rows_ref = bf16[512,1024]{1,0:T(8,128)(2,1)S(1)} custom-call(s32[16]{0:T(128)S(1)} %copy-done.3, bf16[1024,1024]{1,0:T(8,128)(2,1)S(1)} %copy-done, bf16[1024,1024]{1,0:T(8,128)(2,1)S(1)} %get-tuple-element.25.gated_ref, f32[16,1024]{1,0:T(8,128)S(1)} %copy-done.2, f32[16,1024]{1,0:T(8,128)S(1)} %copy-done.1, ...), custom_call_target="tpu_custom_call" | custom-call | tf_op jit(solution)/shard_map/convolve/pallas_call | solution.py:190
  45.5 3.6 %local_product.2.product_ref = bf16[512,2048]{1,0:T(8,128)(2,1)S(1)} custom-call(bf16[512,1024]{1,0:T(8,128)(2,1)S(1)} %convolve.3.rows_ref, bf16[1024,4096]{1,0:T(8,128)(2,1)S(1)} %bitcast.4), custom_call_target="tpu_custom_call" | custom-call | tf_op jit(solution)/shard_map/local_product/pallas_call | solution.py:574
  49.3 1.5 collective-permute-start.17
  50.8 2.9 %collective-permute-start.2 = (bf16[128,1024]{1,0:T(8,128)(2,1)S(1)}, bf16[128,1024]{1,0:T(8,128)(2,1)S(1)}, u32[]{:S(2)}, u32[]{:S(2)}) collective-permute-start(bf16[128,1024]{1,0:T(8,128)(2,1)S(1)} %get-tuple-element.24), channel_id=1, source_target_pairs={{0,3},{1,2},{2,1},{3,0},{4,7},{5,6},{6,5},{7,4},{8,11},{9,10},{10,... | collective-permute-start | bytes 786440 | tf_op jit(solution)/shard_map/ppermute | solution.py:368
  54.4 1.9 %collective-permute-start.1 = (bf16[128,1024]{1,0:T(8,128)(2,1)S(1)}, bf16[128,1024]{1,0:T(8,128)(2,1)S(1)}, u32[]{:S(2)}, u32[]{:S(2)}) collective-permute-start(bf16[128,1024]{1,0:T(8,128)(2,1)S(1)} %get-tuple-element.23), channel_id=1, source_target_pairs={{0,2},{1,3},{2,0},{3,1},{4,6},{5,7},{6,4},{7,5},{8,10},{9,11},{10,... | collective-permute-start | bytes 786440 | tf_op jit(solution)/shard_map/ppermute | solution.py:368
  56.4 3.6 %local_product.3.product_ref = bf16[512,2048]{1,0:T(8,128)(2,1)S(1)} custom-call(bf16[512,1024]{1,0:T(8,128)(2,1)S(1)} %convolve.3.rows_ref, bf16[1024,4096]{1,0:T(8,128)(2,1)S(1)} %bitcast.4), custom_call_target="tpu_custom_call" | custom-call | tf_op jit(solution)/shard_map/local_product/pallas_call | solution.py:574
  60.1 12.1 %collective-permute-done.2 = bf16[128,1024]{1,0:T(8,128)(2,1)S(1)} collective-permute-done((bf16[128,1024]{1,0:T(8,128)(2,1)S(1)}, bf16[128,1024]{1,0:T(8,128)(2,1)S(1)}, u32[]{:S(2)}, u32[]{:S(2)}) %collective-permute-start.2) | collective-permute-done | bytes 262176 | tf_op jit(solution)/shard_map/ppermute | solution.py:368
  72.2 16.4 %collective-permute-done.1 = bf16[128,1024]{1,0:T(8,128)(2,1)S(1)} collective-permute-done((bf16[128,1024]{1,0:T(8,128)(2,1)S(1)}, bf16[128,1024]{1,0:T(8,128)(2,1)S(1)}, u32[]{:S(2)}, u32[]{:S(2)}) %collective-permute-start.1) | collective-permute-done | bytes 262176 | tf_op jit(solution)/shard_map/ppermute | solution.py:368
  94.6 9.0 %collective-permute-start.23 = (bf16[512,512]{1,0:T(8,128)(2,1)S(1)}, bf16[512,512]{1,0:T(8,128)(2,1)S(1)}, u32[]{:S(2)}, u32[]{:S(2)}) collective-permute-start(bf16[512,512]{1,0:T(8,128)(2,1)S(1)} %get-tuple-element.32), channel_id=1, source_target_pairs={{0,1},{1,0},{2,3},{3,2},{4,5},{5,4},{6,7},{7,6},{8,9},{9,8},{10,11... | collective-permute-start | bytes 1572872 | tf_op jit(solution)/shard_map/ppermute | solution.py:597
  103.7 6.2 %collective-permute-done.4.refs_3_ = bf16[3,128,1024]{2,1,0:T(8,128)(2,1)S(1)} collective-permute-done((bf16[3,128,1024]{2,1,0:T(8,128)(2,1)S(1)}, bf16[3,128,1024]{2,1,0:T(8,128)(2,1)S(1)}, u32[]{:S(2)}, u32[]{:S(2)}) %collective-permute-start.4) | collective-permute-done | bytes 786464 | tf_op jit(solution)/shard_map/ppermute | solution.py:372
  109.9 14.8 %collective-permute-done.6.refs_5_ = bf16[3,128,1024]{2,1,0:T(8,128)(2,1)S(1)} collective-permute-done((bf16[3,128,1024]{2,1,0:T(8,128)(2,1)S(1)}, bf16[3,128,1024]{2,1,0:T(8,128)(2,1)S(1)}, u32[]{:S(2)}, u32[]{:S(2)}) %collective-permute-start.6) | collective-permute-done | bytes 786464 | tf_op jit(solution)/shard_map/ppermute | solution.py:372
  127.8 20.2 %collective-permute-start.26 = (bf16[512,512]{1,0:T(8,128)(2,1)S(1)}, bf16[512,512]{1,0:T(8,128)(2,1)S(1)}, u32[]{:S(2)}, u32[]{:S(2)}) collective-permute-start(bf16[512,512]{1,0:T(8,128)(2,1)S(1)} %get-tuple-element.35), channel_id=1, source_target_pairs={{0,1},{1,0},{2,3},{3,2},{4,5},{5,4},{6,7},{7,6},{8,9},{9,8},{10,11... | collective-permute-start | bytes 1572872 | tf_op jit(solution)/shard_map/ppermute | solution.py:597
  148.9 2.8 %collective-permute-start.28 = (bf16[512,512]{1,0:T(8,128)(2,1)S(1)}, bf16[512,512]{1,0:T(8,128)(2,1)S(1)}, u32[]{:S(2)}, u32[]{:S(2)}) collective-permute-start(bf16[512,512]{1,0:T(8,128)(2,1)S(1)} %get-tuple-element.37), channel_id=1, source_target_pairs={{0,1},{1,0},{2,3},{3,2},{4,5},{5,4},{6,7},{7,6},{8,9},{9,8},{10,11... | collective-permute-start | bytes 1572872 | tf_op jit(solution)/shard_map/ppermute | solution.py:597
  152.4 10.2 %upper.1.unused_ref = bf16[1024,1024]{1,0:T(8,128)(2,1)} custom-call(bf16[1024,4096]{1,0:T(8,128)(2,1)} %refs_0_.1, bf16[3,128,1024]{2,1,0:T(8,128)(2,1)S(1)} %pad_maximum_fusion.refs_1_, bf16[3,128,1024]{2,1,0:T(8,128)(2,1)S(1)} %collective-permute-done.3.refs_2_, bf16[3,128,1024]{2,1,0:T(8,128)(2,1)S(1)} %collective-permute-done.4.refs_3_, ...), custom_call_target="tpu_custom_call" | custom-call | tf_op jit(solution)/shard_map/upper/pallas_call | solution.py:457
  163.6 5.3 %collective-permute-done.28.left_ref = bf16[512,512]{1,0:T(8,128)(2,1)S(1)} collective-permute-done((bf16[512,512]{1,0:T(8,128)(2,1)S(1)}, bf16[512,512]{1,0:T(8,128)(2,1)S(1)}, u32[]{:S(2)}, u32[]{:S(2)}) %collective-permute-start.28) | collective-permute-done | bytes 524320 | tf_op jit(solution)/shard_map/ppermute | solution.py:597
  (71 shorter events, 17.9 us)
Async XLA Ops:
  11.2 7.8 %collective-permute-start.11 = (f32[2,16,1024]{2,1,0:T(8,128)S(1)}, f32[2,16,1024]{2,1,0:T(8,128)S(1)}, u32[]{:S(2)}, u32[]{:S(2)}) collective-permute-start(f32[2,16,1024]{2,1,0:T(8,128)S(1)} %get-tuple-element.26), channel_id=1, source_target_pairs={{0,16},{4,20},{8,24},{12,28},{16,0},{20,4},{24,8},{28,12},{1,17},{... | collective-permute-start | bytes 393224 | tf_op jit(solution)/shard_map/ppermute | solution.py:328
  25.2 23.9 %collective-permute-start.14 = (bf16[512,512]{1,0:T(8,128)(2,1)S(1)}, bf16[512,512]{1,0:T(8,128)(2,1)S(1)}, u32[]{:S(2)}, u32[]{:S(2)}) collective-permute-start(bf16[512,512]{1,0:T(8,128)(2,1)S(1)} %complete.1.refs_9_), channel_id=1, source_target_pairs={{0,1},{1,0},{2,3},{3,2},{4,5},{5,4},{6,7},{7,6},{8,9},{9,8},{10,11... | collective-permute-start | bytes 1572872 | tf_op jit(solution)/shard_map/ppermute | solution.py:597
  26.8 22.3 %collective-permute-start.16 = (bf16[512,512]{1,0:T(8,128)(2,1)S(1)}, bf16[512,512]{1,0:T(8,128)(2,1)S(1)}, u32[]{:S(2)}, u32[]{:S(2)}) collective-permute-start(bf16[512,512]{1,0:T(8,128)(2,1)S(1)} %complete.1.refs_9_), channel_id=1, source_target_pairs={{1,2},{2,1},{5,6},{6,5},{9,10},{10,9},{13,14},{14,13},{17,18},{18,... | collective-permute-start | bytes 1572872 | tf_op jit(solution)/shard_map/ppermute | solution.py:598
  31.6 22.8 %collective-permute-start.15 = (bf16[512,512]{1,0:T(8,128)(2,1)S(1)}, bf16[512,512]{1,0:T(8,128)(2,1)S(1)}, u32[]{:S(2)}, u32[]{:S(2)}) collective-permute-start(bf16[512,512]{1,0:T(8,128)(2,1)S(1)} %convolve.2.refs_10_), channel_id=1, source_target_pairs={{0,1},{1,0},{2,3},{3,2},{4,5},{5,4},{6,7},{7,6},{8,9},{9,8},{10,11... | collective-permute-start | bytes 1572872 | tf_op jit(solution)/shard_map/ppermute | solution.py:597
  36.0 20.3 %collective-permute-start.18 = (bf16[512,512]{1,0:T(8,128)(2,1)S(1)}, bf16[512,512]{1,0:T(8,128)(2,1)S(1)}, u32[]{:S(2)}, u32[]{:S(2)}) collective-permute-start(bf16[512,512]{1,0:T(8,128)(2,1)S(1)} %convolve.2.refs_10_), channel_id=1, source_target_pairs={{1,2},{2,1},{5,6},{6,5},{9,10},{10,9},{13,14},{14,13},{17,18},{18,... | collective-permute-start | bytes 1572872 | tf_op jit(solution)/shard_map/ppermute | solution.py:598
  49.3 41.4 %collective-permute-start.17 = (bf16[512,512]{1,0:T(8,128)(2,1)S(1)}, bf16[512,512]{1,0:T(8,128)(2,1)S(1)}, u32[]{:S(2)}, u32[]{:S(2)}) collective-permute-start(bf16[512,512]{1,0:T(8,128)(2,1)S(1)} %get-tuple-element.27), channel_id=1, source_target_pairs={{0,1},{1,0},{2,3},{3,2},{4,5},{5,4},{6,7},{7,6},{8,9},{9,8},{10,11... | collective-permute-start | bytes 1572872 | tf_op jit(solution)/shard_map/ppermute | solution.py:597
  50.8 21.4 %collective-permute-start.2 = (bf16[128,1024]{1,0:T(8,128)(2,1)S(1)}, bf16[128,1024]{1,0:T(8,128)(2,1)S(1)}, u32[]{:S(2)}, u32[]{:S(2)}) collective-permute-start(bf16[128,1024]{1,0:T(8,128)(2,1)S(1)} %get-tuple-element.24), channel_id=1, source_target_pairs={{0,3},{1,2},{2,1},{3,0},{4,7},{5,6},{6,5},{7,4},{8,11},{9,10},{10,... | collective-permute-start | bytes 786440 | tf_op jit(solution)/shard_map/ppermute | solution.py:368
  53.7 37.8 %collective-permute-start.20 = (bf16[512,512]{1,0:T(8,128)(2,1)S(1)}, bf16[512,512]{1,0:T(8,128)(2,1)S(1)}, u32[]{:S(2)}, u32[]{:S(2)}) collective-permute-start(bf16[512,512]{1,0:T(8,128)(2,1)S(1)} %get-tuple-element.29), channel_id=1, source_target_pairs={{1,2},{2,1},{5,6},{6,5},{9,10},{10,9},{13,14},{14,13},{17,18},{18,... | collective-permute-start | bytes 1572872 | tf_op jit(solution)/shard_map/ppermute | solution.py:598
  54.4 34.2 %collective-permute-start.1 = (bf16[128,1024]{1,0:T(8,128)(2,1)S(1)}, bf16[128,1024]{1,0:T(8,128)(2,1)S(1)}, u32[]{:S(2)}, u32[]{:S(2)}) collective-permute-start(bf16[128,1024]{1,0:T(8,128)(2,1)S(1)} %get-tuple-element.23), channel_id=1, source_target_pairs={{0,2},{1,3},{2,0},{3,1},{4,6},{5,7},{6,4},{7,5},{8,10},{9,11},{10,... | collective-permute-start | bytes 786440 | tf_op jit(solution)/shard_map/ppermute | solution.py:368
  56.4 33.0 %collective-permute-start = (bf16[128,1024]{1,0:T(8,128)(2,1)S(1)}, bf16[128,1024]{1,0:T(8,128)(2,1)S(1)}, u32[]{:S(2)}, u32[]{:S(2)}) collective-permute-start(bf16[128,1024]{1,0:T(8,128)(2,1)S(1)} %get-tuple-element.22), channel_id=1, source_target_pairs={{0,1},{1,0},{2,3},{3,2},{4,5},{5,4},{6,7},{7,6},{8,9},{9,8},{10,11... | collective-permute-start | bytes 786440 | tf_op jit(solution)/shard_map/ppermute | solution.py:368
  72.2 20.9 %collective-permute-start.19 = (bf16[512,512]{1,0:T(8,128)(2,1)S(1)}, bf16[512,512]{1,0:T(8,128)(2,1)S(1)}, u32[]{:S(2)}, u32[]{:S(2)}) collective-permute-start(bf16[512,512]{1,0:T(8,128)(2,1)S(1)} %get-tuple-element.28), channel_id=1, source_target_pairs={{0,1},{1,0},{2,3},{3,2},{4,5},{5,4},{6,7},{7,6},{8,9},{9,8},{10,11... | collective-permute-start | bytes 1572872 | tf_op jit(solution)/shard_map/ppermute | solution.py:597
  89.4 20.5 %collective-permute-start.4 = (bf16[3,128,1024]{2,1,0:T(8,128)(2,1)S(1)}, bf16[3,128,1024]{2,1,0:T(8,128)(2,1)S(1)}, u32[]{:S(2)}, u32[]{:S(2)}) collective-permute-start(bf16[3,128,1024]{2,1,0:T(8,128)(2,1)S(1)} %pad_maximum_fusion.refs_1_), channel_id=1, source_target_pairs={{0,8},{4,12},{8,0},{12,4},{16,24},{20,28},{24,16},{28,20},{1,9},{5... | collective-permute-start | bytes 2359304 | tf_op jit(solution)/shard_map/ppermute | solution.py:372
  90.7 34.0 %collective-permute-start.6 = (bf16[3,128,1024]{2,1,0:T(8,128)(2,1)S(1)}, bf16[3,128,1024]{2,1,0:T(8,128)(2,1)S(1)}, u32[]{:S(2)}, u32[]{:S(2)}) collective-permute-start(bf16[3,128,1024]{2,1,0:T(8,128)(2,1)S(1)} %pad_maximum_fusion.refs_1_), channel_id=1, source_target_pairs={{0,16},{4,20},{8,24},{12,28},{16,0},{20,4},{24,8},{28,12},{1,17},{... | collective-permute-start | bytes 2359304 | tf_op jit(solution)/shard_map/ppermute | solution.py:372
  91.6 34.8 %collective-permute-start.8 = (bf16[3,128,1024]{2,1,0:T(8,128)(2,1)S(1)}, bf16[3,128,1024]{2,1,0:T(8,128)(2,1)S(1)}, u32[]{:S(2)}, u32[]{:S(2)}) collective-permute-start(bf16[3,128,1024]{2,1,0:T(8,128)(2,1)S(1)} %pad_maximum_fusion.refs_1_), channel_id=1, source_target_pairs={{0,24},{4,28},{8,16},{12,20},{16,8},{20,12},{24,0},{28,4},{1,25},{... | collective-permute-start | bytes 2359304 | tf_op jit(solution)/shard_map/ppermute | solution.py:372
  93.2 33.2 %collective-permute-start.21 = (bf16[512,512]{1,0:T(8,128)(2,1)S(1)}, bf16[512,512]{1,0:T(8,128)(2,1)S(1)}, u32[]{:S(2)}, u32[]{:S(2)}) collective-permute-start(bf16[512,512]{1,0:T(8,128)(2,1)S(1)} %get-tuple-element.30), channel_id=1, source_target_pairs={{0,1},{1,0},{2,3},{3,2},{4,5},{5,4},{6,7},{7,6},{8,9},{9,8},{10,11... | collective-permute-start | bytes 1572872 | tf_op jit(solution)/shard_map/ppermute | solution.py:597
  94.6 32.2 %collective-permute-start.23 = (bf16[512,512]{1,0:T(8,128)(2,1)S(1)}, bf16[512,512]{1,0:T(8,128)(2,1)S(1)}, u32[]{:S(2)}, u32[]{:S(2)}) collective-permute-start(bf16[512,512]{1,0:T(8,128)(2,1)S(1)} %get-tuple-element.32), channel_id=1, source_target_pairs={{0,1},{1,0},{2,3},{3,2},{4,5},{5,4},{6,7},{7,6},{8,9},{9,8},{10,11... | collective-permute-start | bytes 1572872 | tf_op jit(solution)/shard_map/ppermute | solution.py:597
  109.9 38.3 %collective-permute-start.3 = (bf16[3,128,1024]{2,1,0:T(8,128)(2,1)S(1)}, bf16[3,128,1024]{2,1,0:T(8,128)(2,1)S(1)}, u32[]{:S(2)}, u32[]{:S(2)}) collective-permute-start(bf16[3,128,1024]{2,1,0:T(8,128)(2,1)S(1)} %pad_maximum_fusion.refs_1_), channel_id=1, source_target_pairs={{0,4},{4,0},{8,12},{12,8},{16,20},{20,16},{24,28},{28,24},{1,5},{5... | collective-permute-start | bytes 2359304 | tf_op jit(solution)/shard_map/ppermute | solution.py:374
  126.3 22.6 %collective-permute-start.5 = (bf16[3,128,1024]{2,1,0:T(8,128)(2,1)S(1)}, bf16[3,128,1024]{2,1,0:T(8,128)(2,1)S(1)}, u32[]{:S(2)}, u32[]{:S(2)}) collective-permute-start(bf16[3,128,1024]{2,1,0:T(8,128)(2,1)S(1)} %collective-permute-done.4.refs_3_), channel_id=1, source_target_pairs={{0,4},{4,0},{8,12},{12,8},{16,20},{20,16},{24,28},{28,24},{1,5},{5... | collective-permute-start | bytes 2359304 | tf_op jit(solution)/shard_map/ppermute | solution.py:374
  126.3 25.4 %collective-permute-start.7 = (bf16[3,128,1024]{2,1,0:T(8,128)(2,1)S(1)}, bf16[3,128,1024]{2,1,0:T(8,128)(2,1)S(1)}, u32[]{:S(2)}, u32[]{:S(2)}) collective-permute-start(bf16[3,128,1024]{2,1,0:T(8,128)(2,1)S(1)} %collective-permute-done.6.refs_5_), channel_id=1, source_target_pairs={{0,4},{4,0},{8,12},{12,8},{16,20},{20,16},{24,28},{28,24},{1,5},{5... | collective-permute-start | bytes 2359304 | tf_op jit(solution)/shard_map/ppermute | solution.py:374
  127.5 24.8 %collective-permute-start.9 = (bf16[3,128,1024]{2,1,0:T(8,128)(2,1)S(1)}, bf16[3,128,1024]{2,1,0:T(8,128)(2,1)S(1)}, u32[]{:S(2)}, u32[]{:S(2)}) collective-permute-start(bf16[3,128,1024]{2,1,0:T(8,128)(2,1)S(1)} %collective-permute-done.8.refs_7_), channel_id=1, source_target_pairs={{0,4},{4,0},{8,12},{12,8},{16,20},{20,16},{24,28},{28,24},{1,5},{5... | collective-permute-start | bytes 2359304 | tf_op jit(solution)/shard_map/ppermute | solution.py:374
  127.8 34.8 %collective-permute-start.26 = (bf16[512,512]{1,0:T(8,128)(2,1)S(1)}, bf16[512,512]{1,0:T(8,128)(2,1)S(1)}, u32[]{:S(2)}, u32[]{:S(2)}) collective-permute-start(bf16[512,512]{1,0:T(8,128)(2,1)S(1)} %get-tuple-element.35), channel_id=1, source_target_pairs={{0,1},{1,0},{2,3},{3,2},{4,5},{5,4},{6,7},{7,6},{8,9},{9,8},{10,11... | collective-permute-start | bytes 1572872 | tf_op jit(solution)/shard_map/ppermute | solution.py:597
  148.2 14.4 %collective-permute-start.27 = (bf16[512,512]{1,0:T(8,128)(2,1)S(1)}, bf16[512,512]{1,0:T(8,128)(2,1)S(1)}, u32[]{:S(2)}, u32[]{:S(2)}) collective-permute-start(bf16[512,512]{1,0:T(8,128)(2,1)S(1)} %get-tuple-element.36), channel_id=1, source_target_pairs={{1,2},{2,1},{5,6},{6,5},{9,10},{10,9},{13,14},{14,13},{17,18},{18,... | collective-permute-start | bytes 1572872 | tf_op jit(solution)/shard_map/ppermute | solution.py:598
  148.9 20.0 %collective-permute-start.28 = (bf16[512,512]{1,0:T(8,128)(2,1)S(1)}, bf16[512,512]{1,0:T(8,128)(2,1)S(1)}, u32[]{:S(2)}, u32[]{:S(2)}) collective-permute-start(bf16[512,512]{1,0:T(8,128)(2,1)S(1)} %get-tuple-element.37), channel_id=1, source_target_pairs={{0,1},{1,0},{2,3},{3,2},{4,5},{5,4},{6,7},{7,6},{8,9},{9,8},{10,11... | collective-permute-start | bytes 1572872 | tf_op jit(solution)/shard_map/ppermute | solution.py:597
  151.7 17.2 %collective-permute-start.29 = (bf16[512,512]{1,0:T(8,128)(2,1)S(1)}, bf16[512,512]{1,0:T(8,128)(2,1)S(1)}, u32[]{:S(2)}, u32[]{:S(2)}) collective-permute-start(bf16[512,512]{1,0:T(8,128)(2,1)S(1)} %get-tuple-element.38), channel_id=1, source_target_pairs={{1,2},{2,1},{5,6},{6,5},{9,10},{10,9},{13,14},{14,13},{17,18},{18,... | collective-permute-start | bytes 1572872 | tf_op jit(solution)/shard_map/ppermute | solution.py:598
  (12 other events, 115.3 us)

commit v6 on v5

--- a/solution.py
+++ b/solution.py
@@ -41,31 +41,40 @@
             copy.start()
         copies.append(pair)
     table.wait()
-    for index, (span, first) in enumerate(groups):
-        for copy in copies[index]:
-            copy.wait()
-        across = pl.ds(first, lanes)
+    sent = []
+    for start in range(0, len(groups), spans):
+        across = pl.ds(groups[start][1], lanes)
         decay = jnp.exp(-rates_ref[:, across])
-
-        def body(step, state, index=index, span=span, across=across, decay=decay):
+        for index in range(start, start + spans):
+            for copy in copies[index]:
+                copy.wait()
+
+        def body(step, states, start=start, decay=decay):
             base = pl.multiple_of(step * ROWS, ROWS)
             rows = pl.ds(base, ROWS)
-            keys = keys_buf[index, rows, :].astype(jnp.float32)
-            gated = (keys * values_buf[index, rows, :].astype(jnp.float32)).astype(jnp.bfloat16)
-            gated_buf[index, rows, :] = gated
-            rows_buf[rows, :] = gated.astype(jnp.float32)
+            for span in range(spans):
+                keys = keys_buf[start + span, rows, :].astype(jnp.float32)
+                gated = (keys * values_buf[start + span, rows, :].astype(jnp.float32)).astype(jnp.bfloat16)
+                gated_buf[start + span, rows, :] = gated
+                rows_buf[span, rows, :] = gated.astype(jnp.float32)
             for row in range(ROWS):
-                state = decay * state + rows_buf[pl.ds(base + row, 1), :]
-            return state
-
-        zero = jnp.zeros(decay.shape, jnp.float32)
-        out_ref[span, :, across] = lax.fori_loop(0, length // ROWS, body, zero, unroll=DEPTH)
-        copy = pltpu.make_async_copy(
-            gated_buf.at[index], gated_ref.at[pl.ds(span * length, length), across], sems.at[2, index]
-        )
-        copy.start()
-        copies[index] = copy
-    for copy in copies:
+                states = tuple(
+                    decay * state + rows_buf[span, pl.ds(base + row, 1), :] for span, state in enumerate(states)
+                )
+            return states
+
+        zeros = tuple(jnp.zeros(decay.shape, jnp.float32) for _ in range(spans))
+        finals = lax.fori_loop(0, length // ROWS, body, zeros, unroll=DEPTH)
+        for span in range(spans):
+            out_ref[span, :, across] = finals[span]
+            copy = pltpu.make_async_copy(
+                gated_buf.at[start + span],
+                gated_ref.at[pl.ds(span * length, length), across],
+                sems.at[2, start + span],
+            )
+            copy.start()
+            sent.append(copy)
+    for copy in sent:
         copy.wait()
 
 
@@ -89,11 +98,11 @@
             pltpu.VMEM((count, length, lanes), jnp.bfloat16),
             pltpu.VMEM((count, length, lanes), jnp.bfloat16),
             pltpu.VMEM((count, length, lanes), jnp.bfloat16),
-            pltpu.VMEM((length, lanes), jnp.float32),
+            pltpu.VMEM((spans, length, lanes), jnp.float32),
             pltpu.SemaphoreType.DMA((3, count)),
             pltpu.SemaphoreType.DMA(()),
         ],
-        compiler_params=pltpu.CompilerParams(vmem_limit_bytes=8 << 20),
+        compiler_params=pltpu.CompilerParams(vmem_limit_bytes=10 << 20),
         name="span_states",
     )(held_out(keys), held_out(values), held_out(rates))
 

time: 172 us -> 172 us (level)
  no operation moved by 1% of the time
where the time goes in v6:
time: 172 us; the launch traced here: 170 us
  waiting for transfers between devices  62 us (36%)
  starting transfers between devices  60.1 us (35%)
  Pallas kernels  47 us (27%)
    ppermute x8, starting transfers between devices, exchange(): evens[slot, part] = lax.ppermute(even, 'tp', pairs[0])  41 us
    ppermute x3, waiting for transfers between devices, gather_weights(): lax.ppermute(cut[shift - 1], 'tp', [(i, i ^ shift) for i in range(n)])  28.5 us
    ppermute x3, waiting for transfers between devices, gather_weights(): lax.ppermute(held, 'ctx', [(i, i ^ other) for i in range(ctx)])  21.9 us
    pallas_call x2, Pallas kernels, convolve(): pl.pallas_call(functools.partial(convolve_kernel, span, spans, first, len...  11.6 us
    pallas_call x1, Pallas kernels, upper(): pl.pallas_call(functools.partial(upper_kernel, n, ctx, parts), out_shape=...  10.2 us
    pallas_call x1, Pallas kernels, span_states(): pl.pallas_call(functools.partial(states_kernel, spans), out_shape=[jax.Sh...  7.78 us
    pallas_call x2, Pallas kernels, local_product(): pl.pallas_call(functools.partial(product_kernel, start, columns), out_sha...  7.15 us
    ppermute x3, waiting for transfers between devices, exchange_states(): lax.ppermute(totals, 'ctx', [(i, i ^ other) for i in range(ctx)])  6.19 us
  transfers between devices with their start and end apart: 30, of which 8 were waited for; matrix products, arithmetic and copies ran while one was open for 0% of the time, Pallas kernels for 21%

profile of v6, /device:TPU:0, one launch (start us, length us, event | category | flops | bytes accessed | tf_op | source)
XLA Modules:
  0.0 169.6 jit_solution(6578435688933600175)
XLA Ops:
  0.0 7.8 %span_states.1 = (f32[2,16,1024]{2,1,0:T(8,128)S(1)}, bf16[1024,1024]{1,0:T(8,128)(2,1)S(1)}) custom-call(bf16[1024,1024]{1,0:T(8,128)(2,1)} %keys_ref.1, bf16[1024,1024]{1,0:T(8,128)(2,1)} %values_ref.1, f32[16,1024]{1,0:T(8,128)} %rates_ref.7), custom_call_target="tpu_custom_call" | custom-call | tf_op jit(solution)/shard_map/span_states/pallas_call | solution.py:88
  7.8 3.0 %collective-permute-start.10 = (f32[2,16,1024]{2,1,0:T(8,128)S(1)}, f32[2,16,1024]{2,1,0:T(8,128)S(1)}, u32[]{:S(2)}, u32[]{:S(2)}) collective-permute-start(f32[2,16,1024]{2,1,0:T(8,128)S(1)} %get-tuple-element.26), channel_id=1, source_target_pairs={{0,8},{4,12},{8,0},{12,4},{16,24},{20,28},{24,16},{28,20},{1,9},{5... | collective-permute-start | bytes 393224 | tf_op jit(solution)/shard_map/ppermute | solution.py:337
  12.4 2.3 %collective-permute-done.10 = f32[2,16,1024]{2,1,0:T(8,128)S(1)} collective-permute-done((f32[2,16,1024]{2,1,0:T(8,128)S(1)}, f32[2,16,1024]{2,1,0:T(8,128)S(1)}, u32[]{:S(2)}, u32[]{:S(2)}) %collective-permute-start.10) | collective-permute-done | bytes 131104 | tf_op jit(solution)/shard_map/ppermute | solution.py:337
  14.7 3.9 %collective-permute-done.11 = f32[2,16,1024]{2,1,0:T(8,128)S(1)} collective-permute-done((f32[2,16,1024]{2,1,0:T(8,128)S(1)}, f32[2,16,1024]{2,1,0:T(8,128)S(1)}, u32[]{:S(2)}, u32[]{:S(2)}) %collective-permute-start.11) | collective-permute-done | bytes 131104 | tf_op jit(solution)/shard_map/ppermute | solution.py:337
  18.7 3.2 %span_response.1.response_ref = f32[512,512]{1,0:T(8,128)S(1)} custom-call(bf16[1024,1024]{1,0:T(8,128)(2,1)S(1)} %get-tuple-element.25.gated_ref, f32[16,1024]{1,0:T(8,128)S(1)} %copy-done.2, f32[16,1024]{1,0:T(8,128)S(1)} %copy-done.1), custom_call_target="tpu_custom_call" | custom-call | tf_op jit(solution)/shard_map/span_response/pallas_call | solution.py:245
  22.0 2.8 %complete.1.refs_9_ = bf16[512,512]{1,0:T(8,128)(2,1)S(1)} custom-call(s32[16]{0:T(128)S(1)} %copy-done.3, bf16[1024,1024]{1,0:T(8,128)(2,1)S(1)} %copy-done, f32[512,512]{1,0:T(8,128)S(1)} %span_response.1.response_ref, f32[16,1024]{1,0:T(8,128)S(1)} %copy-done.2, f32[16,1024]{1,0:T(8,128)S(1)} %copy-done.1, ...), custom_call_target="tpu_custom_call" | custom-call | tf_op jit(solution)/shard_map/complete/pallas_call | solution.py:311
  24.8 1.6 collective-permute-start.14
  27.2 4.0 %convolve.2.refs_10_ = bf16[512,512]{1,0:T(8,128)(2,1)S(1)} custom-call(s32[16]{0:T(128)S(1)} %copy-done.3, bf16[1024,1024]{1,0:T(8,128)(2,1)S(1)} %copy-done, bf16[1024,1024]{1,0:T(8,128)(2,1)S(1)} %get-tuple-element.25.gated_ref, f32[16,1024]{1,0:T(8,128)S(1)} %copy-done.2, f32[16,1024]{1,0:T(8,128)S(1)} %copy-done.1, ...), custom_call_target="tpu_custom_call" | custom-call | tf_op jit(solution)/shard_map/convolve/pallas_call | solution.py:199
  31.2 4.4 %collective-permute-start.15 = (bf16[512,512]{1,0:T(8,128)(2,1)S(1)}, bf16[512,512]{1,0:T(8,128)(2,1)S(1)}, u32[]{:S(2)}, u32[]{:S(2)}) collective-permute-start(bf16[512,512]{1,0:T(8,128)(2,1)S(1)} %convolve.2.refs_10_), channel_id=1, source_target_pairs={{0,1},{1,0},{2,3},{3,2},{4,5},{5,4},{6,7},{7,6},{8,9},{9,8},{10,11... | collective-permute-start | bytes 1572872 | tf_op jit(solution)/shard_map/ppermute | solution.py:606
  37.5 7.6 %convolve.3.rows_ref = bf16[512,1024]{1,0:T(8,128)(2,1)S(1)} custom-call(s32[16]{0:T(128)S(1)} %copy-done.3, bf16[1024,1024]{1,0:T(8,128)(2,1)S(1)} %copy-done, bf16[1024,1024]{1,0:T(8,128)(2,1)S(1)} %get-tuple-element.25.gated_ref, f32[16,1024]{1,0:T(8,128)S(1)} %copy-done.2, f32[16,1024]{1,0:T(8,128)S(1)} %copy-done.1, ...), custom_call_target="tpu_custom_call" | custom-call | tf_op jit(solution)/shard_map/convolve/pallas_call | solution.py:199
  45.1 3.6 %local_product.2.product_ref = bf16[512,2048]{1,0:T(8,128)(2,1)S(1)} custom-call(bf16[512,1024]{1,0:T(8,128)(2,1)S(1)} %convolve.3.rows_ref, bf16[1024,4096]{1,0:T(8,128)(2,1)S(1)} %bitcast.4), custom_call_target="tpu_custom_call" | custom-call | tf_op jit(solution)/shard_map/local_product/pallas_call | solution.py:583
  48.9 1.5 collective-permute-start.17
  50.5 2.9 %collective-permute-start.2 = (bf16[128,1024]{1,0:T(8,128)(2,1)S(1)}, bf16[128,1024]{1,0:T(8,128)(2,1)S(1)}, u32[]{:S(2)}, u32[]{:S(2)}) collective-permute-start(bf16[128,1024]{1,0:T(8,128)(2,1)S(1)} %get-tuple-element.24), channel_id=1, source_target_pairs={{0,3},{1,2},{2,1},{3,0},{4,7},{5,6},{6,5},{7,4},{8,11},{9,10},{10,... | collective-permute-start | bytes 786440 | tf_op jit(solution)/shard_map/ppermute | solution.py:377
  54.1 1.9 %collective-permute-start.1 = (bf16[128,1024]{1,0:T(8,128)(2,1)S(1)}, bf16[128,1024]{1,0:T(8,128)(2,1)S(1)}, u32[]{:S(2)}, u32[]{:S(2)}) collective-permute-start(bf16[128,1024]{1,0:T(8,128)(2,1)S(1)} %get-tuple-element.23), channel_id=1, source_target_pairs={{0,2},{1,3},{2,0},{3,1},{4,6},{5,7},{6,4},{7,5},{8,10},{9,11},{10,... | collective-permute-start | bytes 786440 | tf_op jit(solution)/shard_map/ppermute | solution.py:377
  56.0 3.6 %local_product.3.product_ref = bf16[512,2048]{1,0:T(8,128)(2,1)S(1)} custom-call(bf16[512,1024]{1,0:T(8,128)(2,1)S(1)} %convolve.3.rows_ref, bf16[1024,4096]{1,0:T(8,128)(2,1)S(1)} %bitcast.4), custom_call_target="tpu_custom_call" | custom-call | tf_op jit(solution)/shard_map/local_product/pallas_call | solution.py:583
  59.8 12.1 %collective-permute-done.2 = bf16[128,1024]{1,0:T(8,128)(2,1)S(1)} collective-permute-done((bf16[128,1024]{1,0:T(8,128)(2,1)S(1)}, bf16[128,1024]{1,0:T(8,128)(2,1)S(1)}, u32[]{:S(2)}, u32[]{:S(2)}) %collective-permute-start.2) | collective-permute-done | bytes 262176 | tf_op jit(solution)/shard_map/ppermute | solution.py:377
  71.9 16.4 %collective-permute-done.1 = bf16[128,1024]{1,0:T(8,128)(2,1)S(1)} collective-permute-done((bf16[128,1024]{1,0:T(8,128)(2,1)S(1)}, bf16[128,1024]{1,0:T(8,128)(2,1)S(1)}, u32[]{:S(2)}, u32[]{:S(2)}) %collective-permute-start.1) | collective-permute-done | bytes 262176 | tf_op jit(solution)/shard_map/ppermute | solution.py:377
  94.3 9.0 %collective-permute-start.23 = (bf16[512,512]{1,0:T(8,128)(2,1)S(1)}, bf16[512,512]{1,0:T(8,128)(2,1)S(1)}, u32[]{:S(2)}, u32[]{:S(2)}) collective-permute-start(bf16[512,512]{1,0:T(8,128)(2,1)S(1)} %get-tuple-element.32), channel_id=1, source_target_pairs={{0,1},{1,0},{2,3},{3,2},{4,5},{5,4},{6,7},{7,6},{8,9},{9,8},{10,11... | collective-permute-start | bytes 1572872 | tf_op jit(solution)/shard_map/ppermute | solution.py:606
  103.3 6.2 %collective-permute-done.4.refs_3_ = bf16[3,128,1024]{2,1,0:T(8,128)(2,1)S(1)} collective-permute-done((bf16[3,128,1024]{2,1,0:T(8,128)(2,1)S(1)}, bf16[3,128,1024]{2,1,0:T(8,128)(2,1)S(1)}, u32[]{:S(2)}, u32[]{:S(2)}) %collective-permute-start.4) | collective-permute-done | bytes 786464 | tf_op jit(solution)/shard_map/ppermute | solution.py:381
  109.6 14.8 %collective-permute-done.6.refs_5_ = bf16[3,128,1024]{2,1,0:T(8,128)(2,1)S(1)} collective-permute-done((bf16[3,128,1024]{2,1,0:T(8,128)(2,1)S(1)}, bf16[3,128,1024]{2,1,0:T(8,128)(2,1)S(1)}, u32[]{:S(2)}, u32[]{:S(2)}) %collective-permute-start.6) | collective-permute-done | bytes 786464 | tf_op jit(solution)/shard_map/ppermute | solution.py:381
  127.4 20.2 %collective-permute-start.26 = (bf16[512,512]{1,0:T(8,128)(2,1)S(1)}, bf16[512,512]{1,0:T(8,128)(2,1)S(1)}, u32[]{:S(2)}, u32[]{:S(2)}) collective-permute-start(bf16[512,512]{1,0:T(8,128)(2,1)S(1)} %get-tuple-element.35), channel_id=1, source_target_pairs={{0,1},{1,0},{2,3},{3,2},{4,5},{5,4},{6,7},{7,6},{8,9},{9,8},{10,11... | collective-permute-start | bytes 1572872 | tf_op jit(solution)/shard_map/ppermute | solution.py:606
  148.5 2.8 %collective-permute-start.28 = (bf16[512,512]{1,0:T(8,128)(2,1)S(1)}, bf16[512,512]{1,0:T(8,128)(2,1)S(1)}, u32[]{:S(2)}, u32[]{:S(2)}) collective-permute-start(bf16[512,512]{1,0:T(8,128)(2,1)S(1)} %get-tuple-element.37), channel_id=1, source_target_pairs={{0,1},{1,0},{2,3},{3,2},{4,5},{5,4},{6,7},{7,6},{8,9},{9,8},{10,11... | collective-permute-start | bytes 1572872 | tf_op jit(solution)/shard_map/ppermute | solution.py:606
  152.0 10.2 %upper.1.unused_ref = bf16[1024,1024]{1,0:T(8,128)(2,1)} custom-call(bf16[1024,4096]{1,0:T(8,128)(2,1)} %refs_0_.1, bf16[3,128,1024]{2,1,0:T(8,128)(2,1)S(1)} %pad_maximum_fusion.refs_1_, bf16[3,128,1024]{2,1,0:T(8,128)(2,1)S(1)} %collective-permute-done.3.refs_2_, bf16[3,128,1024]{2,1,0:T(8,128)(2,1)S(1)} %collective-permute-done.4.refs_3_, ...), custom_call_target="tpu_custom_call" | custom-call | tf_op jit(solution)/shard_map/upper/pallas_call | solution.py:466
  163.3 5.3 %collective-permute-done.28.left_ref = bf16[512,512]{1,0:T(8,128)(2,1)S(1)} collective-permute-done((bf16[512,512]{1,0:T(8,128)(2,1)S(1)}, bf16[512,512]{1,0:T(8,128)(2,1)S(1)}, u32[]{:S(2)}, u32[]{:S(2)}) %collective-permute-start.28) | collective-permute-done | bytes 524320 | tf_op jit(solution)/shard_map/ppermute | solution.py:606
  (71 shorter events, 17.9 us)
Async XLA Ops:
  10.8 7.8 %collective-permute-start.11 = (f32[2,16,1024]{2,1,0:T(8,128)S(1)}, f32[2,16,1024]{2,1,0:T(8,128)S(1)}, u32[]{:S(2)}, u32[]{:S(2)}) collective-permute-start(f32[2,16,1024]{2,1,0:T(8,128)S(1)} %get-tuple-element.26), channel_id=1, source_target_pairs={{0,16},{4,20},{8,24},{12,28},{16,0},{20,4},{24,8},{28,12},{1,17},{... | collective-permute-start | bytes 393224 | tf_op jit(solution)/shard_map/ppermute | solution.py:337
  24.8 23.9 %collective-permute-start.14 = (bf16[512,512]{1,0:T(8,128)(2,1)S(1)}, bf16[512,512]{1,0:T(8,128)(2,1)S(1)}, u32[]{:S(2)}, u32[]{:S(2)}) collective-permute-start(bf16[512,512]{1,0:T(8,128)(2,1)S(1)} %complete.1.refs_9_), channel_id=1, source_target_pairs={{0,1},{1,0},{2,3},{3,2},{4,5},{5,4},{6,7},{7,6},{8,9},{9,8},{10,11... | collective-permute-start | bytes 1572872 | tf_op jit(solution)/shard_map/ppermute | solution.py:606
  26.5 22.3 %collective-permute-start.16 = (bf16[512,512]{1,0:T(8,128)(2,1)S(1)}, bf16[512,512]{1,0:T(8,128)(2,1)S(1)}, u32[]{:S(2)}, u32[]{:S(2)}) collective-permute-start(bf16[512,512]{1,0:T(8,128)(2,1)S(1)} %complete.1.refs_9_), channel_id=1, source_target_pairs={{1,2},{2,1},{5,6},{6,5},{9,10},{10,9},{13,14},{14,13},{17,18},{18,... | collective-permute-start | bytes 1572872 | tf_op jit(solution)/shard_map/ppermute | solution.py:607
  31.2 22.8 %collective-permute-start.15 = (bf16[512,512]{1,0:T(8,128)(2,1)S(1)}, bf16[512,512]{1,0:T(8,128)(2,1)S(1)}, u32[]{:S(2)}, u32[]{:S(2)}) collective-permute-start(bf16[512,512]{1,0:T(8,128)(2,1)S(1)} %convolve.2.refs_10_), channel_id=1, source_target_pairs={{0,1},{1,0},{2,3},{3,2},{4,5},{5,4},{6,7},{7,6},{8,9},{9,8},{10,11... | collective-permute-start | bytes 1572872 | tf_op jit(solution)/shard_map/ppermute | solution.py:606
  35.7 20.3 %collective-permute-start.18 = (bf16[512,512]{1,0:T(8,128)(2,1)S(1)}, bf16[512,512]{1,0:T(8,128)(2,1)S(1)}, u32[]{:S(2)}, u32[]{:S(2)}) collective-permute-start(bf16[512,512]{1,0:T(8,128)(2,1)S(1)} %convolve.2.refs_10_), channel_id=1, source_target_pairs={{1,2},{2,1},{5,6},{6,5},{9,10},{10,9},{13,14},{14,13},{17,18},{18,... | collective-permute-start | bytes 1572872 | tf_op jit(solution)/shard_map/ppermute | solution.py:607
  48.9 41.4 %collective-permute-start.17 = (bf16[512,512]{1,0:T(8,128)(2,1)S(1)}, bf16[512,512]{1,0:T(8,128)(2,1)S(1)}, u32[]{:S(2)}, u32[]{:S(2)}) collective-permute-start(bf16[512,512]{1,0:T(8,128)(2,1)S(1)} %get-tuple-element.27), channel_id=1, source_target_pairs={{0,1},{1,0},{2,3},{3,2},{4,5},{5,4},{6,7},{7,6},{8,9},{9,8},{10,11... | collective-permute-start | bytes 1572872 | tf_op jit(solution)/shard_map/ppermute | solution.py:606
  50.5 21.4 %collective-permute-start.2 = (bf16[128,1024]{1,0:T(8,128)(2,1)S(1)}, bf16[128,1024]{1,0:T(8,128)(2,1)S(1)}, u32[]{:S(2)}, u32[]{:S(2)}) collective-permute-start(bf16[128,1024]{1,0:T(8,128)(2,1)S(1)} %get-tuple-element.24), channel_id=1, source_target_pairs={{0,3},{1,2},{2,1},{3,0},{4,7},{5,6},{6,5},{7,4},{8,11},{9,10},{10,... | collective-permute-start | bytes 786440 | tf_op jit(solution)/shard_map/ppermute | solution.py:377
  53.4 37.8 %collective-permute-start.20 = (bf16[512,512]{1,0:T(8,128)(2,1)S(1)}, bf16[512,512]{1,0:T(8,128)(2,1)S(1)}, u32[]{:S(2)}, u32[]{:S(2)}) collective-permute-start(bf16[512,512]{1,0:T(8,128)(2,1)S(1)} %get-tuple-element.29), channel_id=1, source_target_pairs={{1,2},{2,1},{5,6},{6,5},{9,10},{10,9},{13,14},{14,13},{17,18},{18,... | collective-permute-start | bytes 1572872 | tf_op jit(solution)/shard_map/ppermute | solution.py:607
  54.1 34.2 %collective-permute-start.1 = (bf16[128,1024]{1,0:T(8,128)(2,1)S(1)}, bf16[128,1024]{1,0:T(8,128)(2,1)S(1)}, u32[]{:S(2)}, u32[]{:S(2)}) collective-permute-start(bf16[128,1024]{1,0:T(8,128)(2,1)S(1)} %get-tuple-element.23), channel_id=1, source_target_pairs={{0,2},{1,3},{2,0},{3,1},{4,6},{5,7},{6,4},{7,5},{8,10},{9,11},{10,... | collective-permute-start | bytes 786440 | tf_op jit(solution)/shard_map/ppermute | solution.py:377
  56.0 33.0 %collective-permute-start = (bf16[128,1024]{1,0:T(8,128)(2,1)S(1)}, bf16[128,1024]{1,0:T(8,128)(2,1)S(1)}, u32[]{:S(2)}, u32[]{:S(2)}) collective-permute-start(bf16[128,1024]{1,0:T(8,128)(2,1)S(1)} %get-tuple-element.22), channel_id=1, source_target_pairs={{0,1},{1,0},{2,3},{3,2},{4,5},{5,4},{6,7},{7,6},{8,9},{9,8},{10,11... | collective-permute-start | bytes 786440 | tf_op jit(solution)/shard_map/ppermute | solution.py:377
  71.9 20.9 %collective-permute-start.19 = (bf16[512,512]{1,0:T(8,128)(2,1)S(1)}, bf16[512,512]{1,0:T(8,128)(2,1)S(1)}, u32[]{:S(2)}, u32[]{:S(2)}) collective-permute-start(bf16[512,512]{1,0:T(8,128)(2,1)S(1)} %get-tuple-element.28), channel_id=1, source_target_pairs={{0,1},{1,0},{2,3},{3,2},{4,5},{5,4},{6,7},{7,6},{8,9},{9,8},{10,11... | collective-permute-start | bytes 1572872 | tf_op jit(solution)/shard_map/ppermute | solution.py:606
  89.1 20.5 %collective-permute-start.4 = (bf16[3,128,1024]{2,1,0:T(8,128)(2,1)S(1)}, bf16[3,128,1024]{2,1,0:T(8,128)(2,1)S(1)}, u32[]{:S(2)}, u32[]{:S(2)}) collective-permute-start(bf16[3,128,1024]{2,1,0:T(8,128)(2,1)S(1)} %pad_maximum_fusion.refs_1_), channel_id=1, source_target_pairs={{0,8},{4,12},{8,0},{12,4},{16,24},{20,28},{24,16},{28,20},{1,9},{5... | collective-permute-start | bytes 2359304 | tf_op jit(solution)/shard_map/ppermute | solution.py:381
  90.3 34.0 %collective-permute-start.6 = (bf16[3,128,1024]{2,1,0:T(8,128)(2,1)S(1)}, bf16[3,128,1024]{2,1,0:T(8,128)(2,1)S(1)}, u32[]{:S(2)}, u32[]{:S(2)}) collective-permute-start(bf16[3,128,1024]{2,1,0:T(8,128)(2,1)S(1)} %pad_maximum_fusion.refs_1_), channel_id=1, source_target_pairs={{0,16},{4,20},{8,24},{12,28},{16,0},{20,4},{24,8},{28,12},{1,17},{... | collective-permute-start | bytes 2359304 | tf_op jit(solution)/shard_map/ppermute | solution.py:381
  91.2 34.8 %collective-permute-start.8 = (bf16[3,128,1024]{2,1,0:T(8,128)(2,1)S(1)}, bf16[3,128,1024]{2,1,0:T(8,128)(2,1)S(1)}, u32[]{:S(2)}, u32[]{:S(2)}) collective-permute-start(bf16[3,128,1024]{2,1,0:T(8,128)(2,1)S(1)} %pad_maximum_fusion.refs_1_), channel_id=1, source_target_pairs={{0,24},{4,28},{8,16},{12,20},{16,8},{20,12},{24,0},{28,4},{1,25},{... | collective-permute-start | bytes 2359304 | tf_op jit(solution)/shard_map/ppermute | solution.py:381
  92.8 33.2 %collective-permute-start.21 = (bf16[512,512]{1,0:T(8,128)(2,1)S(1)}, bf16[512,512]{1,0:T(8,128)(2,1)S(1)}, u32[]{:S(2)}, u32[]{:S(2)}) collective-permute-start(bf16[512,512]{1,0:T(8,128)(2,1)S(1)} %get-tuple-element.30), channel_id=1, source_target_pairs={{0,1},{1,0},{2,3},{3,2},{4,5},{5,4},{6,7},{7,6},{8,9},{9,8},{10,11... | collective-permute-start | bytes 1572872 | tf_op jit(solution)/shard_map/ppermute | solution.py:606
  94.3 32.2 %collective-permute-start.23 = (bf16[512,512]{1,0:T(8,128)(2,1)S(1)}, bf16[512,512]{1,0:T(8,128)(2,1)S(1)}, u32[]{:S(2)}, u32[]{:S(2)}) collective-permute-start(bf16[512,512]{1,0:T(8,128)(2,1)S(1)} %get-tuple-element.32), channel_id=1, source_target_pairs={{0,1},{1,0},{2,3},{3,2},{4,5},{5,4},{6,7},{7,6},{8,9},{9,8},{10,11... | collective-permute-start | bytes 1572872 | tf_op jit(solution)/shard_map/ppermute | solution.py:606
  109.6 38.3 %collective-permute-start.3 = (bf16[3,128,1024]{2,1,0:T(8,128)(2,1)S(1)}, bf16[3,128,1024]{2,1,0:T(8,128)(2,1)S(1)}, u32[]{:S(2)}, u32[]{:S(2)}) collective-permute-start(bf16[3,128,1024]{2,1,0:T(8,128)(2,1)S(1)} %pad_maximum_fusion.refs_1_), channel_id=1, source_target_pairs={{0,4},{4,0},{8,12},{12,8},{16,20},{20,16},{24,28},{28,24},{1,5},{5... | collective-permute-start | bytes 2359304 | tf_op jit(solution)/shard_map/ppermute | solution.py:383
  126.0 22.6 %collective-permute-start.5 = (bf16[3,128,1024]{2,1,0:T(8,128)(2,1)S(1)}, bf16[3,128,1024]{2,1,0:T(8,128)(2,1)S(1)}, u32[]{:S(2)}, u32[]{:S(2)}) collective-permute-start(bf16[3,128,1024]{2,1,0:T(8,128)(2,1)S(1)} %collective-permute-done.4.refs_3_), channel_id=1, source_target_pairs={{0,4},{4,0},{8,12},{12,8},{16,20},{20,16},{24,28},{28,24},{1,5},{5... | collective-permute-start | bytes 2359304 | tf_op jit(solution)/shard_map/ppermute | solution.py:383
  126.0 25.4 %collective-permute-start.7 = (bf16[3,128,1024]{2,1,0:T(8,128)(2,1)S(1)}, bf16[3,128,1024]{2,1,0:T(8,128)(2,1)S(1)}, u32[]{:S(2)}, u32[]{:S(2)}) collective-permute-start(bf16[3,128,1024]{2,1,0:T(8,128)(2,1)S(1)} %collective-permute-done.6.refs_5_), channel_id=1, source_target_pairs={{0,4},{4,0},{8,12},{12,8},{16,20},{20,16},{24,28},{28,24},{1,5},{5... | collective-permute-start | bytes 2359304 | tf_op jit(solution)/shard_map/ppermute | solution.py:383
  127.2 24.8 %collective-permute-start.9 = (bf16[3,128,1024]{2,1,0:T(8,128)(2,1)S(1)}, bf16[3,128,1024]{2,1,0:T(8,128)(2,1)S(1)}, u32[]{:S(2)}, u32[]{:S(2)}) collective-permute-start(bf16[3,128,1024]{2,1,0:T(8,128)(2,1)S(1)} %collective-permute-done.8.refs_7_), channel_id=1, source_target_pairs={{0,4},{4,0},{8,12},{12,8},{16,20},{20,16},{24,28},{28,24},{1,5},{5... | collective-permute-start | bytes 2359304 | tf_op jit(solution)/shard_map/ppermute | solution.py:383
  127.4 34.8 %collective-permute-start.26 = (bf16[512,512]{1,0:T(8,128)(2,1)S(1)}, bf16[512,512]{1,0:T(8,128)(2,1)S(1)}, u32[]{:S(2)}, u32[]{:S(2)}) collective-permute-start(bf16[512,512]{1,0:T(8,128)(2,1)S(1)} %get-tuple-element.35), channel_id=1, source_target_pairs={{0,1},{1,0},{2,3},{3,2},{4,5},{5,4},{6,7},{7,6},{8,9},{9,8},{10,11... | collective-permute-start | bytes 1572872 | tf_op jit(solution)/shard_map/ppermute | solution.py:606
  147.8 14.4 %collective-permute-start.27 = (bf16[512,512]{1,0:T(8,128)(2,1)S(1)}, bf16[512,512]{1,0:T(8,128)(2,1)S(1)}, u32[]{:S(2)}, u32[]{:S(2)}) collective-permute-start(bf16[512,512]{1,0:T(8,128)(2,1)S(1)} %get-tuple-element.36), channel_id=1, source_target_pairs={{1,2},{2,1},{5,6},{6,5},{9,10},{10,9},{13,14},{14,13},{17,18},{18,... | collective-permute-start | bytes 1572872 | tf_op jit(solution)/shard_map/ppermute | solution.py:607
  148.5 20.0 %collective-permute-start.28 = (bf16[512,512]{1,0:T(8,128)(2,1)S(1)}, bf16[512,512]{1,0:T(8,128)(2,1)S(1)}, u32[]{:S(2)}, u32[]{:S(2)}) collective-permute-start(bf16[512,512]{1,0:T(8,128)(2,1)S(1)} %get-tuple-element.37), channel_id=1, source_target_pairs={{0,1},{1,0},{2,3},{3,2},{4,5},{5,4},{6,7},{7,6},{8,9},{9,8},{10,11... | collective-permute-start | bytes 1572872 | tf_op jit(solution)/shard_map/ppermute | solution.py:606
  151.3 17.2 %collective-permute-start.29 = (bf16[512,512]{1,0:T(8,128)(2,1)S(1)}, bf16[512,512]{1,0:T(8,128)(2,1)S(1)}, u32[]{:S(2)}, u32[]{:S(2)}) collective-permute-start(bf16[512,512]{1,0:T(8,128)(2,1)S(1)} %get-tuple-element.38), channel_id=1, source_target_pairs={{1,2},{2,1},{5,6},{6,5},{9,10},{10,9},{13,14},{14,13},{17,18},{18,... | collective-permute-start | bytes 1572872 | tf_op jit(solution)/shard_map/ppermute | solution.py:607
  (12 other events, 114.6 us)

commit v7 on v6

--- a/solution.py
+++ b/solution.py
@@ -14,7 +14,7 @@
 FIRST = 4
 WIDE = 512
 UNROLL = 8
-DEPTH = 2
+DEPTH = 4
 
 
 def held_out(array):
@@ -301,7 +301,7 @@
             out_ref[rows, cells] = (gate * mixed).astype(jnp.bfloat16)
             return unused
 
-        lax.fori_loop(0, length // ROWS, body, 0, unroll=2)
+        lax.fori_loop(0, length // ROWS, body, 0, unroll=4)
 
 
 def complete(order, queries, response, residues, rates, states, spans, span, first):
@@ -488,20 +488,23 @@
     height, width = left_ref.shape
     at = pl.ds(pl.multiple_of(lax.axis_index("tp") * width, 128), width)
 
-    @pl.loop(0, height // 64)
-    def _(block):
-        rows = pl.ds(pl.multiple_of(block * 64, 64), 64)
-        result_ref[rows, :] = (
-            product_ref[rows, at].astype(jnp.float32)
-            + left_ref[rows, :].astype(jnp.float32)
-            + right_ref[rows, :].astype(jnp.float32)
-        ).astype(jnp.bfloat16)
-
-    copy = pltpu.make_async_copy(
-        result_ref, out_ref.at[pl.ds(out_ref.shape[0] - height, height), pl.ds(first, width)], sem
-    )
-    copy.start()
-    copy.wait()
+    piece = height // 4
+    copies = []
+    for part in range(4):
+        for start in range(part * piece, (part + 1) * piece, 64):
+            rows = pl.ds(start, 64)
+            result_ref[rows, :] = (
+                product_ref[rows, at].astype(jnp.float32)
+                + left_ref[rows, :].astype(jnp.float32)
+                + right_ref[rows, :].astype(jnp.float32)
+            ).astype(jnp.bfloat16)
+        rows = pl.ds(part * piece, piece)
+        target = (pl.ds(out_ref.shape[0] - height + part * piece, piece), pl.ds(first, width))
+        copy = pltpu.make_async_copy(result_ref.at[rows], out_ref.at[target], sem.at[part])
+        copy.start()
+        copies.append(copy)
+    for copy in copies:
+        copy.wait()
 
 
 def finish(result, product, left, right, first):
@@ -512,7 +515,7 @@
         out_shape=jax.ShapeDtypeStruct(result.shape, result.dtype),
         in_specs=[anywhere, inside, inside, inside],
         out_specs=anywhere,
-        scratch_shapes=[pltpu.VMEM(left.shape, jnp.bfloat16), pltpu.SemaphoreType.DMA(())],
+        scratch_shapes=[pltpu.VMEM(left.shape, jnp.bfloat16), pltpu.SemaphoreType.DMA((4,))],
         input_output_aliases={0: 0},
         compiler_params=pltpu.CompilerParams(vmem_limit_bytes=2 << 20),
         name="finish",

time: 172 us -> 171 us (level)
  no operation moved by 1% of the time
where the time goes in v7:
time: 171 us; the launch traced here: 169 us
  waiting for transfers between devices  62.3 us (36%)
  starting transfers between devices  60.1 us (35%)
  Pallas kernels  46 us (27%)
    ppermute x8, starting transfers between devices, exchange(): evens[slot, part] = lax.ppermute(even, 'tp', pairs[0])  41 us
    ppermute x3, waiting for transfers between devices, gather_weights(): lax.ppermute(cut[shift - 1], 'tp', [(i, i ^ shift) for i in range(n)])  28.7 us
    ppermute x3, waiting for transfers between devices, gather_weights(): lax.ppermute(held, 'ctx', [(i, i ^ other) for i in range(ctx)])  22 us
    pallas_call x2, Pallas kernels, convolve(): pl.pallas_call(functools.partial(convolve_kernel, span, spans, first, len...  11.4 us
    pallas_call x1, Pallas kernels, upper(): pl.pallas_call(functools.partial(upper_kernel, n, ctx, parts), out_shape=...  10.2 us
    pallas_call x1, Pallas kernels, span_states(): pl.pallas_call(functools.partial(states_kernel, spans), out_shape=[jax.Sh...  7.7 us
    pallas_call x2, Pallas kernels, local_product(): pl.pallas_call(functools.partial(product_kernel, start, columns), out_sha...  7.15 us
    ppermute x3, waiting for transfers between devices, exchange_states(): lax.ppermute(totals, 'ctx', [(i, i ^ other) for i in range(ctx)])  6.19 us
  transfers between devices with their start and end apart: 30, of which 8 were waited for; matrix products, arithmetic and copies ran while one was open for 0% of the time, Pallas kernels for 21%

profile of v7, /device:TPU:0, one launch (start us, length us, event | category | flops | bytes accessed | tf_op | source)
XLA Modules:
  0.0 169.0 jit_solution(7637030934660560816)
XLA Ops:
  0.0 7.7 %span_states.1 = (f32[2,16,1024]{2,1,0:T(8,128)S(1)}, bf16[1024,1024]{1,0:T(8,128)(2,1)S(1)}) custom-call(bf16[1024,1024]{1,0:T(8,128)(2,1)} %keys_ref.1, bf16[1024,1024]{1,0:T(8,128)(2,1)} %values_ref.1, f32[16,1024]{1,0:T(8,128)} %rates_ref.7), custom_call_target="tpu_custom_call" | custom-call | tf_op jit(solution)/shard_map/span_states/pallas_call | solution.py:88
  7.7 3.0 %collective-permute-start.10 = (f32[2,16,1024]{2,1,0:T(8,128)S(1)}, f32[2,16,1024]{2,1,0:T(8,128)S(1)}, u32[]{:S(2)}, u32[]{:S(2)}) collective-permute-start(f32[2,16,1024]{2,1,0:T(8,128)S(1)} %get-tuple-element.26), channel_id=1, source_target_pairs={{0,8},{4,12},{8,0},{12,4},{16,24},{20,28},{24,16},{28,20},{1,9},{5... | collective-permute-start | bytes 393224 | tf_op jit(solution)/shard_map/ppermute | solution.py:337
  12.3 2.3 %collective-permute-done.10 = f32[2,16,1024]{2,1,0:T(8,128)S(1)} collective-permute-done((f32[2,16,1024]{2,1,0:T(8,128)S(1)}, f32[2,16,1024]{2,1,0:T(8,128)S(1)}, u32[]{:S(2)}, u32[]{:S(2)}) %collective-permute-start.10) | collective-permute-done | bytes 131104 | tf_op jit(solution)/shard_map/ppermute | solution.py:337
  14.6 3.9 %collective-permute-done.11 = f32[2,16,1024]{2,1,0:T(8,128)S(1)} collective-permute-done((f32[2,16,1024]{2,1,0:T(8,128)S(1)}, f32[2,16,1024]{2,1,0:T(8,128)S(1)}, u32[]{:S(2)}, u32[]{:S(2)}) %collective-permute-start.11) | collective-permute-done | bytes 131104 | tf_op jit(solution)/shard_map/ppermute | solution.py:337
  18.7 3.1 %span_response.1.response_ref = f32[512,512]{1,0:T(8,128)S(1)} custom-call(bf16[1024,1024]{1,0:T(8,128)(2,1)S(1)} %get-tuple-element.25.gated_ref, f32[16,1024]{1,0:T(8,128)S(1)} %copy-done.2, f32[16,1024]{1,0:T(8,128)S(1)} %copy-done.1), custom_call_target="tpu_custom_call" | custom-call | tf_op jit(solution)/shard_map/span_response/pallas_call | solution.py:245
  21.8 2.6 %complete.1.refs_9_ = bf16[512,512]{1,0:T(8,128)(2,1)S(1)} custom-call(s32[16]{0:T(128)S(1)} %copy-done.3, bf16[1024,1024]{1,0:T(8,128)(2,1)S(1)} %copy-done, f32[512,512]{1,0:T(8,128)S(1)} %span_response.1.response_ref, f32[16,1024]{1,0:T(8,128)S(1)} %copy-done.2, f32[16,1024]{1,0:T(8,128)S(1)} %copy-done.1, ...), custom_call_target="tpu_custom_call" | custom-call | tf_op jit(solution)/shard_map/complete/pallas_call | solution.py:311
  24.4 1.6 collective-permute-start.14
  26.7 4.0 %convolve.2.refs_10_ = bf16[512,512]{1,0:T(8,128)(2,1)S(1)} custom-call(s32[16]{0:T(128)S(1)} %copy-done.3, bf16[1024,1024]{1,0:T(8,128)(2,1)S(1)} %copy-done, bf16[1024,1024]{1,0:T(8,128)(2,1)S(1)} %get-tuple-element.25.gated_ref, f32[16,1024]{1,0:T(8,128)S(1)} %copy-done.2, f32[16,1024]{1,0:T(8,128)S(1)} %copy-done.1, ...), custom_call_target="tpu_custom_call" | custom-call | tf_op jit(solution)/shard_map/convolve/pallas_call | solution.py:199
  30.7 4.4 %collective-permute-start.15 = (bf16[512,512]{1,0:T(8,128)(2,1)S(1)}, bf16[512,512]{1,0:T(8,128)(2,1)S(1)}, u32[]{:S(2)}, u32[]{:S(2)}) collective-permute-start(bf16[512,512]{1,0:T(8,128)(2,1)S(1)} %convolve.2.refs_10_), channel_id=1, source_target_pairs={{0,1},{1,0},{2,3},{3,2},{4,5},{5,4},{6,7},{7,6},{8,9},{9,8},{10,11... | collective-permute-start | bytes 1572872 | tf_op jit(solution)/shard_map/ppermute | solution.py:609
  37.0 7.4 %convolve.3.rows_ref = bf16[512,1024]{1,0:T(8,128)(2,1)S(1)} custom-call(s32[16]{0:T(128)S(1)} %copy-done.3, bf16[1024,1024]{1,0:T(8,128)(2,1)S(1)} %copy-done, bf16[1024,1024]{1,0:T(8,128)(2,1)S(1)} %get-tuple-element.25.gated_ref, f32[16,1024]{1,0:T(8,128)S(1)} %copy-done.2, f32[16,1024]{1,0:T(8,128)S(1)} %copy-done.1, ...), custom_call_target="tpu_custom_call" | custom-call | tf_op jit(solution)/shard_map/convolve/pallas_call | solution.py:199
  44.5 3.6 %local_product.2.product_ref = bf16[512,2048]{1,0:T(8,128)(2,1)S(1)} custom-call(bf16[512,1024]{1,0:T(8,128)(2,1)S(1)} %convolve.3.rows_ref, bf16[1024,4096]{1,0:T(8,128)(2,1)S(1)} %bitcast.4), custom_call_target="tpu_custom_call" | custom-call | tf_op jit(solution)/shard_map/local_product/pallas_call | solution.py:586
  48.3 1.6 collective-permute-start.17
  49.8 2.9 %collective-permute-start.2 = (bf16[128,1024]{1,0:T(8,128)(2,1)S(1)}, bf16[128,1024]{1,0:T(8,128)(2,1)S(1)}, u32[]{:S(2)}, u32[]{:S(2)}) collective-permute-start(bf16[128,1024]{1,0:T(8,128)(2,1)S(1)} %get-tuple-element.24), channel_id=1, source_target_pairs={{0,3},{1,2},{2,1},{3,0},{4,7},{5,6},{6,5},{7,4},{8,11},{9,10},{10,... | collective-permute-start | bytes 786440 | tf_op jit(solution)/shard_map/ppermute | solution.py:377
  53.4 1.9 %collective-permute-start.1 = (bf16[128,1024]{1,0:T(8,128)(2,1)S(1)}, bf16[128,1024]{1,0:T(8,128)(2,1)S(1)}, u32[]{:S(2)}, u32[]{:S(2)}) collective-permute-start(bf16[128,1024]{1,0:T(8,128)(2,1)S(1)} %get-tuple-element.23), channel_id=1, source_target_pairs={{0,2},{1,3},{2,0},{3,1},{4,6},{5,7},{6,4},{7,5},{8,10},{9,11},{10,... | collective-permute-start | bytes 786440 | tf_op jit(solution)/shard_map/ppermute | solution.py:377
  55.4 3.6 %local_product.3.product_ref = bf16[512,2048]{1,0:T(8,128)(2,1)S(1)} custom-call(bf16[512,1024]{1,0:T(8,128)(2,1)S(1)} %convolve.3.rows_ref, bf16[1024,4096]{1,0:T(8,128)(2,1)S(1)} %bitcast.4), custom_call_target="tpu_custom_call" | custom-call | tf_op jit(solution)/shard_map/local_product/pallas_call | solution.py:586
  59.1 12.1 %collective-permute-done.2 = bf16[128,1024]{1,0:T(8,128)(2,1)S(1)} collective-permute-done((bf16[128,1024]{1,0:T(8,128)(2,1)S(1)}, bf16[128,1024]{1,0:T(8,128)(2,1)S(1)}, u32[]{:S(2)}, u32[]{:S(2)}) %collective-permute-start.2) | collective-permute-done | bytes 262176 | tf_op jit(solution)/shard_map/ppermute | solution.py:377
  71.2 16.6 %collective-permute-done.1 = bf16[128,1024]{1,0:T(8,128)(2,1)S(1)} collective-permute-done((bf16[128,1024]{1,0:T(8,128)(2,1)S(1)}, bf16[128,1024]{1,0:T(8,128)(2,1)S(1)}, u32[]{:S(2)}, u32[]{:S(2)}) %collective-permute-start.1) | collective-permute-done | bytes 262176 | tf_op jit(solution)/shard_map/ppermute | solution.py:377
  93.9 9.0 %collective-permute-start.23 = (bf16[512,512]{1,0:T(8,128)(2,1)S(1)}, bf16[512,512]{1,0:T(8,128)(2,1)S(1)}, u32[]{:S(2)}, u32[]{:S(2)}) collective-permute-start(bf16[512,512]{1,0:T(8,128)(2,1)S(1)} %get-tuple-element.32), channel_id=1, source_target_pairs={{0,1},{1,0},{2,3},{3,2},{4,5},{5,4},{6,7},{7,6},{8,9},{9,8},{10,11... | collective-permute-start | bytes 1572872 | tf_op jit(solution)/shard_map/ppermute | solution.py:609
  102.9 6.2 %collective-permute-done.4.refs_3_ = bf16[3,128,1024]{2,1,0:T(8,128)(2,1)S(1)} collective-permute-done((bf16[3,128,1024]{2,1,0:T(8,128)(2,1)S(1)}, bf16[3,128,1024]{2,1,0:T(8,128)(2,1)S(1)}, u32[]{:S(2)}, u32[]{:S(2)}) %collective-permute-start.4) | collective-permute-done | bytes 786464 | tf_op jit(solution)/shard_map/ppermute | solution.py:381
  109.1 14.8 %collective-permute-done.6.refs_5_ = bf16[3,128,1024]{2,1,0:T(8,128)(2,1)S(1)} collective-permute-done((bf16[3,128,1024]{2,1,0:T(8,128)(2,1)S(1)}, bf16[3,128,1024]{2,1,0:T(8,128)(2,1)S(1)}, u32[]{:S(2)}, u32[]{:S(2)}) %collective-permute-start.6) | collective-permute-done | bytes 786464 | tf_op jit(solution)/shard_map/ppermute | solution.py:381
  127.0 20.2 %collective-permute-start.26 = (bf16[512,512]{1,0:T(8,128)(2,1)S(1)}, bf16[512,512]{1,0:T(8,128)(2,1)S(1)}, u32[]{:S(2)}, u32[]{:S(2)}) collective-permute-start(bf16[512,512]{1,0:T(8,128)(2,1)S(1)} %get-tuple-element.35), channel_id=1, source_target_pairs={{0,1},{1,0},{2,3},{3,2},{4,5},{5,4},{6,7},{7,6},{8,9},{9,8},{10,11... | collective-permute-start | bytes 1572872 | tf_op jit(solution)/shard_map/ppermute | solution.py:609
  148.1 2.8 %collective-permute-start.28 = (bf16[512,512]{1,0:T(8,128)(2,1)S(1)}, bf16[512,512]{1,0:T(8,128)(2,1)S(1)}, u32[]{:S(2)}, u32[]{:S(2)}) collective-permute-start(bf16[512,512]{1,0:T(8,128)(2,1)S(1)} %get-tuple-element.37), channel_id=1, source_target_pairs={{0,1},{1,0},{2,3},{3,2},{4,5},{5,4},{6,7},{7,6},{8,9},{9,8},{10,11... | collective-permute-start | bytes 1572872 | tf_op jit(solution)/shard_map/ppermute | solution.py:609
  151.6 10.2 %upper.1.unused_ref = bf16[1024,1024]{1,0:T(8,128)(2,1)} custom-call(bf16[1024,4096]{1,0:T(8,128)(2,1)} %refs_0_.1, bf16[3,128,1024]{2,1,0:T(8,128)(2,1)S(1)} %pad_maximum_fusion.refs_1_, bf16[3,128,1024]{2,1,0:T(8,128)(2,1)S(1)} %collective-permute-done.3.refs_2_, bf16[3,128,1024]{2,1,0:T(8,128)(2,1)S(1)} %collective-permute-done.4.refs_3_, ...), custom_call_target="tpu_custom_call" | custom-call | tf_op jit(solution)/shard_map/upper/pallas_call | solution.py:466
  162.7 5.4 %collective-permute-done.28.left_ref = bf16[512,512]{1,0:T(8,128)(2,1)S(1)} collective-permute-done((bf16[512,512]{1,0:T(8,128)(2,1)S(1)}, bf16[512,512]{1,0:T(8,128)(2,1)S(1)}, u32[]{:S(2)}, u32[]{:S(2)}) %collective-permute-start.28) | collective-permute-done | bytes 524320 | tf_op jit(solution)/shard_map/ppermute | solution.py:609
  (71 shorter events, 17.6 us)
Async XLA Ops:
  10.7 7.8 %collective-permute-start.11 = (f32[2,16,1024]{2,1,0:T(8,128)S(1)}, f32[2,16,1024]{2,1,0:T(8,128)S(1)}, u32[]{:S(2)}, u32[]{:S(2)}) collective-permute-start(f32[2,16,1024]{2,1,0:T(8,128)S(1)} %get-tuple-element.26), channel_id=1, source_target_pairs={{0,16},{4,20},{8,24},{12,28},{16,0},{20,4},{24,8},{28,12},{1,17},{... | collective-permute-start | bytes 393224 | tf_op jit(solution)/shard_map/ppermute | solution.py:337
  24.4 23.7 %collective-permute-start.14 = (bf16[512,512]{1,0:T(8,128)(2,1)S(1)}, bf16[512,512]{1,0:T(8,128)(2,1)S(1)}, u32[]{:S(2)}, u32[]{:S(2)}) collective-permute-start(bf16[512,512]{1,0:T(8,128)(2,1)S(1)} %complete.1.refs_9_), channel_id=1, source_target_pairs={{0,1},{1,0},{2,3},{3,2},{4,5},{5,4},{6,7},{7,6},{8,9},{9,8},{10,11... | collective-permute-start | bytes 1572872 | tf_op jit(solution)/shard_map/ppermute | solution.py:609
  26.0 22.0 %collective-permute-start.16 = (bf16[512,512]{1,0:T(8,128)(2,1)S(1)}, bf16[512,512]{1,0:T(8,128)(2,1)S(1)}, u32[]{:S(2)}, u32[]{:S(2)}) collective-permute-start(bf16[512,512]{1,0:T(8,128)(2,1)S(1)} %complete.1.refs_9_), channel_id=1, source_target_pairs={{1,2},{2,1},{5,6},{6,5},{9,10},{10,9},{13,14},{14,13},{17,18},{18,... | collective-permute-start | bytes 1572872 | tf_op jit(solution)/shard_map/ppermute | solution.py:610
  30.7 22.7 %collective-permute-start.15 = (bf16[512,512]{1,0:T(8,128)(2,1)S(1)}, bf16[512,512]{1,0:T(8,128)(2,1)S(1)}, u32[]{:S(2)}, u32[]{:S(2)}) collective-permute-start(bf16[512,512]{1,0:T(8,128)(2,1)S(1)} %convolve.2.refs_10_), channel_id=1, source_target_pairs={{0,1},{1,0},{2,3},{3,2},{4,5},{5,4},{6,7},{7,6},{8,9},{9,8},{10,11... | collective-permute-start | bytes 1572872 | tf_op jit(solution)/shard_map/ppermute | solution.py:609
  35.2 20.2 %collective-permute-start.18 = (bf16[512,512]{1,0:T(8,128)(2,1)S(1)}, bf16[512,512]{1,0:T(8,128)(2,1)S(1)}, u32[]{:S(2)}, u32[]{:S(2)}) collective-permute-start(bf16[512,512]{1,0:T(8,128)(2,1)S(1)} %convolve.2.refs_10_), channel_id=1, source_target_pairs={{1,2},{2,1},{5,6},{6,5},{9,10},{10,9},{13,14},{14,13},{17,18},{18,... | collective-permute-start | bytes 1572872 | tf_op jit(solution)/shard_map/ppermute | solution.py:610
  48.3 41.6 %collective-permute-start.17 = (bf16[512,512]{1,0:T(8,128)(2,1)S(1)}, bf16[512,512]{1,0:T(8,128)(2,1)S(1)}, u32[]{:S(2)}, u32[]{:S(2)}) collective-permute-start(bf16[512,512]{1,0:T(8,128)(2,1)S(1)} %get-tuple-element.27), channel_id=1, source_target_pairs={{0,1},{1,0},{2,3},{3,2},{4,5},{5,4},{6,7},{7,6},{8,9},{9,8},{10,11... | collective-permute-start | bytes 1572872 | tf_op jit(solution)/shard_map/ppermute | solution.py:609
  49.8 21.4 %collective-permute-start.2 = (bf16[128,1024]{1,0:T(8,128)(2,1)S(1)}, bf16[128,1024]{1,0:T(8,128)(2,1)S(1)}, u32[]{:S(2)}, u32[]{:S(2)}) collective-permute-start(bf16[128,1024]{1,0:T(8,128)(2,1)S(1)} %get-tuple-element.24), channel_id=1, source_target_pairs={{0,3},{1,2},{2,1},{3,0},{4,7},{5,6},{6,5},{7,4},{8,11},{9,10},{10,... | collective-permute-start | bytes 786440 | tf_op jit(solution)/shard_map/ppermute | solution.py:377
  52.7 38.0 %collective-permute-start.20 = (bf16[512,512]{1,0:T(8,128)(2,1)S(1)}, bf16[512,512]{1,0:T(8,128)(2,1)S(1)}, u32[]{:S(2)}, u32[]{:S(2)}) collective-permute-start(bf16[512,512]{1,0:T(8,128)(2,1)S(1)} %get-tuple-element.29), channel_id=1, source_target_pairs={{1,2},{2,1},{5,6},{6,5},{9,10},{10,9},{13,14},{14,13},{17,18},{18,... | collective-permute-start | bytes 1572872 | tf_op jit(solution)/shard_map/ppermute | solution.py:610
  53.4 34.4 %collective-permute-start.1 = (bf16[128,1024]{1,0:T(8,128)(2,1)S(1)}, bf16[128,1024]{1,0:T(8,128)(2,1)S(1)}, u32[]{:S(2)}, u32[]{:S(2)}) collective-permute-start(bf16[128,1024]{1,0:T(8,128)(2,1)S(1)} %get-tuple-element.23), channel_id=1, source_target_pairs={{0,2},{1,3},{2,0},{3,1},{4,6},{5,7},{6,4},{7,5},{8,10},{9,11},{10,... | collective-permute-start | bytes 786440 | tf_op jit(solution)/shard_map/ppermute | solution.py:377
  55.4 33.2 %collective-permute-start = (bf16[128,1024]{1,0:T(8,128)(2,1)S(1)}, bf16[128,1024]{1,0:T(8,128)(2,1)S(1)}, u32[]{:S(2)}, u32[]{:S(2)}) collective-permute-start(bf16[128,1024]{1,0:T(8,128)(2,1)S(1)} %get-tuple-element.22), channel_id=1, source_target_pairs={{0,1},{1,0},{2,3},{3,2},{4,5},{5,4},{6,7},{7,6},{8,9},{9,8},{10,11... | collective-permute-start | bytes 786440 | tf_op jit(solution)/shard_map/ppermute | solution.py:377
  71.2 21.1 %collective-permute-start.19 = (bf16[512,512]{1,0:T(8,128)(2,1)S(1)}, bf16[512,512]{1,0:T(8,128)(2,1)S(1)}, u32[]{:S(2)}, u32[]{:S(2)}) collective-permute-start(bf16[512,512]{1,0:T(8,128)(2,1)S(1)} %get-tuple-element.28), channel_id=1, source_target_pairs={{0,1},{1,0},{2,3},{3,2},{4,5},{5,4},{6,7},{7,6},{8,9},{9,8},{10,11... | collective-permute-start | bytes 1572872 | tf_op jit(solution)/shard_map/ppermute | solution.py:609
  88.6 20.5 %collective-permute-start.4 = (bf16[3,128,1024]{2,1,0:T(8,128)(2,1)S(1)}, bf16[3,128,1024]{2,1,0:T(8,128)(2,1)S(1)}, u32[]{:S(2)}, u32[]{:S(2)}) collective-permute-start(bf16[3,128,1024]{2,1,0:T(8,128)(2,1)S(1)} %pad_maximum_fusion.refs_1_), channel_id=1, source_target_pairs={{0,8},{4,12},{8,0},{12,4},{16,24},{20,28},{24,16},{28,20},{1,9},{5... | collective-permute-start | bytes 2359304 | tf_op jit(solution)/shard_map/ppermute | solution.py:381
  89.9 34.0 %collective-permute-start.6 = (bf16[3,128,1024]{2,1,0:T(8,128)(2,1)S(1)}, bf16[3,128,1024]{2,1,0:T(8,128)(2,1)S(1)}, u32[]{:S(2)}, u32[]{:S(2)}) collective-permute-start(bf16[3,128,1024]{2,1,0:T(8,128)(2,1)S(1)} %pad_maximum_fusion.refs_1_), channel_id=1, source_target_pairs={{0,16},{4,20},{8,24},{12,28},{16,0},{20,4},{24,8},{28,12},{1,17},{... | collective-permute-start | bytes 2359304 | tf_op jit(solution)/shard_map/ppermute | solution.py:381
  90.8 34.8 %collective-permute-start.8 = (bf16[3,128,1024]{2,1,0:T(8,128)(2,1)S(1)}, bf16[3,128,1024]{2,1,0:T(8,128)(2,1)S(1)}, u32[]{:S(2)}, u32[]{:S(2)}) collective-permute-start(bf16[3,128,1024]{2,1,0:T(8,128)(2,1)S(1)} %pad_maximum_fusion.refs_1_), channel_id=1, source_target_pairs={{0,24},{4,28},{8,16},{12,20},{16,8},{20,12},{24,0},{28,4},{1,25},{... | collective-permute-start | bytes 2359304 | tf_op jit(solution)/shard_map/ppermute | solution.py:381
  92.4 33.2 %collective-permute-start.21 = (bf16[512,512]{1,0:T(8,128)(2,1)S(1)}, bf16[512,512]{1,0:T(8,128)(2,1)S(1)}, u32[]{:S(2)}, u32[]{:S(2)}) collective-permute-start(bf16[512,512]{1,0:T(8,128)(2,1)S(1)} %get-tuple-element.30), channel_id=1, source_target_pairs={{0,1},{1,0},{2,3},{3,2},{4,5},{5,4},{6,7},{7,6},{8,9},{9,8},{10,11... | collective-permute-start | bytes 1572872 | tf_op jit(solution)/shard_map/ppermute | solution.py:609
  93.9 32.2 %collective-permute-start.23 = (bf16[512,512]{1,0:T(8,128)(2,1)S(1)}, bf16[512,512]{1,0:T(8,128)(2,1)S(1)}, u32[]{:S(2)}, u32[]{:S(2)}) collective-permute-start(bf16[512,512]{1,0:T(8,128)(2,1)S(1)} %get-tuple-element.32), channel_id=1, source_target_pairs={{0,1},{1,0},{2,3},{3,2},{4,5},{5,4},{6,7},{7,6},{8,9},{9,8},{10,11... | collective-permute-start | bytes 1572872 | tf_op jit(solution)/shard_map/ppermute | solution.py:609
  109.1 38.3 %collective-permute-start.3 = (bf16[3,128,1024]{2,1,0:T(8,128)(2,1)S(1)}, bf16[3,128,1024]{2,1,0:T(8,128)(2,1)S(1)}, u32[]{:S(2)}, u32[]{:S(2)}) collective-permute-start(bf16[3,128,1024]{2,1,0:T(8,128)(2,1)S(1)} %pad_maximum_fusion.refs_1_), channel_id=1, source_target_pairs={{0,4},{4,0},{8,12},{12,8},{16,20},{20,16},{24,28},{28,24},{1,5},{5... | collective-permute-start | bytes 2359304 | tf_op jit(solution)/shard_map/ppermute | solution.py:383
  125.5 22.6 %collective-permute-start.5 = (bf16[3,128,1024]{2,1,0:T(8,128)(2,1)S(1)}, bf16[3,128,1024]{2,1,0:T(8,128)(2,1)S(1)}, u32[]{:S(2)}, u32[]{:S(2)}) collective-permute-start(bf16[3,128,1024]{2,1,0:T(8,128)(2,1)S(1)} %collective-permute-done.4.refs_3_), channel_id=1, source_target_pairs={{0,4},{4,0},{8,12},{12,8},{16,20},{20,16},{24,28},{28,24},{1,5},{5... | collective-permute-start | bytes 2359304 | tf_op jit(solution)/shard_map/ppermute | solution.py:383
  125.5 25.4 %collective-permute-start.7 = (bf16[3,128,1024]{2,1,0:T(8,128)(2,1)S(1)}, bf16[3,128,1024]{2,1,0:T(8,128)(2,1)S(1)}, u32[]{:S(2)}, u32[]{:S(2)}) collective-permute-start(bf16[3,128,1024]{2,1,0:T(8,128)(2,1)S(1)} %collective-permute-done.6.refs_5_), channel_id=1, source_target_pairs={{0,4},{4,0},{8,12},{12,8},{16,20},{20,16},{24,28},{28,24},{1,5},{5... | collective-permute-start | bytes 2359304 | tf_op jit(solution)/shard_map/ppermute | solution.py:383
  126.7 24.8 %collective-permute-start.9 = (bf16[3,128,1024]{2,1,0:T(8,128)(2,1)S(1)}, bf16[3,128,1024]{2,1,0:T(8,128)(2,1)S(1)}, u32[]{:S(2)}, u32[]{:S(2)}) collective-permute-start(bf16[3,128,1024]{2,1,0:T(8,128)(2,1)S(1)} %collective-permute-done.8.refs_7_), channel_id=1, source_target_pairs={{0,4},{4,0},{8,12},{12,8},{16,20},{20,16},{24,28},{28,24},{1,5},{5... | collective-permute-start | bytes 2359304 | tf_op jit(solution)/shard_map/ppermute | solution.py:383
  127.0 34.8 %collective-permute-start.26 = (bf16[512,512]{1,0:T(8,128)(2,1)S(1)}, bf16[512,512]{1,0:T(8,128)(2,1)S(1)}, u32[]{:S(2)}, u32[]{:S(2)}) collective-permute-start(bf16[512,512]{1,0:T(8,128)(2,1)S(1)} %get-tuple-element.35), channel_id=1, source_target_pairs={{0,1},{1,0},{2,3},{3,2},{4,5},{5,4},{6,7},{7,6},{8,9},{9,8},{10,11... | collective-permute-start | bytes 1572872 | tf_op jit(solution)/shard_map/ppermute | solution.py:609
  147.4 14.4 %collective-permute-start.27 = (bf16[512,512]{1,0:T(8,128)(2,1)S(1)}, bf16[512,512]{1,0:T(8,128)(2,1)S(1)}, u32[]{:S(2)}, u32[]{:S(2)}) collective-permute-start(bf16[512,512]{1,0:T(8,128)(2,1)S(1)} %get-tuple-element.36), channel_id=1, source_target_pairs={{1,2},{2,1},{5,6},{6,5},{9,10},{10,9},{13,14},{14,13},{17,18},{18,... | collective-permute-start | bytes 1572872 | tf_op jit(solution)/shard_map/ppermute | solution.py:610
  148.1 20.0 %collective-permute-start.28 = (bf16[512,512]{1,0:T(8,128)(2,1)S(1)}, bf16[512,512]{1,0:T(8,128)(2,1)S(1)}, u32[]{:S(2)}, u32[]{:S(2)}) collective-permute-start(bf16[512,512]{1,0:T(8,128)(2,1)S(1)} %get-tuple-element.37), channel_id=1, source_target_pairs={{0,1},{1,0},{2,3},{3,2},{4,5},{5,4},{6,7},{7,6},{8,9},{9,8},{10,11... | collective-permute-start | bytes 1572872 | tf_op jit(solution)/shard_map/ppermute | solution.py:609
  150.9 17.2 %collective-permute-start.29 = (bf16[512,512]{1,0:T(8,128)(2,1)S(1)}, bf16[512,512]{1,0:T(8,128)(2,1)S(1)}, u32[]{:S(2)}, u32[]{:S(2)}) collective-permute-start(bf16[512,512]{1,0:T(8,128)(2,1)S(1)} %get-tuple-element.38), channel_id=1, source_target_pairs={{1,2},{2,1},{5,6},{6,5},{9,10},{10,9},{13,14},{14,13},{17,18},{18,... | collective-permute-start | bytes 1572872 | tf_op jit(solution)/shard_map/ppermute | solution.py:610
  (12 other events, 113.9 us)
